TPU v7x, 32 devices: a whole 2x2x4 slice. The times are simulated.
32 devices in a mesh: dp: 16 (over z, y, x), tensor: 2 (over core).
Axes of the slice: x: 2, y: 2, z: 4, core: 2. Of those that a mesh axis runs over, the one named last changes fastest.
Arguments:
- tokens: bfloat16 [768, 16, 768], P('dp', 'tensor'), may hold values from -6 to 6
- cotangent: bfloat16 [768, 16, 768], P('dp', 'tensor'), may hold values from -6 to 6
- block_route: int32 [768], P('dp'), may hold values from 0 to 767, as said below
- lengths: int32 [48, 3], P('dp'), may hold values from 1 to 170, 256 in all within a row
- w_query: bfloat16 [768, 768], P('dp', 'tensor'), may hold values from -0.3125 to 0.3125
- w_key: bfloat16 [768, 768], P('dp', 'tensor'), may hold values from -0.3125 to 0.3125
- w_value: bfloat16 [768, 768], P('dp', 'tensor'), may hold values from -0.21875 to 0.21875
- b_query: bfloat16 [2, 384], P('tensor'), may hold values from -3 to 3
- b_value: bfloat16 [2, 384], P('tensor'), may hold values from -3 to 3
- w_out: bfloat16 [768, 768], P('tensor', 'dp'), may hold values from -1.25 to 1.25
- b_out: bfloat16 [768], P('dp'), may hold values from -3 to 3
- gain_attn: bfloat16 [768], P('dp'), may hold values from 0.5 to 1.5
- shift_attn: bfloat16 [768], P('dp'), may hold values from -2 to 2
- w_inner: bfloat16 [768, 3072], P('dp', 'tensor'), may hold values from -0.21875 to 0.21875
- b_inner: bfloat16 [2, 1536], P('tensor', 'dp'), may hold values from -3 to 3
- w_outer: bfloat16 [3072, 768], P('tensor', 'dp'), may hold values from -0.15625 to 0.15625
- b_outer: bfloat16 [768], P('dp'), may hold values from -2 to 2
- gain_ffn: bfloat16 [768], P('dp'), may hold values from 0.5 to 1.5
- shift_ffn: bfloat16 [768], P('dp'), may hold values from -2 to 2
Outputs:
- layer_out: bfloat16 [768, 16, 768], P('dp', 'tensor')
- grad_tokens: bfloat16 [768, 16, 768], P('dp', 'tensor')
- grad_w_query: float32 [768, 768], P('dp', 'tensor')
- grad_w_key: float32 [768, 768], P('dp', 'tensor')
- grad_w_value: float32 [768, 768], P('dp', 'tensor')
- grad_b_query: float32 [2, 384], P('tensor')
- grad_b_value: float32 [2, 384], P('tensor')
- grad_w_out: float32 [768, 768], P('tensor', 'dp')
- grad_b_out: float32 [768], P('dp')
- grad_gain_attn: float32 [768], P('dp')
- grad_shift_attn: float32 [768], P('dp')
- grad_w_inner: float32 [768, 3072], P('dp', 'tensor')
- grad_b_inner: float32 [2, 1536], P('tensor', 'dp')
- grad_w_outer: float32 [3072, 768], P('tensor', 'dp')
- grad_b_outer: float32 [768], P('dp')
- grad_gain_ffn: float32 [768], P('dp')
- grad_shift_ffn: float32 [768], P('dp')
Inputs may be any that keep to these rules, and one draw needn't show every extreme that they name: block_route is a permutation of the 768 block indices. Given block s * 3 * 16 + m * 16 + k goes to packed index d * 3 * 16 + m * 16 + j: it stays in micro-batch m; among the 16 blocks of one s and one m every d appears once, and bin (d, m) receives exactly one block from every s. `lengths`: each row sums to 256.
All inputs are finite; a program needn't handle non-finite values.
Results may differ from a plain program's by a relative error of at most 0.017.
Values may be sent and summed in bfloat16 or wider, within the bound.
A program may use at most 128 MiB of HBM per device.

v0:
```python
from functools import partial
import math

import jax
import jax.numpy as jnp
from jax import lax
from jax.sharding import PartitionSpec as P

HEADS = 12
HD = 64


EPS_NORM = 1e-12


def layer_norm(residual, norm_gain, norm_shift):
    centre = residual - jnp.mean(residual, axis=-1, keepdims=True)
    spread = lax.rsqrt(jnp.mean(centre * centre, axis=-1, keepdims=True) + EPS_NORM)
    normed = centre * spread
    return (normed * norm_gain + norm_shift, normed, spread)


def norm_back(grad_out, normed, spread, norm_gain):
    scaled = grad_out * norm_gain
    inner_term = (
        scaled
        - jnp.mean(scaled, axis=-1, keepdims=True)
        - normed * jnp.mean(scaled * normed, axis=-1, keepdims=True)
    )
    return (inner_term * spread, jnp.sum(grad_out * normed, axis=0), jnp.sum(grad_out, axis=0))


def segment_of(seq_lengths, count_rows):
    seq_ends = jnp.cumsum(seq_lengths)
    positions = jnp.arange(count_rows, dtype=jnp.int32)
    return jnp.sum((positions[:, None] >= seq_ends[None, :-1]).astype(jnp.int32), axis=1)


def masked_scores(query_block, key_heads, segment, first_row, block_rows, score_scale):
    scores = (
        jnp.einsum("qhd,khd->hqk", query_block, key_heads, preferred_element_type=jnp.float32)
        * score_scale
    )
    allowed = segment[first_row : first_row + block_rows, None] == segment[None, :]
    return jnp.where(allowed[None], scores, -1e30)


def attend_forward(query_heads, key_heads, value_heads, segment, block_rows, score_scale):
    scores = masked_scores(query_heads, key_heads, segment, 0, block_rows, score_scale)
    row_peak = jnp.max(scores, axis=-1, keepdims=True)
    exp_scores = jnp.exp(scores - row_peak)
    row_total = jnp.sum(exp_scores, axis=-1, keepdims=True)
    prob_low = (exp_scores / row_total).astype(jnp.bfloat16)
    out_block = jnp.einsum(
        "hqk,khd->qhd", prob_low, value_heads, preferred_element_type=jnp.float32
    )
    out_rows = out_block.astype(jnp.bfloat16)
    lse_rows = row_peak + jnp.log(row_total)
    return (out_rows, lse_rows)


def attend_backward(
    query_heads, key_heads, value_heads, grad_heads, log_totals, segment, block_rows, score_scale
):
    scores = masked_scores(query_heads, key_heads, segment, 0, block_rows, score_scale)
    probs_full = jnp.exp(scores - log_totals)
    prob_low = probs_full.astype(jnp.bfloat16)
    grad_values = jnp.einsum(
        "hqk,qhd->khd", prob_low, grad_heads, preferred_element_type=jnp.float32
    )
    grad_probs = jnp.einsum(
        "qhd,khd->hqk", grad_heads, value_heads, preferred_element_type=jnp.float32
    )
    row_inner = jnp.sum(probs_full * grad_probs, axis=-1, keepdims=True)
    grad_scores = (probs_full * (grad_probs - row_inner)).astype(jnp.bfloat16)
    grad_query_rows = (
        jnp.einsum("hqk,khd->qhd", grad_scores, key_heads, preferred_element_type=jnp.float32)
        * score_scale
    )
    grad_keys = (
        jnp.einsum("hqk,qhd->khd", grad_scores, query_heads, preferred_element_type=jnp.float32)
        * score_scale
    )
    return (grad_query_rows, grad_keys, grad_values)


def shards(
    tokens,
    cotangent,
    block_route,
    lengths,
    w_query,
    w_key,
    w_value,
    b_query,
    b_value,
    w_out,
    b_out,
    gain_attn,
    shift_attn,
    w_inner,
    b_inner,
    w_outer,
    b_outer,
    gain_ffn,
    shift_ffn,
):
    dp_count = lax.axis_size("dp")
    micro_count = lengths.shape[0]
    half_rows = tokens.shape[1]
    model_width = tokens.shape[2]
    local_heads = HEADS // lax.axis_size("tensor")
    score_scale = HD ** (-0.5)
    blocks = tokens.reshape(micro_count, dp_count, half_rows, model_width)
    upstream = cotangent.reshape(micro_count, dp_count, half_rows, model_width)
    target = block_route.reshape(micro_count, dp_count)
    dest_dev = target // (micro_count * dp_count)
    bin_place = target % dp_count
    micro_ids = jnp.broadcast_to(
        jnp.arange(micro_count, dtype=jnp.int32)[:, None], (micro_count, dp_count)
    )
    slot_ids = jnp.broadcast_to(
        jnp.arange(dp_count, dtype=jnp.int32)[None, :], (micro_count, dp_count)
    )
    inverse = jnp.zeros((micro_count, dp_count), jnp.int32).at[micro_ids, dest_dev].set(slot_ids)
    by_dest = jnp.take_along_axis(blocks, inverse[:, :, None, None], axis=1)
    grad_dest = jnp.take_along_axis(upstream, inverse[:, :, None, None], axis=1)
    place_dest = jnp.take_along_axis(bin_place, inverse, axis=1)
    arrived, arrived_grad, arrived_place = (
        lax.all_to_all(by_dest, "dp", split_axis=1, concat_axis=1, tiled=True),
        lax.all_to_all(grad_dest, "dp", split_axis=1, concat_axis=1, tiled=True),
        lax.all_to_all(place_dest, "dp", split_axis=1, concat_axis=1, tiled=True),
    )
    anchor = (
        jnp.zeros((micro_count, dp_count), jnp.int32).at[micro_ids, arrived_place].set(slot_ids)
    )
    bin_tokens = jnp.take_along_axis(arrived, anchor[:, :, None, None], axis=1)
    bin_grads = jnp.take_along_axis(arrived_grad, anchor[:, :, None, None], axis=1)
    acc_query = jnp.zeros((model_width, w_query.shape[1]), jnp.float32)
    acc_key = jnp.zeros((model_width, w_key.shape[1]), jnp.float32)
    acc_value = jnp.zeros((model_width, w_value.shape[1]), jnp.float32)
    acc_out = jnp.zeros((w_out.shape[0], model_width), jnp.float32)
    acc_inner = jnp.zeros((model_width, w_inner.shape[1]), jnp.float32)
    acc_outer = jnp.zeros((w_outer.shape[0], model_width), jnp.float32)
    acc_bias_query = jnp.zeros((1, w_query.shape[1]), jnp.float32)
    acc_bias_value = jnp.zeros((1, w_value.shape[1]), jnp.float32)
    acc_bias_inner = jnp.zeros((1, w_inner.shape[1]), jnp.float32)
    acc_vectors = jnp.zeros((6, model_width), jnp.float32)
    out_bins = []
    grad_bins = []
    for micro_step in range(micro_count):
        gathered = (
            lax.all_gather(w_query, "dp", axis=0, tiled=True),
            lax.all_gather(w_key, "dp", axis=0, tiled=True),
            lax.all_gather(w_value, "dp", axis=0, tiled=True),
            lax.all_gather(w_out, "dp", axis=1, tiled=True),
            lax.all_gather(w_inner, "dp", axis=0, tiled=True),
            lax.all_gather(w_outer, "dp", axis=1, tiled=True),
            lax.all_gather(b_inner, "dp", axis=1, tiled=True),
            lax.all_gather(b_out, "dp", axis=0, tiled=True),
            lax.all_gather(gain_attn, "dp", axis=0, tiled=True),
            lax.all_gather(shift_attn, "dp", axis=0, tiled=True),
            lax.all_gather(b_outer, "dp", axis=0, tiled=True),
            lax.all_gather(gain_ffn, "dp", axis=0, tiled=True),
            lax.all_gather(shift_ffn, "dp", axis=0, tiled=True),
        )
        (
            full_query,
            full_key,
            full_value,
            full_out,
            full_inner,
            full_outer,
            bias_inner,
            bias_out,
            full_gain_attn,
            full_shift_attn,
            bias_outer,
            full_gain_ffn,
            full_shift_ffn,
        ) = gathered
        own_rows = bin_tokens[micro_step]
        whole_bin = lax.all_gather(own_rows, "tensor", axis=1, tiled=True).reshape(-1, model_width)
        bin_rows = whole_bin.shape[0]
        block_rows = math.gcd(bin_rows, 512)
        segment = segment_of(lengths[micro_step], bin_rows)
        query = (
            jnp.dot(whole_bin, full_query, preferred_element_type=jnp.float32) + b_query[0]
        ).astype(jnp.bfloat16)
        keys = jnp.dot(whole_bin, full_key, preferred_element_type=jnp.float32).astype(jnp.bfloat16)
        values = (
            jnp.dot(whole_bin, full_value, preferred_element_type=jnp.float32) + b_value[0]
        ).astype(jnp.bfloat16)
        query_heads = query.reshape(bin_rows, local_heads, HD)
        key_heads = keys.reshape(bin_rows, local_heads, HD)
        value_heads = values.reshape(bin_rows, local_heads, HD)
        attn_heads, log_totals = attend_forward(
            query_heads, key_heads, value_heads, segment, block_rows, score_scale
        )
        attn = attn_heads.reshape(bin_rows, local_heads * HD)
        attn_partial = jnp.dot(attn, full_out, preferred_element_type=jnp.float32).reshape(
            dp_count, -1, model_width
        )
        branch = lax.psum_scatter(attn_partial, "tensor", scatter_dimension=1, tiled=True).reshape(
            -1, model_width
        )
        mid = own_rows.reshape(-1, model_width).astype(jnp.float32) + branch + bias_out
        hidden, normed_attn, spread_attn = layer_norm(mid, full_gain_attn, full_shift_attn)
        hidden_low = hidden.astype(jnp.bfloat16).reshape(dp_count, half_rows, model_width)
        hidden_whole = lax.all_gather(hidden_low, "tensor", axis=1, tiled=True).reshape(
            -1, model_width
        )
        inner = (
            jnp.dot(hidden_whole, full_inner, preferred_element_type=jnp.float32) + bias_inner[0]
        )
        gelu_value, gelu_pull = jax.vjp(partial(jax.nn.gelu, approximate=False), inner)
        gelu_low = gelu_value.astype(jnp.bfloat16)
        ffn_partial = jnp.dot(gelu_low, full_outer, preferred_element_type=jnp.float32).reshape(
            dp_count, -1, model_width
        )
        ffn = lax.psum_scatter(ffn_partial, "tensor", scatter_dimension=1, tiled=True).reshape(
            -1, model_width
        )
        top = hidden + ffn + bias_outer
        result, normed_ffn, spread_ffn = layer_norm(top, full_gain_ffn, full_shift_ffn)
        out_bins.append(result.astype(jnp.bfloat16).reshape(dp_count, half_rows, model_width))
        back_full = (
            lax.all_gather(w_query, "dp", axis=0, tiled=True),
            lax.all_gather(w_key, "dp", axis=0, tiled=True),
            lax.all_gather(w_value, "dp", axis=0, tiled=True),
            lax.all_gather(w_out, "dp", axis=1, tiled=True),
            lax.all_gather(w_inner, "dp", axis=0, tiled=True),
            lax.all_gather(w_outer, "dp", axis=1, tiled=True),
            lax.all_gather(gain_attn, "dp", axis=0, tiled=True),
            lax.all_gather(gain_ffn, "dp", axis=0, tiled=True),
        )
        (
            back_query,
            back_key,
            back_value,
            back_out,
            back_inner,
            back_outer,
            back_gain_attn,
            back_gain_ffn,
        ) = back_full
        grad_result = bin_grads[micro_step].reshape(-1, model_width).astype(jnp.float32)
        grad_top, grad_gain_ffn, grad_shift_ffn = norm_back(
            grad_result, normed_ffn, spread_ffn, back_gain_ffn
        )
        grad_ffn_low = grad_top.astype(jnp.bfloat16)
        grad_bias_outer = jnp.sum(grad_ffn_low.astype(jnp.float32), axis=0)
        grad_ffn_whole = lax.all_gather(
            grad_ffn_low.reshape(dp_count, half_rows, model_width), "tensor", axis=1, tiled=True
        ).reshape(-1, model_width)
        acc_outer = acc_outer + jnp.einsum(
            "nf,nd->fd", gelu_low, grad_ffn_whole, preferred_element_type=jnp.float32
        )
        grad_gelu = jnp.einsum(
            "nd,fd->nf", grad_ffn_whole, back_outer, preferred_element_type=jnp.float32
        )
        grad_inner_low = gelu_pull(grad_gelu)[0].astype(jnp.bfloat16)
        acc_bias_inner = acc_bias_inner + jnp.sum(grad_inner_low.astype(jnp.float32), axis=0)[None]
        acc_inner = acc_inner + jnp.einsum(
            "nd,nf->df", hidden_whole, grad_inner_low, preferred_element_type=jnp.float32
        )
        hidden_partial = jnp.einsum(
            "nf,df->nd", grad_inner_low, back_inner, preferred_element_type=jnp.float32
        ).reshape(dp_count, -1, model_width)
        grad_hidden = grad_top + lax.psum_scatter(
            hidden_partial, "tensor", scatter_dimension=1, tiled=True
        ).reshape(-1, model_width)
        grad_mid, grad_gain_attn, grad_shift_attn = norm_back(
            grad_hidden, normed_attn, spread_attn, back_gain_attn
        )
        grad_branch_low = grad_mid.astype(jnp.bfloat16)
        grad_bias_out = jnp.sum(grad_branch_low.astype(jnp.float32), axis=0)
        grad_branch_whole = lax.all_gather(
            grad_branch_low.reshape(dp_count, half_rows, model_width), "tensor", axis=1, tiled=True
        ).reshape(-1, model_width)
        acc_out = acc_out + jnp.einsum(
            "nh,nd->hd", attn, grad_branch_whole, preferred_element_type=jnp.float32
        )
        grad_attn_low = jnp.einsum(
            "nd,hd->nh", grad_branch_whole, back_out, preferred_element_type=jnp.float32
        ).astype(jnp.bfloat16)
        grad_heads = grad_attn_low.reshape(bin_rows, local_heads, HD)
        grad_query, grad_keys, grad_values = attend_backward(
            query_heads,
            key_heads,
            value_heads,
            grad_heads,
            log_totals,
            segment,
            block_rows,
            score_scale,
        )
        grad_query_low = grad_query.reshape(bin_rows, -1).astype(jnp.bfloat16)
        grad_key_low = grad_keys.reshape(bin_rows, -1).astype(jnp.bfloat16)
        grad_value_low = grad_values.reshape(bin_rows, -1).astype(jnp.bfloat16)
        acc_bias_query = acc_bias_query + jnp.sum(grad_query_low.astype(jnp.float32), axis=0)[None]
        acc_bias_value = acc_bias_value + jnp.sum(grad_value_low.astype(jnp.float32), axis=0)[None]
        acc_query = acc_query + jnp.einsum(
            "nd,nh->dh", whole_bin, grad_query_low, preferred_element_type=jnp.float32
        )
        acc_key = acc_key + jnp.einsum(
            "nd,nh->dh", whole_bin, grad_key_low, preferred_element_type=jnp.float32
        )
        acc_value = acc_value + jnp.einsum(
            "nd,nh->dh", whole_bin, grad_value_low, preferred_element_type=jnp.float32
        )
        input_partial = (
            jnp.einsum("nh,dh->nd", grad_query_low, back_query, preferred_element_type=jnp.float32)
            + jnp.einsum("nh,dh->nd", grad_key_low, back_key, preferred_element_type=jnp.float32)
            + jnp.einsum(
                "nh,dh->nd", grad_value_low, back_value, preferred_element_type=jnp.float32
            )
        )
        grad_input = grad_mid + lax.psum_scatter(
            input_partial.reshape(dp_count, -1, model_width).astype(jnp.bfloat16),
            "tensor",
            scatter_dimension=1,
            tiled=True,
        ).astype(jnp.float32).reshape(-1, model_width)
        grad_bins.append(grad_input.astype(jnp.bfloat16).reshape(dp_count, half_rows, model_width))
        acc_vectors = acc_vectors + jnp.stack(
            [
                grad_bias_out,
                grad_gain_attn,
                grad_shift_attn,
                grad_bias_outer,
                grad_gain_ffn,
                grad_shift_ffn,
            ]
        )
    out_stack = jnp.stack(out_bins)
    grad_stack = jnp.stack(grad_bins)
    send_out = jnp.take_along_axis(out_stack, arrived_place[:, :, None, None], axis=1)
    send_grad = jnp.take_along_axis(grad_stack, arrived_place[:, :, None, None], axis=1)
    back_out_rows, back_grad_rows = (
        lax.all_to_all(send_out, "dp", split_axis=1, concat_axis=1, tiled=True),
        lax.all_to_all(send_grad, "dp", split_axis=1, concat_axis=1, tiled=True),
    )
    layer_out = jnp.take_along_axis(back_out_rows, dest_dev[:, :, None, None], axis=1).reshape(
        tokens.shape
    )
    grad_tokens = jnp.take_along_axis(back_grad_rows, dest_dev[:, :, None, None], axis=1).reshape(
        tokens.shape
    )
    sum_query, sum_key, sum_value, sum_out, sum_inner, sum_outer, sum_bias_inner = (
        lax.psum_scatter(acc_query, "dp", scatter_dimension=0, tiled=True),
        lax.psum_scatter(acc_key, "dp", scatter_dimension=0, tiled=True),
        lax.psum_scatter(acc_value, "dp", scatter_dimension=0, tiled=True),
        lax.psum_scatter(acc_out, "dp", scatter_dimension=1, tiled=True),
        lax.psum_scatter(acc_inner, "dp", scatter_dimension=0, tiled=True),
        lax.psum_scatter(acc_outer, "dp", scatter_dimension=1, tiled=True),
        lax.psum_scatter(acc_bias_inner, "dp", scatter_dimension=1, tiled=True),
    )
    half_width = w_query.shape[1]
    tensor_pos = lax.axis_index("tensor")
    bias_pair = lax.dynamic_update_slice(
        jnp.zeros((2, model_width), jnp.float32),
        jnp.concatenate([acc_bias_query, acc_bias_value], axis=0),
        (jnp.int32(0), tensor_pos * half_width),
    )
    vectors, bias_total = lax.psum((acc_vectors, bias_pair), ("dp", "tensor"))
    own_width = model_width // dp_count
    vec_own = lax.dynamic_slice_in_dim(vectors, lax.axis_index("dp") * own_width, own_width, 1)
    bias_own = lax.dynamic_slice_in_dim(bias_total, tensor_pos * half_width, half_width, 1)
    return (
        layer_out,
        grad_tokens,
        sum_query,
        sum_key,
        sum_value,
        bias_own[0:1],
        bias_own[1:2],
        sum_out,
        vec_own[0],
        vec_own[1],
        vec_own[2],
        sum_inner,
        sum_bias_inner,
        sum_outer,
        vec_own[3],
        vec_own[4],
        vec_own[5],
    )


def solution(mesh):
    placed = (
        P("dp", "tensor", None),
        P("dp", "tensor", None),
        P("dp"),
        P("dp", None),
        P("dp", "tensor"),
        P("dp", "tensor"),
        P("dp", "tensor"),
        P("tensor", None),
        P("tensor", None),
        P("tensor", "dp"),
        P("dp"),
        P("dp"),
        P("dp"),
        P("dp", "tensor"),
        P("tensor", "dp"),
        P("tensor", "dp"),
        P("dp"),
        P("dp"),
        P("dp"),
    )
    return jax.shard_map(
        shards,
        mesh=mesh,
        in_specs=placed,
        out_specs=(
            P("dp", "tensor", None),
            P("dp", "tensor", None),
            P("dp", "tensor"),
            P("dp", "tensor"),
            P("dp", "tensor"),
            P("tensor", None),
            P("tensor", None),
            P("tensor", "dp"),
            P("dp"),
            P("dp"),
            P("dp"),
            P("dp", "tensor"),
            P("tensor", "dp"),
            P("tensor", "dp"),
            P("dp"),
            P("dp"),
            P("dp"),
        ),
        check_vma=False,
    )
```

profile of v0, /device:TPU:0, one launch (start us, length us, event | category | flops | bytes accessed | tf_op | source)
XLA Modules:
  0.0 1494.2 jit_solution(17571348977875008409)
XLA Ops:
  10.6 2.7 scatter_fusion
  15.3 8.3 all-to-all-start.1
  28.6 2.2 all-to-all-done.1
  30.8 4.8 all-to-all-start
  37.3 45.2 %all_gather.52 = bf16[768,384]{1,0:T(8,128)(2,1)S(1)} all-gather(bf16[48,384]{1,0:T(8,128)(2,1)S(1)} %copy-done.176), channel_id=1, replica_groups=mesh['dp'=16,'tensor'=2] {'dp'}, dimensions={0}, use_global_device_ids=true | all-gather | bytes 626688 | tf_op jit(solution)/shard_map/all_gather | solution.py:153
  82.5 41.0 %all_gather.53 = bf16[768,384]{1,0:T(8,128)(2,1)S(1)} all-gather(bf16[48,384]{1,0:T(8,128)(2,1)S(1)} %copy-done.177), channel_id=1, replica_groups=mesh['dp'=16,'tensor'=2] {'dp'}, dimensions={0}, use_global_device_ids=true | all-gather | bytes 626688 | tf_op jit(solution)/shard_map/all_gather | solution.py:154
  123.6 40.0 %all_gather.51 = bf16[768,384]{1,0:T(8,128)(2,1)S(1)} all-gather(bf16[48,384]{1,0:T(8,128)(2,1)S(1)} %copy-done.178), channel_id=1, replica_groups=mesh['dp'=16,'tensor'=2] {'dp'}, dimensions={0}, use_global_device_ids=true | all-gather | bytes 626688 | tf_op jit(solution)/shard_map/all_gather | solution.py:155
  163.6 4.2 all-to-all-start.3
  168.0 44.1 %all_gather.54 = bf16[384,768]{0,1:T(8,128)(2,1)S(1)} all-gather(bf16[384,48]{0,1:T(8,128)(2,1)S(1)} %copy-done.179), channel_id=1, replica_groups=mesh['dp'=16,'tensor'=2] {'dp'}, dimensions={1}, use_global_device_ids=true | all-gather | bytes 626688 | tf_op jit(solution)/shard_map/all_gather | solution.py:156
  212.2 2.7 scatter_fusion.1
  216.8 2.7 gather_fusion.6
  219.5 2.2 broadcast_select_fusion.3
  222.6 2.1 all-gather.1
  225.9 2.1 all-gather
  234.3 2.1 dot_general.230
  236.3 2.2 fusion.49
  244.8 2.1 dot_general.239
  246.9 2.3 all-gather.2
  249.2 2.7 fusion.47
  252.1 2.1 convolution_convert_fusion.7
  254.2 1.8 copy.197
  256.0 2.1 fusion.32
  259.9 2.1 fusion.31
  268.3 2.4 fusion.45
  278.1 72.9 %all-reduce.8 = (bf16[768]{0:T(1024)(128)(2,1)S(1)}, bf16[768]{0:T(1024)(128)(2,1)S(1)}, bf16[768]{0:T(1024)(128)(2,1)S(1)}, bf16[1536]{0:T(1024)(128)(2,1)S(1)}...) all-reduce(bf16[768]{0:T(1024)(128)(2,1)S(1)} %dynamic-update-slice, ...), channel_id=1, replica_groups=mesh['dp'=16,'tensor'=2] {'dp'}, use_global_device_ids=true, to_apply=%add | all-reduce | flops 6144 | bytes 24576
  356.1 2.2 all_gather.58
  358.4 7.5 multiply_convert_fusion.5
  365.9 32.5 %all-gather.8.cloned.1.call-done = bf16[1536,768]{0,1:T(8,128)(2,1)} async-done(((bf16[1536,48]{0,1:T(8,128)(2,1)}), bf16[1536,768]{0,1:T(8,128)(2,1)}) %all-gather.8.cloned.1.call-update) | async-done | bytes 2359312 | tf_op jit(solution)/shard_map/all_gather | solution.py:158
  398.4 3.6 fusion.168
  402.1 2.7 all_gather.66
  404.8 7.2 multiply_convert_fusion.4
  413.8 2.3 all_gather.68
  416.1 7.1 multiply_convert_fusion.3
  426.9 4.9 reduce-scatter.38.cloned.1.call-done
  431.9 2.1 fusion.159
  435.7 3.2 convert_reduce_fusion.4
  439.2 2.1 all_gather.73
  447.5 6.9 reduce-scatter.44.cloned.1.call-done
  454.5 3.5 multiply_reduce_fusion.3
  458.0 2.1 all_gather.69
  460.0 3.8 convert_reduce_fusion.2
  468.2 6.9 reduce-scatter.40.cloned.1.call-done
  475.2 3.5 multiply_reduce_fusion.5
  478.6 2.2 all_gather.71
  480.9 3.8 convert_reduce_fusion.1
  496.1 2.3 multiply_reduce_fusion.4
  498.5 2.5 convert_reduce_fusion.11
  501.1 2.1 all_gather.72
  506.0 2.4 convert_reduce_fusion.13
  511.9 2.1 all_gather.74
  516.8 2.4 convert_reduce_fusion.12
  523.2 2.1 all_gather.70
  558.7 3.0 add_add_fusion
  565.0 3.0 add_add_fusion.1
  582.0 6.8 all-to-all-start.4
  589.5 102.2 %reduce-scatter.64.cloned.1.call-done = f32[96,1]{1,0:T(8,128)} async-done(((f32[1536,1]{1,0:T(8,128)}), f32[96,1]{1,0:T(8,128)}) %reduce-scatter.64.cloned.1.call-update) | async-done | bytes 400
  693.0 4.7 all-to-all-start.2
  698.2 41.3 %all-reduce.7 = (f32[2,768]{1,0:T(2,128)S(1)}, f32[6,768]{1,0:T(8,128)S(1)}) all-reduce(f32[2,768]{1,0:T(2,128)S(1)} %maximum_dynamic-update-slice_fusion, f32[6,768]{1,0:T(8,128)S(1)} %add_add_fusion.5), channel_id=1, replica_groups=mesh['dp'=16,'tensor'=2] {'dp','tensor'}, use_global_device_ids=true, to_apply=%region_62.64 | all-reduce | flops 6144 | bytes 49152 | tf_op jit(solution)/shard_map/psum | solution.py:366
  743.6 76.1 %reduce-scatter.52.cloned.1.call-done = f32[384,48]{0,1:T(8,128)} async-done(((f32[384,768]{0,1:T(8,128)}), f32[384,48]{0,1:T(8,128)}) %reduce-scatter.52.cloned.1.call-update) | async-done | bytes 73744 | tf_op jit(solution)/shard_map/reduce_scatter | solution.py:354
  819.7 127.8 %reduce-scatter.50.cloned.1.call-done = f32[48,384]{1,0:T(8,128)} async-done(((f32[768,384]{1,0:T(8,128)}), f32[48,384]{1,0:T(8,128)}) %reduce-scatter.50.cloned.1.call-update) | async-done | bytes 73744 | tf_op jit(solution)/shard_map/reduce_scatter | solution.py:353
  947.5 127.8 %reduce-scatter.48.cloned.1.call-done = f32[48,384]{1,0:T(8,128)} async-done(((f32[768,384]{1,0:T(8,128)}), f32[48,384]{1,0:T(8,128)}) %reduce-scatter.48.cloned.1.call-update) | async-done | bytes 73744 | tf_op jit(solution)/shard_map/reduce_scatter | solution.py:352
  1075.3 127.8 %reduce-scatter.46.cloned.1.call-done = f32[48,384]{1,0:T(8,128)} async-done(((f32[768,384]{1,0:T(8,128)}), f32[48,384]{1,0:T(8,128)}) %reduce-scatter.46.cloned.1.call-update) | async-done | bytes 73744 | tf_op jit(solution)/shard_map/reduce_scatter | solution.py:351
  1203.1 140.8 %reduce-scatter.56.cloned.1.call-done = f32[1536,48]{0,1:T(8,128)} async-done(((f32[1536,768]{0,1:T(8,128)}), f32[1536,48]{0,1:T(8,128)}) %reduce-scatter.56.cloned.1.call-update) | async-done | bytes 294928 | tf_op jit(solution)/shard_map/reduce_scatter | solution.py:356
  1343.9 142.7 %reduce-scatter.54.cloned.1.call-done = f32[48,1536]{1,0:T(8,128)} async-done(((f32[768,1536]{1,0:T(8,128)}), f32[48,1536]{1,0:T(8,128)}) %reduce-scatter.54.cloned.1.call-update) | async-done | bytes 294928 | tf_op jit(solution)/shard_map/reduce_scatter | solution.py:355
  (772 shorter events, 144.5 us)
Async XLA Ops:
  8.0 17.7 %copy-start = (bf16[48,8,768]{2,1,0:T(8,128)(2,1)S(1)}, bf16[48,8,768]{2,1,0:T(8,128)(2,1)}, u32[]{:S(2)}) copy-start(bf16[48,8,768]{2,1,0:T(8,128)(2,1)} %param.22) | copy-start | bytes 1769476
  13.3 10.3 copy-start.217
  13.4 13.1 copy-start.114
  15.3 15.5 %all-to-all-start.1 = ((s32[3,16,1]{0,2,1:T(1,128)}), s32[3,16,1]{0,2,1:T(1,128)S(1)}, u32[]{:S(2)}, u32[]{:S(2)}) async-start(s32[3,16,1]{0,2,1:T(1,128)} %copy.178), calls=%async_computation.1 | async-start | bytes 16384 | tf_op jit(solution)/shard_map/all_to_all | solution.py:132
  27.7 9.6 copy-start.176
  28.6 54.0 %copy-start.177 = (bf16[48,384]{1,0:T(8,128)(2,1)S(1)}, bf16[48,384]{1,0:T(8,128)(2,1)}, u32[]{:S(2)}) copy-start(bf16[48,384]{1,0:T(8,128)(2,1)} %param.26) | copy-start | bytes 110596
  28.6 95.0 %copy-start.178 = (bf16[48,384]{1,0:T(8,128)(2,1)S(1)}, bf16[48,384]{1,0:T(8,128)(2,1)}, u32[]{:S(2)}) copy-start(bf16[48,384]{1,0:T(8,128)(2,1)} %param.27) | copy-start | bytes 110596
  30.8 181.3 %copy-start.173 = (s32[3,16,1]{0,2,1:T(1,128)}, s32[3,16,1]{0,2,1:T(1,128)S(1)}, u32[]{:S(2)}) copy-start(s32[3,16,1]{0,2,1:T(1,128)S(1)} %all-to-all-done.1) | copy-start | bytes 580
  30.8 132.8 %all-to-all-start = ((bf16[3,16,8,768]{3,2,0,1:T(8,128)(2,1)}), bf16[3,16,8,768]{3,2,0,1:T(8,128)(2,1)S(1)}, u32[]{:S(2)}, u32[]{:S(2)}) async-start(bf16[3,16,8,768]{3,2,0,1:T(8,128)(2,1)} %copy.184), calls=%async_computation | async-start | bytes 1179648 | tf_op jit(solution)/shard_map/all_to_all | solution.py:130
  36.6 131.4 %copy-start.215 = (bf16[1,384]{1,0:T(2,128)(2,1)S(1)}, bf16[1,384]{1,0:T(2,128)(2,1)}, u32[]{:S(2)}) copy-start(bf16[1,384]{1,0:T(2,128)(2,1)} %param.28) | copy-start | bytes 2308
  36.6 131.4 %copy-start.216 = (bf16[1,384]{1,0:T(2,128)(2,1)S(1)}, bf16[1,384]{1,0:T(2,128)(2,1)}, u32[]{:S(2)}) copy-start(bf16[1,384]{1,0:T(2,128)(2,1)} %param.29) | copy-start | bytes 2308
  36.6 131.4 %copy-start.179 = (bf16[384,48]{0,1:T(8,128)(2,1)S(1)}, bf16[384,48]{0,1:T(8,128)(2,1)}, u32[]{:S(2)}) copy-start(bf16[384,48]{0,1:T(8,128)(2,1)} %param.30) | copy-start | bytes 110596
  82.5 156.1 %copy-start.4 = (bf16[768,384]{1,0:T(8,128)(2,1)}, bf16[768,384]{1,0:T(8,128)(2,1)S(1)}, u32[]{:S(2)}) copy-start(bf16[768,384]{1,0:T(8,128)(2,1)S(1)} %all_gather.52) | copy-start | bytes 1769476
  123.6 104.4 %copy-start.12 = (bf16[768,384]{1,0:T(8,128)(2,1)}, bf16[768,384]{1,0:T(8,128)(2,1)S(1)}, u32[]{:S(2)}) copy-start(bf16[768,384]{1,0:T(8,128)(2,1)S(1)} %all_gather.53) | copy-start | bytes 1769476
  163.6 77.3 %copy-start.10 = (bf16[768,384]{1,0:T(8,128)(2,1)}, bf16[768,384]{1,0:T(8,128)(2,1)S(1)}, u32[]{:S(2)}) copy-start(bf16[768,384]{1,0:T(8,128)(2,1)S(1)} %all_gather.51) | copy-start | bytes 1769476
  163.6 53.2 %all-to-all-start.3 = ((bf16[3,16,8,768]{3,2,0,1:T(8,128)(2,1)}), bf16[3,16,8,768]{3,2,0,1:T(8,128)(2,1)}, u32[]{:S(2)}, u32[]{:S(2)}) async-start(bf16[3,16,8,768]{3,2,0,1:T(8,128)(2,1)} %copy.202), calls=%async_computation.9 | async-start | bytes 1179648 | tf_op jit(solution)/shard_map/all_to_all | solution.py:131
  167.9 184.3 %reduce-scatter.28.cloned.1.call-start = ((), (), s32[]{:S(2)}) async-start(), calls=%async_computation.24 | async-start | bytes 1179648 | tf_op jit(solution)/shard_map/reduce_scatter | solution.py:204
  212.1 24.3 %copy-start.6 = (bf16[384,768]{0,1:T(8,128)(2,1)}, bf16[384,768]{0,1:T(8,128)(2,1)S(1)}, u32[]{:S(2)}) copy-start(bf16[384,768]{0,1:T(8,128)(2,1)S(1)} %all_gather.54) | copy-start | bytes 1769476
  238.6 113.6 %reduce-scatter.32.cloned.1.call-start = ((), (), s32[]{:S(2)}) async-start(), calls=%async_computation.28 | async-start | bytes 1179648 | tf_op jit(solution)/shard_map/reduce_scatter | solution.py:204
  249.2 10.7 copy-start.21
  251.9 100.3 %reduce-scatter.36.cloned.1.call-start = ((), (), s32[]{:S(2)}) async-start(), calls=%async_computation.30 | async-start | bytes 1179648 | tf_op jit(solution)/shard_map/reduce_scatter | solution.py:204
  270.8 87.6 %all-gather.6.cloned.1.call-start = ((), (), s32[]{:S(2)}) async-start(), calls=%async_computation.25 | async-start | bytes 2506752 | tf_op jit(solution)/shard_map/all_gather | solution.py:157
  271.4 127.0 %all-gather.8.cloned.1.call-start = ((), (), s32[]{:S(2)}) async-start(), calls=%async_computation.26 | async-start | bytes 2506752 | tf_op jit(solution)/shard_map/all_gather | solution.py:158
  272.0 155.0 %reduce-scatter.30.cloned.1.call-start = ((), (), s32[]{:S(2)}) async-start(), calls=%async_computation.27 | async-start | bytes 1179648 | tf_op jit(solution)/shard_map/reduce_scatter | solution.py:221
  402.0 24.9 %reduce-scatter.34.cloned.1.call-start = ((), (), s32[]{:S(2)}) async-start(), calls=%async_computation.29 | async-start | bytes 1179648 | tf_op jit(solution)/shard_map/reduce_scatter | solution.py:221
  413.8 18.1 %reduce-scatter.38.cloned.1.call-start = ((), (), s32[]{:S(2)}) async-start(), calls=%async_computation.31 | async-start | bytes 1179648 | tf_op jit(solution)/shard_map/reduce_scatter | solution.py:221
  424.9 29.6 %reduce-scatter.44.cloned.1.call-start = ((), (), s32[]{:S(2)}) async-start(), calls=%async_computation.34 | async-start | bytes 1179648 | tf_op jit(solution)/shard_map/reduce_scatter | solution.py:270
  425.6 143.9 %copy-start.118 = (f32[768]{0:T(1024)}, f32[768]{0:T(1024)S(1)}, u32[]{:S(2)}) copy-start(f32[768]{0:T(1024)S(1)} %convert_element_type.555) | copy-start | bytes 9220
  444.9 30.3 %reduce-scatter.40.cloned.1.call-start = ((), (), s32[]{:S(2)}) async-start(), calls=%async_computation.32 | async-start | bytes 1179648 | tf_op jit(solution)/shard_map/reduce_scatter | solution.py:270
  465.6 30.5 %reduce-scatter.42.cloned.1.call-start = ((), (), s32[]{:S(2)}) async-start(), calls=%async_computation.33 | async-start | bytes 1179648 | tf_op jit(solution)/shard_map/reduce_scatter | solution.py:270
  486.5 86.1 %reduce-scatter.60.cloned.1.call-start = ((), (), s32[]{:S(2)}) async-start(), calls=%async_computation.42 | async-start | bytes 589824
  529.6 44.7 %reduce-scatter.62.cloned.1.call-start = ((), (), s32[]{:S(2)}) async-start(), calls=%async_computation.43 | async-start | bytes 589824
  538.6 37.4 %reduce-scatter.58.cloned.1.call-start = ((), (), s32[]{:S(2)}) async-start(), calls=%async_computation.41 | async-start | bytes 589824
  541.9 149.8 %reduce-scatter.64.cloned.1.call-start = ((), (), s32[]{:S(2)}) async-start(), calls=%async_computation.44 | async-start | bytes 835584
  543.4 276.3 %reduce-scatter.52.cloned.1.call-start = ((), (), s32[]{:S(2)}) async-start(), calls=%async_computation.38 | async-start | bytes 1253376 | tf_op jit(solution)/shard_map/reduce_scatter | solution.py:354
  546.4 401.1 %reduce-scatter.50.cloned.1.call-start = ((), (), s32[]{:S(2)}) async-start(), calls=%async_computation.37 | async-start | bytes 1253376 | tf_op jit(solution)/shard_map/reduce_scatter | solution.py:353
  549.9 525.4 %reduce-scatter.48.cloned.1.call-start = ((), (), s32[]{:S(2)}) async-start(), calls=%async_computation.36 | async-start | bytes 1253376 | tf_op jit(solution)/shard_map/reduce_scatter | solution.py:352
  553.2 649.9 %reduce-scatter.46.cloned.1.call-start = ((), (), s32[]{:S(2)}) async-start(), calls=%async_computation.35 | async-start | bytes 1253376 | tf_op jit(solution)/shard_map/reduce_scatter | solution.py:351
  556.2 787.8 %reduce-scatter.56.cloned.1.call-start = ((), (), s32[]{:S(2)}) async-start(), calls=%async_computation.40 | async-start | bytes 5013504 | tf_op jit(solution)/shard_map/reduce_scatter | solution.py:356
  561.7 925.0 %reduce-scatter.54.cloned.1.call-start = ((), (), s32[]{:S(2)}) async-start(), calls=%async_computation.39 | async-start | bytes 5013504 | tf_op jit(solution)/shard_map/reduce_scatter | solution.py:355
  580.7 8.6 copy-start.201
  580.7 8.6 copy-start.200
  580.7 8.6 copy-start.199
  580.7 8.6 copy-start.198
  580.7 8.6 copy-start.197
  580.7 8.7 copy-start.196
  580.7 8.7 copy-start.188
  580.7 8.7 copy-start.187
  580.7 8.7 copy-start.190
  580.8 8.7 copy-start.189
  582.0 115.8 %copy-start.203 = (f32[6,64]{1,0:T(8,128)S(1)}, f32[6,64]{1,0:T(8,128)}, u32[]{:S(2)}) copy-start(f32[6,64]{1,0:T(8,128)} %get-tuple-element.161) | copy-start | bytes 4612
  582.0 115.8 %copy-start.205 = (f32[6,64]{1,0:T(8,128)S(1)}, f32[6,64]{1,0:T(8,128)}, u32[]{:S(2)}) copy-start(f32[6,64]{1,0:T(8,128)} %get-tuple-element.157) | copy-start | bytes 4612
  582.0 115.8 %copy-start.207 = (f32[6,64]{1,0:T(8,128)S(1)}, f32[6,64]{1,0:T(8,128)}, u32[]{:S(2)}) copy-start(f32[6,64]{1,0:T(8,128)} %get-tuple-element.159) | copy-start | bytes 4612
  582.0 115.8 %copy-start.192 = (f32[768]{0:T(1024)S(1)}, f32[768]{0:T(1024)}, u32[]{:S(2)}) copy-start(f32[768]{0:T(1024)} %get-tuple-element.24) | copy-start | bytes 9220
  582.0 115.8 %copy-start.191 = (f32[768]{0:T(1024)S(1)}, f32[768]{0:T(1024)}, u32[]{:S(2)}) copy-start(f32[768]{0:T(1024)} %get-tuple-element.52) | copy-start | bytes 9220
  582.0 115.8 %copy-start.195 = (f32[768]{0:T(1024)S(1)}, f32[768]{0:T(1024)}, u32[]{:S(2)}) copy-start(f32[768]{0:T(1024)} %get-tuple-element.72) | copy-start | bytes 9220
  582.0 115.9 %copy-start.194 = (f32[768]{0:T(1024)S(1)}, f32[768]{0:T(1024)}, u32[]{:S(2)}) copy-start(f32[768]{0:T(1024)} %get-tuple-element.127) | copy-start | bytes 9220
  582.0 115.9 %copy-start.193 = (f32[768]{0:T(1024)S(1)}, f32[768]{0:T(1024)}, u32[]{:S(2)}) copy-start(f32[768]{0:T(1024)} %get-tuple-element.129) | copy-start | bytes 9220
  582.0 116.0 %copy-start.202 = (f32[6,64]{1,0:T(8,128)S(1)}, f32[6,64]{1,0:T(8,128)}, u32[]{:S(2)}) copy-start(f32[6,64]{1,0:T(8,128)} %get-tuple-element.167) | copy-start | bytes 4612
  582.0 115.9 %copy-start.204 = (f32[6,64]{1,0:T(8,128)S(1)}, f32[6,64]{1,0:T(8,128)}, u32[]{:S(2)}) copy-start(f32[6,64]{1,0:T(8,128)} %get-tuple-element.163) | copy-start | bytes 4612
  582.0 115.9 %copy-start.206 = (f32[6,64]{1,0:T(8,128)S(1)}, f32[6,64]{1,0:T(8,128)}, u32[]{:S(2)}) copy-start(f32[6,64]{1,0:T(8,128)} %get-tuple-element.165) | copy-start | bytes 4612
  582.0 111.0 %all-to-all-start.4 = ((bf16[3,16,8,768]{3,2,0,1:T(8,128)(2,1)}), bf16[3,16,8,768]{3,2,0,1:T(8,128)(2,1)S(1)}, u32[]{:S(2)}, u32[]{:S(2)}) async-start(bf16[3,16,8,768]{3,2,0,1:T(8,128)(2,1)} %get-tuple-element.131), calls=%async_computation.13 | async-start | bytes 1179648 | tf_op jit(solution)/shard_map/all_to_all | solution.py:342
  693.0 48.6 %all-to-all-start.2 = ((bf16[3,16,8,768]{3,2,0,1:T(8,128)(2,1)}), bf16[3,16,8,768]{3,2,0,1:T(8,128)(2,1)S(1)}, u32[]{:S(2)}, u32[]{:S(2)}) async-start(bf16[3,16,8,768]{3,2,0,1:T(8,128)(2,1)} %get-tuple-element.132), calls=%async_computation.8 | async-start | bytes 1179648 | tf_op jit(solution)/shard_map/all_to_all | solution.py:341
  740.8 745.9 %copy-start.1 = (bf16[48,8,768]{2,1,0:T(8,128)(2,1)S(1)}, bf16[48,8,768]{2,1,0:T(8,128)(2,1)}, u32[]{:S(2)}) copy-start(bf16[48,8,768]{2,1,0:T(8,128)(2,1)} %param.22) | copy-start | bytes 1769476
  (196 other events, 540.3 us)
Sparse Core Ops, SparseCore 0:
  238.7 4.7 reduce-scatter.27
  252.0 4.8 reduce-scatter.31
  270.9 4.8 reduce-scatter.35
  402.1 6.5 reduce-scatter.29
  413.9 6.2 reduce-scatter.33
  425.0 6.7 reduce-scatter.37
  445.0 9.4 reduce-scatter.43
  465.7 9.3 reduce-scatter.39
  486.6 9.4 reduce-scatter.41
  529.7 8.9 reduce-scatter.59
  541.0 8.9 reduce-scatter.61
  552.1 8.9 reduce-scatter.57
  565.8 125.7 reduce-scatter.63
  696.8 122.8 reduce-scatter.51
  824.9 122.5 reduce-scatter.49
  952.7 122.6 reduce-scatter.47
  1080.5 122.5 reduce-scatter.45
  1208.7 135.1 reduce-scatter.55
  1350.5 136.1 reduce-scatter.53
Sparse Core Ops, SparseCore 1:
  274.5 59.6 all-gather.5
  337.2 61.1 all-gather.7
where the time goes:
time: 1510 us; the launch traced here: 1490 us
  waiting for transfers between devices  901 us (60%)
  blocking collectives  311 us (21%)
  matrix products  107 us (7%)
  local copies, waits for them, and re-layouts  70.7 us (5%)
  other arithmetic  54 us (4%)
  starting transfers between devices  30.5 us (2%)
  between operations  20.2 us (1%)
    reduce_scatter x1, waiting for transfers between devices, shards(): lax.psum_scatter(acc_inner, 'dp', scatter_dimension=0, tiled=True)  143 us
    reduce_scatter x1, waiting for transfers between devices, shards(): lax.psum_scatter(acc_outer, 'dp', scatter_dimension=1, tiled=True)  141 us
    reduce_scatter x1, waiting for transfers between devices, shards(): lax.psum_scatter(acc_key, 'dp', scatter_dimension=0, tiled=True)  128 us
    reduce_scatter x1, waiting for transfers between devices, shards(): lax.psum_scatter(acc_value, 'dp', scatter_dimension=0, tiled=True)  128 us
    reduce_scatter x1, waiting for transfers between devices, shards(): lax.psum_scatter(acc_query, 'dp', scatter_dimension=0, tiled=True)  128 us
    unnamed x25, waiting for transfers between devices  104 us
    reduce_scatter x1, waiting for transfers between devices, shards(): lax.psum_scatter(acc_out, 'dp', scatter_dimension=1, tiled=True)  76.1 us
    unnamed x1, blocking collectives  72.9 us
  transfers between devices with their start and end apart: 26, of which 13 were waited for; matrix products, arithmetic and copies ran while one was open for 9% of the time, Pallas kernels for 0%

commit v1 on v0

--- a/solution.py
+++ b/solution.py
@@ -4,6 +4,8 @@
 import jax
 import jax.numpy as jnp
 from jax import lax
+from jax.experimental import pallas as pl
+from jax.experimental.pallas import tpu as pltpu
 from jax.sharding import PartitionSpec as P
 
 HEADS = 12
@@ -82,6 +84,667 @@
         * score_scale
     )
     return (grad_query_rows, grad_keys, grad_values)
+
+
+MESH = pl.DeviceIdType.MESH
+
+
+def flip(place, bit):
+    return place + bit * (1 - 2 * ((place // bit) % 2))
+
+
+def bit_of(place, bit):
+    return (place // bit) % 2
+
+
+def orders_of(count):
+    bits = [1 << i for i in range(count.bit_length() - 1)][::-1]
+    return (tuple(bits), tuple(bits[:-2] + bits[-2:][::-1]))
+
+
+def greet(dp_count, place, half):
+    barrier = pltpu.get_barrier_semaphore()
+
+    def hello(step, carry):
+        peer = lax.rem(place + step, dp_count)
+        pl.semaphore_signal(barrier, inc=1, device_id=(peer, half), device_id_type=MESH)
+        return carry
+
+    lax.fori_loop(1, dp_count, hello, 0)
+    pl.semaphore_wait(barrier, dp_count - 1)
+
+
+def exchange_start(dp_count, place, half, send_ref, recv_ref, send_sem, recv_sem):
+    def push(step, carry):
+        peer = lax.rem(place + step, dp_count)
+        pltpu.make_async_remote_copy(
+            src_ref=send_ref.at[peer],
+            dst_ref=recv_ref.at[place],
+            send_sem=send_sem.at[step],
+            recv_sem=recv_sem.at[step],
+            device_id=(peer, half),
+            device_id_type=MESH,
+        ).start()
+        return carry
+
+    lax.fori_loop(1, dp_count, push, 0)
+
+
+def exchange_wait(dp_count, place, half, send_ref, recv_ref, send_sem, recv_sem):
+    def settle(step, carry):
+        source = lax.rem(place + dp_count - step, dp_count)
+        pltpu.make_async_remote_copy(
+            src_ref=send_ref.at[source],
+            dst_ref=recv_ref.at[source],
+            send_sem=send_sem.at[step],
+            recv_sem=recv_sem.at[step],
+            device_id=(source, half),
+            device_id_type=MESH,
+        ).wait()
+        return carry
+
+    lax.fori_loop(1, dp_count, settle, 0)
+
+
+def copy_block(send_ref, recv_ref, place):
+    recv_ref[place] = send_ref[place]
+
+
+class Gather:
+    def __init__(self, dp_count, place, half, order, ref, start, size, send_sem, recv_sem):
+        self.place, self.half, self.order = place, half, order
+        self.bits = [1 << i for i in range(dp_count.bit_length() - 1)][::-1]
+        self.ref, self.cols = ref, pl.ds(start, size)
+        self.send_sem, self.recv_sem = send_sem, recv_sem
+
+    def copy(self, stage):
+        done = self.order[:stage]
+        index = tuple(
+            slice(None) if bit in done else bit_of(self.place, bit) for bit in self.bits
+        ) + (slice(None), self.cols)
+        return pltpu.make_async_remote_copy(
+            src_ref=self.ref.at[index],
+            dst_ref=self.ref.at[index],
+            send_sem=self.send_sem.at[stage],
+            recv_sem=self.recv_sem.at[stage],
+            device_id=(flip(self.place, self.order[stage]), self.half),
+            device_id_type=MESH,
+        )
+
+    def start(self, stage):
+        self.copy(stage).start()
+
+    def wait_recv(self, stage):
+        self.copy(stage).wait_recv()
+
+    def wait_send(self, stage):
+        self.copy(stage).wait_send()
+
+
+class Scatter:
+    def __init__(self, dp_count, place, half, order, ref, start, size, landing, send_sem, recv_sem):
+        self.place, self.half = place, half
+        self.order = order[::-1]
+        self.bits = [1 << i for i in range(dp_count.bit_length() - 1)][::-1]
+        self.ref, self.start_col, self.size = ref, start, size
+        self.landing = landing
+        self.send_sem, self.recv_sem = send_sem, recv_sem
+
+    def view(self, stage, chosen):
+        left = [bit for bit in self.bits if bit not in self.order[:stage]]
+        own = bit_of(self.place, self.order[stage])
+        index = tuple(
+            (own if chosen == "own" else 1 - own) if bit == self.order[stage] else slice(None)
+            for bit in left
+        )
+        if stage == 0:
+            return self.ref.at[index + (slice(None), pl.ds(self.start_col, self.size))]
+        return self.landing[stage - 1].at[index]
+
+    def copy(self, stage):
+        return pltpu.make_async_remote_copy(
+            src_ref=self.view(stage, "other"),
+            dst_ref=self.landing[stage],
+            send_sem=self.send_sem.at[stage],
+            recv_sem=self.recv_sem.at[stage],
+            device_id=(flip(self.place, self.order[stage]), self.half),
+            device_id_type=MESH,
+        )
+
+    def start(self, stage):
+        self.copy(stage).start()
+
+    def wait_recv(self, stage):
+        self.copy(stage).wait_recv()
+
+    def wait_send(self, stage):
+        self.copy(stage).wait_send()
+
+    def add(self, stage, out_ref=None):
+        kept = self.view(stage, "own")
+        land = self.landing[stage]
+        lead = land.shape[:-2]
+        count = math.prod(lead)
+
+        def one(i, carry):
+            index, rest = [], i
+            for extent in lead[::-1]:
+                index.append(lax.rem(rest, extent))
+                rest = rest // extent
+            index = tuple(index[::-1])
+            total = kept[index].astype(jnp.float32) + land[index].astype(jnp.float32)
+            land[index] = total.astype(land.dtype)
+            return carry
+
+        if out_ref is not None:
+            out_ref[:, pl.ds(self.start_col, self.size)] = kept[...].astype(
+                jnp.float32
+            ) + land[...].astype(jnp.float32)
+        elif count == 1:
+            one(0, 0)
+        else:
+            lax.fori_loop(0, count, one, 0)
+
+
+def bring_in(
+    dp_count,
+    plan,
+    x_ref,
+    dy_ref,
+    w_ref,
+    v_ref,
+    xr_ref,
+    dyr_ref,
+    full_ref,
+    vec_ref,
+    vec_buf,
+    vec_land,
+    x_sems,
+    dy_sems,
+    w_sems,
+    v_sems,
+):
+    place, half = lax.axis_index("dp"), lax.axis_index("tensor")
+    stages = dp_count.bit_length() - 1
+    orders = orders_of(dp_count)
+    bits = orders[0]
+    own = tuple(bit_of(place, bit) for bit in bits)
+    full_ref[own] = w_ref[...]
+    vec_buf[0] = v_ref[...]
+    greet(dp_count, place, half)
+    gathers = [
+        Gather(
+            dp_count, place, half, orders[which], full_ref, start, size, w_sems.at[0, i], w_sems.at[1, i]
+        )
+        for i, (group, which, start, size) in enumerate(plan)
+    ]
+    groups = max(group for group, _, _, _ in plan) + 1
+    exchange_start(dp_count, place, half, x_ref, xr_ref, x_sems.at[0], x_sems.at[1])
+
+    def vec_copy(stage):
+        return pltpu.make_async_remote_copy(
+            src_ref=vec_buf.at[stage],
+            dst_ref=vec_land.at[stage],
+            send_sem=v_sems.at[0, stage],
+            recv_sem=v_sems.at[1, stage],
+            device_id=(flip(place, bits[stage]), half),
+            device_id_type=MESH,
+        )
+
+    for step in range(groups + stages - 1):
+        for (group, _, _, _), gather in zip(plan, gathers):
+            stage = step - group
+            if 0 <= stage < stages:
+                if stage > 0:
+                    gather.wait_recv(stage - 1)
+                gather.start(stage)
+        if step < stages:
+            vec_copy(step).start()
+            vec_copy(step).wait()
+            if step < stages - 1:
+                vec_buf[step + 1] = vec_buf[step] + vec_land[step]
+            else:
+                vec_ref[...] = vec_buf[step] + vec_land[step]
+        if step == stages - 1:
+            exchange_start(dp_count, place, half, dy_ref, dyr_ref, dy_sems.at[0], dy_sems.at[1])
+    copy_block(x_ref, xr_ref, place)
+    copy_block(dy_ref, dyr_ref, place)
+    for gather in gathers:
+        gather.wait_recv(stages - 1)
+    for gather in gathers:
+        for stage in range(stages):
+            gather.wait_send(stage)
+    exchange_wait(dp_count, place, half, x_ref, xr_ref, x_sems.at[0], x_sems.at[1])
+    exchange_wait(dp_count, place, half, dy_ref, dyr_ref, dy_sems.at[0], dy_sems.at[1])
+
+
+def send_out(
+    dp_count,
+    plan,
+    out_ref,
+    gx_ref,
+    g_ref,
+    v_ref,
+    back_ref,
+    gback_ref,
+    sum_ref,
+    vec_ref,
+    *scratch,
+):
+    stages = dp_count.bit_length() - 1
+    landings, rest = scratch[: len(plan) * stages], scratch[len(plan) * stages :]
+    vec_buf, vec_land, x_sems, dy_sems, w_sems, v_sems = rest
+    place, half = lax.axis_index("dp"), lax.axis_index("tensor")
+    orders = orders_of(dp_count)
+    bits = orders[0]
+    vec_buf[0] = v_ref[...]
+    greet(dp_count, place, half)
+    scatters = [
+        Scatter(
+            dp_count,
+            place,
+            half,
+            orders[which],
+            g_ref,
+            start,
+            size,
+            landings[i * stages : (i + 1) * stages],
+            w_sems.at[0, i],
+            w_sems.at[1, i],
+        )
+        for i, (group, which, start, size) in enumerate(plan)
+    ]
+    groups = max(group for group, _, _, _ in plan) + 1
+    exchange_start(dp_count, place, half, out_ref, back_ref, x_sems.at[0], x_sems.at[1])
+
+    def vec_copy(stage):
+        return pltpu.make_async_remote_copy(
+            src_ref=vec_buf.at[stage],
+            dst_ref=vec_land.at[stage],
+            send_sem=v_sems.at[0, stage],
+            recv_sem=v_sems.at[1, stage],
+            device_id=(flip(place, bits[stage]), half),
+            device_id_type=MESH,
+        )
+
+    for step in range(groups + stages):
+        for (group, _, _, _), scatter in zip(plan, scatters):
+            stage = step - group
+            if 0 <= stage <= stages:
+                if stage > 0:
+                    scatter.wait_recv(stage - 1)
+                    scatter.add(stage - 1, sum_ref if stage == stages else None)
+                if stage < stages:
+                    scatter.start(stage)
+        if step < stages:
+            vec_copy(step).start()
+            vec_copy(step).wait()
+            if step < stages - 1:
+                vec_buf[step + 1] = vec_buf[step] + vec_land[step]
+            else:
+                vec_ref[...] = vec_buf[step] + vec_land[step]
+        if step == stages - 1:
+            exchange_start(dp_count, place, half, gx_ref, gback_ref, dy_sems.at[0], dy_sems.at[1])
+    copy_block(out_ref, back_ref, place)
+    copy_block(gx_ref, gback_ref, place)
+    for scatter in scatters:
+        for stage in range(stages):
+            scatter.wait_send(stage)
+    exchange_wait(dp_count, place, half, out_ref, back_ref, x_sems.at[0], x_sems.at[1])
+    exchange_wait(dp_count, place, half, gx_ref, gback_ref, dy_sems.at[0], dy_sems.at[1])
+
+
+def plan_of(columns, groups):
+    size = columns // (2 * groups)
+    return [
+        (group, which, (2 * group + which) * size, size) for group in range(groups) for which in range(2)
+    ]
+
+
+def call_bring_in(dp_count, tokens_by, grads_by, shard, vectors):
+    bits = (2,) * (dp_count.bit_length() - 1)
+    stages = len(bits)
+    plan = plan_of(shard.shape[1], 3)
+    spec = pl.BlockSpec(memory_space=pltpu.VMEM)
+    dma = pltpu.SemaphoreType.DMA
+    return pl.pallas_call(
+        partial(bring_in, dp_count, plan),
+        out_shape=(
+            jax.ShapeDtypeStruct(tokens_by.shape, tokens_by.dtype),
+            jax.ShapeDtypeStruct(grads_by.shape, grads_by.dtype),
+            jax.ShapeDtypeStruct(bits + shard.shape, shard.dtype),
+            jax.ShapeDtypeStruct(vectors.shape, vectors.dtype),
+        ),
+        in_specs=[spec] * 4,
+        out_specs=[spec] * 4,
+        scratch_shapes=[
+            pltpu.VMEM((stages,) + vectors.shape, vectors.dtype),
+            pltpu.VMEM((stages,) + vectors.shape, vectors.dtype),
+            dma((2, dp_count)),
+            dma((2, dp_count)),
+            dma((2, len(plan), stages)),
+            dma((2, stages)),
+        ],
+        compiler_params=pltpu.CompilerParams(
+            collective_id=0, has_side_effects=True, vmem_limit_bytes=40 << 20
+        ),
+        name="bring_in",
+    )(tokens_by, grads_by, shard, vectors)
+
+
+def call_send_out(dp_count, out_by, gx_by, grads, vectors):
+    bits = (2,) * (dp_count.bit_length() - 1)
+    stages = len(bits)
+    plan = plan_of(grads.shape[-1], 3)
+    rows = grads.shape[-2]
+    spec = pl.BlockSpec(memory_space=pltpu.VMEM)
+    dma = pltpu.SemaphoreType.DMA
+    landings = [
+        pltpu.VMEM((2,) * (stages - 1 - stage) + (rows, size), grads.dtype)
+        for _, _, _, size in plan
+        for stage in range(stages)
+    ]
+    return pl.pallas_call(
+        partial(send_out, dp_count, plan),
+        out_shape=(
+            jax.ShapeDtypeStruct(out_by.shape, out_by.dtype),
+            jax.ShapeDtypeStruct(gx_by.shape, gx_by.dtype),
+            jax.ShapeDtypeStruct((rows, grads.shape[-1]), jnp.float32),
+            jax.ShapeDtypeStruct(vectors.shape, vectors.dtype),
+        ),
+        in_specs=[spec] * 4,
+        out_specs=[spec] * 4,
+        scratch_shapes=landings
+        + [
+            pltpu.VMEM((stages,) + vectors.shape, vectors.dtype),
+            pltpu.VMEM((stages,) + vectors.shape, vectors.dtype),
+            dma((2, dp_count)),
+            dma((2, dp_count)),
+            dma((2, len(plan), stages)),
+            dma((2, stages)),
+        ],
+        compiler_params=pltpu.CompilerParams(
+            collective_id=1, has_side_effects=True, vmem_limit_bytes=40 << 20
+        ),
+        name="send_out",
+    )(out_by, gx_by, grads, vectors)
+
+
+def segment_at(seq_lengths, places, half_rows):
+    seq_ends = jnp.cumsum(seq_lengths)
+    within = jnp.arange(2 * half_rows, dtype=jnp.int32)
+    positions = (places[:, None] * (2 * half_rows) + within[None, :]).reshape(-1)
+    return jnp.sum((positions[:, None] >= seq_ends[None, :-1]).astype(jnp.int32), axis=1)
+
+
+def shards_fast(
+    tokens,
+    cotangent,
+    block_route,
+    lengths,
+    w_query,
+    w_key,
+    w_value,
+    b_query,
+    b_value,
+    w_out,
+    b_out,
+    gain_attn,
+    shift_attn,
+    w_inner,
+    b_inner,
+    w_outer,
+    b_outer,
+    gain_ffn,
+    shift_ffn,
+):
+    dp_count = lax.axis_size("dp")
+    micro_count = lengths.shape[0]
+    half_rows = tokens.shape[1]
+    model_width = tokens.shape[2]
+    half_width = w_query.shape[1]
+    ff_half = w_inner.shape[1]
+    local_heads = HEADS // lax.axis_size("tensor")
+    score_scale = HD ** (-0.5)
+    place = lax.axis_index("dp")
+    blocks = tokens.reshape(micro_count, dp_count, half_rows, model_width)
+    upstream = cotangent.reshape(micro_count, dp_count, half_rows, model_width)
+    target = block_route.reshape(micro_count, dp_count)
+    dest_dev = target // (micro_count * dp_count)
+    inverse = jnp.argmax(
+        dest_dev[:, None, :] == jnp.arange(dp_count, dtype=jnp.int32)[None, :, None], axis=2
+    )
+    by_dest = jnp.take_along_axis(blocks, inverse[:, :, None, None], axis=1).swapaxes(0, 1)
+    grad_dest = jnp.take_along_axis(upstream, inverse[:, :, None, None], axis=1).swapaxes(0, 1)
+    shard = jnp.concatenate([w_query, w_key, w_value, w_out.T, w_inner, w_outer.T], axis=1)
+    own_width = model_width // dp_count
+    six = jnp.stack([b_out, gain_attn, shift_attn, b_outer, gain_ffn, shift_ffn]).astype(jnp.float32)
+    vectors = jnp.zeros((16, model_width), jnp.float32)
+    vectors = lax.dynamic_update_slice(vectors, six, (jnp.int32(0), place * own_width))
+    own_inner = b_inner.shape[1]
+    bias_row = lax.dynamic_update_slice(
+        jnp.zeros((1, ff_half), jnp.float32), b_inner.astype(jnp.float32), (jnp.int32(0), place * own_inner)
+    ).reshape(2, model_width)
+    vectors = lax.dynamic_update_slice(vectors, bias_row, (jnp.int32(6), jnp.int32(0)))
+    vectors = lax.dynamic_update_slice(
+        vectors,
+        block_route.astype(jnp.float32)[None],
+        (jnp.int32(8), place * (micro_count * dp_count)),
+    )
+    xr, dyr, full, vec = call_bring_in(dp_count, by_dest, grad_dest, shard, vectors)
+    route = vec[8].astype(jnp.int32).reshape(dp_count, micro_count, dp_count)
+    mine = (route // (micro_count * dp_count)) == place
+    arrived_place = jnp.sum(jnp.where(mine, route % dp_count, 0), axis=2).T
+    full = full.reshape(model_width, -1)
+    full_query, full_key, full_value, full_out, full_inner, full_outer = jnp.split(
+        full, [half_width, 2 * half_width, 3 * half_width, 4 * half_width, 4 * half_width + ff_half], axis=1
+    )
+    full_out, full_outer = full_out.T, full_outer.T
+    bias_out, full_gain_attn, full_shift_attn, bias_outer, full_gain_ffn, full_shift_ffn = vec[:6]
+    bias_inner = vec[6:8].reshape(1, ff_half)
+    bin_tokens = xr.swapaxes(0, 1)
+    bin_grads = dyr.swapaxes(0, 1)
+    acc_query = jnp.zeros((model_width, half_width), jnp.float32)
+    acc_key = acc_value = acc_query
+    acc_out = jnp.zeros((half_width, model_width), jnp.float32)
+    acc_inner = jnp.zeros((model_width, ff_half), jnp.float32)
+    acc_outer = jnp.zeros((ff_half, model_width), jnp.float32)
+    acc_bias_query = jnp.zeros((1, half_width), jnp.float32)
+    acc_bias_value = acc_bias_query
+    acc_bias_inner = jnp.zeros((1, ff_half), jnp.float32)
+    acc_vectors = jnp.zeros((6, model_width), jnp.float32)
+    out_bins = []
+    grad_bins = []
+    for micro_step in range(micro_count):
+        own_rows = bin_tokens[micro_step]
+        whole_bin = lax.all_gather(own_rows, "tensor", axis=1, tiled=True).reshape(-1, model_width)
+        bin_rows = whole_bin.shape[0]
+        block_rows = math.gcd(bin_rows, 512)
+        segment = segment_at(lengths[micro_step], arrived_place[micro_step], half_rows)
+        query = (
+            jnp.dot(whole_bin, full_query, preferred_element_type=jnp.float32) + b_query[0]
+        ).astype(jnp.bfloat16)
+        keys = jnp.dot(whole_bin, full_key, preferred_element_type=jnp.float32).astype(jnp.bfloat16)
+        values = (
+            jnp.dot(whole_bin, full_value, preferred_element_type=jnp.float32) + b_value[0]
+        ).astype(jnp.bfloat16)
+        query_heads = query.reshape(bin_rows, local_heads, HD)
+        key_heads = keys.reshape(bin_rows, local_heads, HD)
+        value_heads = values.reshape(bin_rows, local_heads, HD)
+        attn_heads, log_totals = attend_forward(
+            query_heads, key_heads, value_heads, segment, block_rows, score_scale
+        )
+        attn = attn_heads.reshape(bin_rows, local_heads * HD)
+        attn_partial = jnp.dot(attn, full_out, preferred_element_type=jnp.float32).reshape(
+            dp_count, -1, model_width
+        )
+        branch = lax.psum_scatter(attn_partial, "tensor", scatter_dimension=1, tiled=True).reshape(
+            -1, model_width
+        )
+        mid = own_rows.reshape(-1, model_width).astype(jnp.float32) + branch + bias_out
+        hidden, normed_attn, spread_attn = layer_norm(mid, full_gain_attn, full_shift_attn)
+        hidden_low = hidden.astype(jnp.bfloat16).reshape(dp_count, half_rows, model_width)
+        hidden_whole = lax.all_gather(hidden_low, "tensor", axis=1, tiled=True).reshape(
+            -1, model_width
+        )
+        inner = (
+            jnp.dot(hidden_whole, full_inner, preferred_element_type=jnp.float32) + bias_inner[0]
+        )
+        gelu_value, gelu_pull = jax.vjp(partial(jax.nn.gelu, approximate=False), inner)
+        gelu_low = gelu_value.astype(jnp.bfloat16)
+        ffn_partial = jnp.dot(gelu_low, full_outer, preferred_element_type=jnp.float32).reshape(
+            dp_count, -1, model_width
+        )
+        ffn = lax.psum_scatter(ffn_partial, "tensor", scatter_dimension=1, tiled=True).reshape(
+            -1, model_width
+        )
+        top = hidden + ffn + bias_outer
+        result, normed_ffn, spread_ffn = layer_norm(top, full_gain_ffn, full_shift_ffn)
+        out_bins.append(result.astype(jnp.bfloat16).reshape(dp_count, half_rows, model_width))
+        back_query, back_key, back_value, back_out, back_inner, back_outer = full_query, full_key, full_value, full_out, full_inner, full_outer
+        back_gain_attn, back_gain_ffn = full_gain_attn, full_gain_ffn
+        grad_result = bin_grads[micro_step].reshape(-1, model_width).astype(jnp.float32)
+        grad_top, grad_gain_ffn, grad_shift_ffn = norm_back(
+            grad_result, normed_ffn, spread_ffn, back_gain_ffn
+        )
+        grad_ffn_low = grad_top.astype(jnp.bfloat16)
+        grad_bias_outer = jnp.sum(grad_ffn_low.astype(jnp.float32), axis=0)
+        grad_ffn_whole = lax.all_gather(
+            grad_ffn_low.reshape(dp_count, half_rows, model_width), "tensor", axis=1, tiled=True
+        ).reshape(-1, model_width)
+        acc_outer = acc_outer + jnp.einsum(
+            "nf,nd->fd", gelu_low, grad_ffn_whole, preferred_element_type=jnp.float32
+        )
+        grad_gelu = jnp.einsum(
+            "nd,fd->nf", grad_ffn_whole, back_outer, preferred_element_type=jnp.float32
+        )
+        grad_inner_low = gelu_pull(grad_gelu)[0].astype(jnp.bfloat16)
+        acc_bias_inner = acc_bias_inner + jnp.sum(grad_inner_low.astype(jnp.float32), axis=0)[None]
+        acc_inner = acc_inner + jnp.einsum(
+            "nd,nf->df", hidden_whole, grad_inner_low, preferred_element_type=jnp.float32
+        )
+        hidden_partial = jnp.einsum(
+            "nf,df->nd", grad_inner_low, back_inner, preferred_element_type=jnp.float32
+        ).reshape(dp_count, -1, model_width)
+        grad_hidden = grad_top + lax.psum_scatter(
+            hidden_partial, "tensor", scatter_dimension=1, tiled=True
+        ).reshape(-1, model_width)
+        grad_mid, grad_gain_attn, grad_shift_attn = norm_back(
+            grad_hidden, normed_attn, spread_attn, back_gain_attn
+        )
+        grad_branch_low = grad_mid.astype(jnp.bfloat16)
+        grad_bias_out = jnp.sum(grad_branch_low.astype(jnp.float32), axis=0)
+        grad_branch_whole = lax.all_gather(
+            grad_branch_low.reshape(dp_count, half_rows, model_width), "tensor", axis=1, tiled=True
+        ).reshape(-1, model_width)
+        acc_out = acc_out + jnp.einsum(
+            "nh,nd->hd", attn, grad_branch_whole, preferred_element_type=jnp.float32
+        )
+        grad_attn_low = jnp.einsum(
+            "nd,hd->nh", grad_branch_whole, back_out, preferred_element_type=jnp.float32
+        ).astype(jnp.bfloat16)
+        grad_heads = grad_attn_low.reshape(bin_rows, local_heads, HD)
+        grad_query, grad_keys, grad_values = attend_backward(
+            query_heads,
+            key_heads,
+            value_heads,
+            grad_heads,
+            log_totals,
+            segment,
+            block_rows,
+            score_scale,
+        )
+        grad_query_low = grad_query.reshape(bin_rows, -1).astype(jnp.bfloat16)
+        grad_key_low = grad_keys.reshape(bin_rows, -1).astype(jnp.bfloat16)
+        grad_value_low = grad_values.reshape(bin_rows, -1).astype(jnp.bfloat16)
+        acc_bias_query = acc_bias_query + jnp.sum(grad_query_low.astype(jnp.float32), axis=0)[None]
+        acc_bias_value = acc_bias_value + jnp.sum(grad_value_low.astype(jnp.float32), axis=0)[None]
+        acc_query = acc_query + jnp.einsum(
+            "nd,nh->dh", whole_bin, grad_query_low, preferred_element_type=jnp.float32
+        )
+        acc_key = acc_key + jnp.einsum(
+            "nd,nh->dh", whole_bin, grad_key_low, preferred_element_type=jnp.float32
+        )
+        acc_value = acc_value + jnp.einsum(
+            "nd,nh->dh", whole_bin, grad_value_low, preferred_element_type=jnp.float32
+        )
+        input_partial = (
+            jnp.einsum("nh,dh->nd", grad_query_low, back_query, preferred_element_type=jnp.float32)
+            + jnp.einsum("nh,dh->nd", grad_key_low, back_key, preferred_element_type=jnp.float32)
+            + jnp.einsum(
+                "nh,dh->nd", grad_value_low, back_value, preferred_element_type=jnp.float32
+            )
+        )
+        grad_input = grad_mid + lax.psum_scatter(
+            input_partial.reshape(dp_count, -1, model_width).astype(jnp.bfloat16),
+            "tensor",
+            scatter_dimension=1,
+            tiled=True,
+        ).astype(jnp.float32).reshape(-1, model_width)
+        grad_bins.append(grad_input.astype(jnp.bfloat16).reshape(dp_count, half_rows, model_width))
+        acc_vectors = acc_vectors + jnp.stack(
+            [
+                grad_bias_out,
+                grad_gain_attn,
+                grad_shift_attn,
+                grad_bias_outer,
+                grad_gain_ffn,
+                grad_shift_ffn,
+            ]
+        )
+    out_by = jnp.stack(out_bins, axis=1)
+    gx_by = jnp.stack(grad_bins, axis=1)
+    grads = jnp.concatenate(
+        [acc_query, acc_key, acc_value, acc_out.T, acc_inner, acc_outer.T], axis=1
+    ).astype(jnp.bfloat16)
+    bits = (2,) * (dp_count.bit_length() - 1)
+    small = jnp.concatenate(
+        [
+            acc_vectors,
+            acc_bias_inner.reshape(2, model_width),
+            jnp.concatenate([acc_bias_query, acc_bias_value], axis=1),
+            jnp.zeros((7, model_width), jnp.float32),
+        ],
+        axis=0,
+    )
+    back, gback, sums, total = call_send_out(
+        dp_count, out_by, gx_by, grads.reshape(bits + (own_width, grads.shape[1])), small
+    )
+    vec_own = lax.dynamic_slice_in_dim(
+        lax.psum(total[:6], "tensor"), place * own_width, own_width, 1
+    )
+    sum_bias_inner = lax.dynamic_slice_in_dim(
+        total[6:8].reshape(1, ff_half), place * own_inner, own_inner, 1
+    )
+    bias_qv = total[8:9]
+    layer_out = jnp.take_along_axis(
+        back.swapaxes(0, 1), dest_dev[:, :, None, None], axis=1
+    ).reshape(tokens.shape)
+    grad_tokens = jnp.take_along_axis(
+        gback.swapaxes(0, 1), dest_dev[:, :, None, None], axis=1
+    ).reshape(tokens.shape)
+    sum_query, sum_key, sum_value, sum_out, sum_inner, sum_outer = jnp.split(
+        sums, [half_width, 2 * half_width, 3 * half_width, 4 * half_width, 4 * half_width + ff_half], axis=1
+    )
+    return (
+        layer_out,
+        grad_tokens,
+        sum_query,
+        sum_key,
+        sum_value,
+        bias_qv[:, :half_width],
+        bias_qv[:, half_width:],
+        sum_out.T,
+        vec_own[0],
+        vec_own[1],
+        vec_own[2],
+        sum_inner,
+        sum_bias_inner,
+        sum_outer.T,
+        vec_own[3],
+        vec_own[4],
+        vec_own[5],
+    )
 
 
 def shards(
@@ -410,8 +1073,20 @@
         P("dp"),
         P("dp"),
     )
+    dp_count = mesh.shape["dp"]
+
+    def body(*args):
+        tokens, w_query, b_inner = args[0], args[4], args[14]
+        fits = (
+            dp_count & (dp_count - 1) == 0
+            and w_query.shape[0] % 16 == 0
+            and tokens.shape[1] % 8 == 0
+            and mesh.shape["tensor"] == 2
+        )
+        return (shards_fast if fits else shards)(*args)
+
     return jax.shard_map(
-        shards,
+        body,
         mesh=mesh,
         in_specs=placed,
         out_specs=(

time: 1510 us -> 537 us (0.36)
  waiting for transfers between devices: 901 us -> 17.7 us
  blocking collectives: 311 us -> 29.9 us
  Pallas kernels: 0 us -> 214 us
  matrix products: 107 us -> 145 us
  starting transfers between devices: 30.5 us -> 0.71 us
    reduce_scatter x15 -> x9, waiting for transfers between devices: 762 us -> 17.5 us  [the longest x3 9.71 us: shards_fast(): lax.psum_scatter(attn_partial, 'tensor', scatter_dimension=1, tiled=True)]
    pallas_call x0 -> x2, Pallas kernels: none -> 214 us  [the longest x1 108 us: call_bring_in(): pl.pallas_call(partial(bring_in, dp_count, plan), out_shape=(jax.ShapeDty...]
    all_gather x16 -> x12, blocking collectives: 197 us -> 26.5 us  [the longest x3 6.88 us: shards_fast(): lax.all_gather(hidden_low, 'tensor', axis=1, tiled=True)]
    unnamed x25 -> x15, waiting for transfers between devices: 104 us -> 0.22 us
    unnamed x1 -> x0, blocking collectives: 72.9 us -> none
    dot_general x54, matrix products: 87.5 us -> 129 us  [the longest x3 22.1 us: shards_fast(): jnp.dot(hidden_whole, full_inner, preferred_element_type=jnp.float32)]
    psum x1, blocking collectives: 41.3 us -> 3.42 us  [shards_fast(): lax.psum(total[:6], 'tensor')]
    all_gather x2 -> x0, waiting for transfers between devices: 32.5 us -> none  [the longest x1 32.5 us: shards(): lax.all_gather(w_outer, 'dp', axis=1, tiled=True)]
  transfers between devices with their start and end apart: 26 -> 12, of which waited for: 13 -> 3; matrix products, arithmetic and copies ran while one was open for 9% -> 25% of each run, Pallas kernels for 0% -> 0%
where the time goes in v1:
time: 537 us; the launch traced here: 528 us
  Pallas kernels  214 us (40%)
  matrix products  145 us (27%)
  local copies, waits for them, and re-layouts  60.1 us (11%)
  other arithmetic  42.3 us (8%)
  blocking collectives  29.9 us (6%)
  between operations  18.1 us (3%)
  waiting for transfers between devices  17.7 us (3%)
    pallas_call x1, Pallas kernels, call_bring_in(): pl.pallas_call(partial(bring_in, dp_count, plan), out_shape=(jax.ShapeDty...  108 us
    pallas_call x1, Pallas kernels, call_send_out(): pl.pallas_call(partial(send_out, dp_count, plan), out_shape=(jax.ShapeDty...  106 us
    unnamed x546, local copies, waits for them, and re-layouts  26.1 us
    dot_general x3, matrix products, shards_fast(): jnp.dot(hidden_whole, full_inner, preferred_element_type=jnp.float32)  22.1 us
    dot_general x3, matrix products, shards_fast(): jnp.einsum('nd,nf->df', hidden_whole, grad_inner_low, preferred_element_t...  13.8 us
    another operation x21, local copies, waits for them, and re-layouts, shards_fast(): jnp.stack([grad_bias_out, grad_gain_attn, grad_shift_attn, grad_bias_oute...  11.9 us
    reduce_sum x4, other arithmetic, norm_back(): jnp.sum(grad_out * normed, axis=0)  11.2 us
    dot_general x3, matrix products, shards_fast(): jnp.einsum('nf,df->nd', grad_inner_low, back_inner, preferred_element_typ...  11 us
  transfers between devices with their start and end apart: 12, of which 3 were waited for; matrix products, arithmetic and copies ran while one was open for 25% of the time, Pallas kernels for 0%

profile of v1, /device:TPU:0, one launch (start us, length us, event | category | flops | bytes accessed | tf_op | source)
XLA Modules:
  0.0 527.6 jit_solution(9558452970919187999)
XLA Ops:
  17.8 108.3 %bring_in.1 = (bf16[16,3,8,768]{3,2,1,0:T(8,128)(2,1)S(1)}, bf16[16,3,8,768]{3,2,1,0:T(8,128)(2,1)S(1)}, bf16[2,2,2,2,48,4608]{5,4,3,2,1,0:T(8,128)(2,1)S(1)}, f32[16,768]{1,0:T(8,128)S(1)}) custom-call(bf16[16,3,8,768]{3,2,1,0:T(8,128)(2,1)S(1)} %get-tuple-element.155.x_ref, bf16[16,3,8,768]{3,2,1,0:T(8,128)(2,1)S(1)} %get-tuple-element.154.dy_ref, ...), custom_call_target="tpu_custom_call" | custom-call | tf_op jit(solution)/shard_map/bring_in/pallas_call | solution.py:410
  126.2 2.8 copy-done.2
  130.1 2.1 all-gather.1
  132.2 1.6 convolution_convert_fusion.9
  139.9 2.5 fusion.78
  142.5 2.1 all-gather.2
  144.6 1.6 convolution_convert_fusion.7
  152.2 2.5 fusion.76
  154.8 2.3 all-gather
  157.1 1.6 convolution_convert_fusion.11
  164.9 2.4 fusion.80
  168.6 9.7 %reduce-scatter.19.cloned.1.call-done = f32[16,8,768]{2,1,0:T(8,128)} async-done(((f32[16,16,768]{2,1,0:T(8,128)}), f32[16,8,768]{2,1,0:T(8,128)}) %reduce-scatter.19.cloned.1.call-update) | async-done | bytes 393232 | tf_op jit(solution)/shard_map/reduce_scatter | solution.py:581
  178.3 1.7 fusion.220
  181.7 2.1 all_gather.41
  183.8 7.3 %multiply_convert_fusion.3 = (bf16[256,1536]{1,0:T(8,128)(2,1)S(1)}, f32[256,1536]{1,0:T(8,128)}, f32[256,1536]{1,0:T(8,128)}) fusion(f32[1536]{0:T(1024)S(1)} %copy-done.242, bf16[256,768]{1,0:T(8,128)(2,1)S(1)} %bitcast.528, bf16[768,4608]{1,0:T(8,128)(2,1)} %bitcast.419), kind=kOutput, calls=%fused_computation.30 | convolution fusion | flops 629932032 | bytes 6690816 | tf_op jit(solution)/shard_map/dot_general | solution.py:591
  191.1 3.7 fusion.49
  194.9 2.7 all_gather.39
  197.6 7.4 %multiply_convert_fusion.4 = (bf16[256,1536]{1,0:T(8,128)(2,1)S(1)}, f32[256,1536]{1,0:T(8,128)}, f32[256,1536]{1,0:T(8,128)}) fusion(f32[1536]{0:T(1024)} %add.869, bf16[256,768]{1,0:T(8,128)(2,1)S(1)} %bitcast.486, bf16[768,4608]{1,0:T(8,128)(2,1)} %bitcast.421), kind=kOutput, calls=%fused_computation.46 | convolution fusion | flops 629932032 | bytes 6692864 | tf_op jit(solution)/shard_map/dot_general | solution.py:591
  205.0 3.7 fusion.51
  208.7 2.1 all_gather.37
  210.8 7.4 %multiply_convert_fusion.5 = (bf16[256,1536]{1,0:T(8,128)(2,1)S(1)}, f32[256,1536]{1,0:T(8,128)}, f32[256,1536]{1,0:T(8,128)}) fusion(f32[1536]{0:T(1024)} %add.869, bf16[256,768]{1,0:T(8,128)(2,1)S(1)} %bitcast.484, bf16[768,4608]{1,0:T(8,128)(2,1)} %bitcast.423), kind=kOutput, calls=%fused_computation.62 | convolution fusion | flops 629932032 | bytes 6692864 | tf_op jit(solution)/shard_map/dot_general | solution.py:591
  218.2 3.7 fusion.53
  224.9 6.7 %reduce-scatter.21.cloned.1.call-done = f32[16,8,768]{2,1,0:T(8,128)} async-done(((f32[16,16,768]{2,1,0:T(8,128)}), f32[16,8,768]{2,1,0:T(8,128)}) %reduce-scatter.21.cloned.1.call-update) | async-done | bytes 393232 | tf_op jit(solution)/shard_map/reduce_scatter | solution.py:598
  231.7 1.8 fusion.218
  235.2 2.4 convert_reduce_fusion.4
  238.6 2.2 all_gather.44
  240.9 3.6 convert_reduce_fusion.1
  244.5 3.7 fusion.63
  252.6 4.2 fusion.240
  257.8 3.2 multiply_reduce_fusion.4
  261.0 2.1 all_gather.42
  263.1 3.5 convert_reduce_fusion.2
  266.7 3.7 fusion.65
  270.6 1.7 fusion.152
  277.8 2.9 fusion.242
  283.1 3.0 fusion.239
  286.1 2.9 fusion.241
  289.0 3.2 multiply_reduce_fusion.5
  292.2 2.1 all_gather.46
  294.3 2.9 convert_reduce_fusion
  297.3 3.6 fusion.61
  304.3 6.6 %add_convert_fusion.1 = bf16[768,1536]{1,0:T(8,128)(2,1)} fusion(f32[768,1536]{1,0:T(8,128)} %fusion.239, f32[768,1536]{1,0:T(8,128)} %fusion.240, bf16[256,768]{1,0:T(8,128)(2,1)} %bitcast.529, bf16[256,1536]{1,0:T(8,128)(2,1)} %copy-done.90), kind=kOutput, calls=%fused_computation.5 | convolution fusion | flops 607518720 | bytes 12976128 | tf_op jit(solution)/shard_map/nd,nf->df/dot_general | solution.py:623
  311.0 4.6 add_convert_fusion
  315.8 3.1 multiply_reduce_fusion.3
  319.6 1.6 convert_reduce_fusion.15
  321.1 2.2 all_gather.47
  324.1 2.1 convolution_convert_fusion.1
  326.2 1.7 copy.219
  328.0 2.6 convert_reduce_fusion.6
  334.0 2.1 all_gather.45
  338.5 1.7 convert_reduce_fusion.7
  340.2 2.3 multiply_reduce_fusion.1
  350.3 1.8 multiply_convert_fusion.1
  354.9 1.5 convolution_add_fusion.14
  356.6 1.6 fusion.26
  361.6 1.6 convert_reduce_fusion.17
  363.2 2.5 all_gather.43
  371.9 2.4 fusion.172
  386.1 2.5 fusion.238
  390.1 1.7 copy.271
  398.4 3.5 constant_dynamic-update-slice_fusion.5
  402.0 1.6 constant_dynamic-update-slice_fusion.4.g_ref
  405.2 105.6 %send_out.1 = (bf16[16,3,8,768]{3,2,1,0:T(8,128)(2,1)S(1)}, bf16[16,3,8,768]{3,2,1,0:T(8,128)(2,1)S(1)}, f32[48,4608]{1,0:T(8,128)S(1)}, f32[16,768]{1,0:T(8,128)S(1)}) custom-call(bf16[16,3,8,768]{3,2,1,0:T(8,128)(2,1)S(1)} %copy.225.out_ref, bf16[16,3,8,768]{3,2,1,0:T(8,128)(2,1)S(1)} %pad_maximum_fusion.1.gx_ref, ...), custom_call_target="tpu_custom_call" | custom-call | tf_op jit(solution)/shard_map/send_out/pallas_call | solution.py:447
  514.5 3.4 psum.7
  (782 shorter events, 108.8 us)
Async XLA Ops:
  7.2 8.0 %copy-start = (bf16[48,8,768]{2,1,0:T(8,128)(2,1)S(1)}, bf16[48,8,768]{2,1,0:T(8,128)(2,1)}, u32[]{:S(2)}) copy-start(bf16[48,8,768]{2,1,0:T(8,128)(2,1)} %param.22) | copy-start | bytes 1769476
  7.2 8.7 %copy-start.108 = (bf16[48,8,768]{2,1,0:T(8,128)(2,1)S(1)}, bf16[48,8,768]{2,1,0:T(8,128)(2,1)}, u32[]{:S(2)}) copy-start(bf16[48,8,768]{2,1,0:T(8,128)(2,1)} %param.21) | copy-start | bytes 1769476
  7.2 10.1 %copy-start.186 = (bf16[48,384]{1,0:T(8,128)(2,1)S(1)}, bf16[48,384]{1,0:T(8,128)(2,1)}, u32[]{:S(2)}) copy-start(bf16[48,384]{1,0:T(8,128)(2,1)} %param.26) | copy-start | bytes 110596
  7.2 10.1 %copy-start.187 = (bf16[48,384]{1,0:T(8,128)(2,1)S(1)}, bf16[48,384]{1,0:T(8,128)(2,1)}, u32[]{:S(2)}) copy-start(bf16[48,384]{1,0:T(8,128)(2,1)} %param.27) | copy-start | bytes 110596
  7.2 10.1 %copy-start.188 = (bf16[384,48]{0,1:T(8,128)(2,1)S(1)}, bf16[384,48]{0,1:T(8,128)(2,1)}, u32[]{:S(2)}) copy-start(bf16[384,48]{0,1:T(8,128)(2,1)} %param.30) | copy-start | bytes 110596
  7.2 10.1 %copy-start.145 = (bf16[48,1536]{1,0:T(8,128)(2,1)S(1)}, bf16[48,1536]{1,0:T(8,128)(2,1)}, u32[]{:S(2)}) copy-start(bf16[48,1536]{1,0:T(8,128)(2,1)} %param.34) | copy-start | bytes 442372
  7.3 161.4 %reduce-scatter.23.cloned.1.call-start = ((), (), s32[]{:S(2)}) async-start(), calls=%async_computation.14 | async-start | bytes 1179648 | tf_op jit(solution)/shard_map/reduce_scatter | solution.py:581
  142.4 26.2 %reduce-scatter.27.cloned.1.call-start = ((), (), s32[]{:S(2)}) async-start(), calls=%async_computation.16 | async-start | bytes 1179648 | tf_op jit(solution)/shard_map/reduce_scatter | solution.py:581
  154.7 23.6 %reduce-scatter.19.cloned.1.call-start = ((), (), s32[]{:S(2)}) async-start(), calls=%async_computation.12 | async-start | bytes 1179648 | tf_op jit(solution)/shard_map/reduce_scatter | solution.py:581
  167.3 57.5 %reduce-scatter.29.cloned.1.call-start = ((), (), s32[]{:S(2)}) async-start(), calls=%async_computation.17 | async-start | bytes 1179648 | tf_op jit(solution)/shard_map/reduce_scatter | solution.py:598
  168.6 11.4 %copy-start.184 = (f32[768]{0:T(1024)}, f32[768]{0:T(1024)S(1)}, u32[]{:S(2)}) copy-start(f32[768]{0:T(1024)S(1)} %get-tuple-element.78) | copy-start | bytes 9220
  168.6 69.0 %copy-start.142 = (f32[768]{0:T(1024)}, f32[768]{0:T(1024)S(1)}, u32[]{:S(2)}) copy-start(f32[768]{0:T(1024)S(1)} %get-tuple-element.73) | copy-start | bytes 9220
  180.1 138.8 %copy-start.7 = (f32[16,8,768]{2,1,0:T(8,128)}, f32[16,8,768]{2,1,0:T(8,128)S(1)}, u32[]{:S(2)}) copy-start(f32[16,8,768]{2,1,0:T(8,128)S(1)} %get-tuple-element.121) | copy-start | bytes 1179652
  180.1 138.8 %copy-start.9 = (f32[16,8,768]{2,1,0:T(8,128)}, f32[16,8,768]{2,1,0:T(8,128)S(1)}, u32[]{:S(2)}) copy-start(f32[16,8,768]{2,1,0:T(8,128)S(1)} %get-tuple-element.123) | copy-start | bytes 1179652
  183.8 7.3 %copy-start.67 = (bf16[16,16,768]{2,1,0:T(8,128)(2,1)}, bf16[16,16,768]{2,1,0:T(8,128)(2,1)S(1)}, u32[]{:S(2)}) copy-start(bf16[16,16,768]{2,1,0:T(8,128)(2,1)S(1)} %all_gather.41) | copy-start | bytes 1179652
  194.8 30.0 %reduce-scatter.25.cloned.1.call-start = ((), (), s32[]{:S(2)}) async-start(), calls=%async_computation.15 | async-start | bytes 1179648 | tf_op jit(solution)/shard_map/reduce_scatter | solution.py:598
  197.6 7.4 %copy-start.36 = (bf16[16,16,768]{2,1,0:T(8,128)(2,1)}, bf16[16,16,768]{2,1,0:T(8,128)(2,1)S(1)}, u32[]{:S(2)}) copy-start(bf16[16,16,768]{2,1,0:T(8,128)(2,1)S(1)} %all_gather.39) | copy-start | bytes 1179652
  208.7 22.9 %reduce-scatter.21.cloned.1.call-start = ((), (), s32[]{:S(2)}) async-start(), calls=%async_computation.13 | async-start | bytes 1179648 | tf_op jit(solution)/shard_map/reduce_scatter | solution.py:598
  210.8 7.4 %copy-start.34 = (bf16[16,16,768]{2,1,0:T(8,128)(2,1)}, bf16[16,16,768]{2,1,0:T(8,128)(2,1)S(1)}, u32[]{:S(2)}) copy-start(bf16[16,16,768]{2,1,0:T(8,128)(2,1)S(1)} %all_gather.37) | copy-start | bytes 1179652
  221.9 9.7 %copy-start.110 = (f32[16,8]{1,0:T(8,128)S(1)}, f32[16,8]{1,0:T(8,128)}, u32[]{:S(2)}) copy-start(f32[16,8]{1,0:T(8,128)} %copy-done.109) | copy-start | bytes 1540
  221.9 9.7 %copy-start.114 = (f32[16,8]{1,0:T(8,128)S(1)}, f32[16,8]{1,0:T(8,128)}, u32[]{:S(2)}) copy-start(f32[16,8]{1,0:T(8,128)} %copy-done.113) | copy-start | bytes 1540
  221.9 9.7 %copy-start.118 = (f32[16,8]{1,0:T(8,128)S(1)}, f32[16,8]{1,0:T(8,128)}, u32[]{:S(2)}) copy-start(f32[16,8]{1,0:T(8,128)} %copy-done.117) | copy-start | bytes 1540
  221.9 9.6 %copy-start.122 = (f32[16,8]{1,0:T(8,128)S(1)}, f32[16,8]{1,0:T(8,128)}, u32[]{:S(2)}) copy-start(f32[16,8]{1,0:T(8,128)} %copy-done.121) | copy-start | bytes 1540
  221.9 9.6 %copy-start.126 = (f32[16,8]{1,0:T(8,128)S(1)}, f32[16,8]{1,0:T(8,128)}, u32[]{:S(2)}) copy-start(f32[16,8]{1,0:T(8,128)} %copy-done.125) | copy-start | bytes 1540
  221.9 9.6 %copy-start.181 = (f32[768]{0:T(1024)S(1)}, f32[768]{0:T(1024)}, u32[]{:S(2)}) copy-start(f32[768]{0:T(1024)} %get-tuple-element.76) | copy-start | bytes 9220
  221.9 9.6 %copy-start.189 = (f32[768]{0:T(1024)S(1)}, f32[768]{0:T(1024)}, u32[]{:S(2)}) copy-start(f32[768]{0:T(1024)} %get-tuple-element.75) | copy-start | bytes 9220
  222.0 35.9 %reduce-scatter.33.cloned.1.call-start = ((), (), s32[]{:S(2)}) async-start(), calls=%async_computation.19 | async-start | bytes 1179648 | tf_op jit(solution)/shard_map/reduce_scatter | solution.py:629
  222.1 11.4 %copy-start.251 = (pred[3,16,1,1]{1,0,3,2:T(4,128)(4,1)}, pred[3,16,1,1]{1,0,3,2:T(4,128)(4,1)S(1)}, u32[]{:S(2)}) copy-start(pred[3,16,1,1]{1,0,3,2:T(4,128)(4,1)S(1)} %and.57) | copy-start | bytes 148
  222.2 9.3 %copy-start.205 = (s32[3,16,1,1]{1,0,3,2:T(4,128)}, s32[3,16,1,1]{1,0,3,2:T(4,128)S(1)}, u32[]{:S(2)}) copy-start(s32[3,16,1,1]{1,0,3,2:T(4,128)S(1)} %div.162) | copy-start | bytes 580
  235.2 5.6 %copy-start.261 = (f32[256,1536]{1,0:T(8,128)S(1)}, f32[256,1536]{1,0:T(8,128)}, u32[]{:S(2)}) copy-start(f32[256,1536]{1,0:T(8,128)} %get-tuple-element.168) | copy-start | bytes 4718596
  237.6 6.8 %copy-start.156 = (f32[16,8]{1,0:T(8,128)}, f32[16,8]{1,0:T(8,128)S(1)}, u32[]{:S(2)}) copy-start(f32[16,8]{1,0:T(8,128)S(1)} %broadcast_multiply_fusion.6) | copy-start | bytes 1540
  237.7 6.8 %copy-start.158 = (f32[16,8]{1,0:T(8,128)}, f32[16,8]{1,0:T(8,128)S(1)}, u32[]{:S(2)}) copy-start(f32[16,8]{1,0:T(8,128)S(1)} %broadcast_multiply_fusion.7) | copy-start | bytes 1540
  244.5 5.1 copy-start.163
  244.5 5.1 copy-start.191
  244.5 5.7 %copy-start.201 = (f32[16,8]{1,0:T(8,128)S(1)}, f32[16,8]{1,0:T(8,128)}, u32[]{:S(2)}) copy-start(f32[16,8]{1,0:T(8,128)} %get-tuple-element.60) | copy-start | bytes 1540
  244.5 6.3 %copy-start.200 = (f32[16,8]{1,0:T(8,128)S(1)}, f32[16,8]{1,0:T(8,128)}, u32[]{:S(2)}) copy-start(f32[16,8]{1,0:T(8,128)} %get-tuple-element.62) | copy-start | bytes 1540
  244.5 6.9 %copy-start.199 = (f32[16,8]{1,0:T(8,128)S(1)}, f32[16,8]{1,0:T(8,128)}, u32[]{:S(2)}) copy-start(f32[16,8]{1,0:T(8,128)} %get-tuple-element.63) | copy-start | bytes 1540
  244.5 7.4 %copy-start.197 = (f32[16,8]{1,0:T(8,128)S(1)}, f32[16,8]{1,0:T(8,128)}, u32[]{:S(2)}) copy-start(f32[16,8]{1,0:T(8,128)} %get-tuple-element.65) | copy-start | bytes 1540
  248.2 40.8 %reduce-scatter.31.cloned.1.call-start = ((), (), s32[]{:S(2)}) async-start(), calls=%async_computation.18 | async-start | bytes 1179648 | tf_op jit(solution)/shard_map/reduce_scatter | solution.py:629
  257.8 5.3 copy-start.258
  257.8 5.3 copy-start.259
  270.5 45.2 %reduce-scatter.35.cloned.1.call-start = ((), (), s32[]{:S(2)}) async-start(), calls=%async_computation.20 | async-start | bytes 1179648 | tf_op jit(solution)/shard_map/reduce_scatter | solution.py:629
  270.5 7.2 %copy-start.38 = (bf16[16,16,768]{2,1,0:T(8,128)(2,1)S(1)}, bf16[16,16,768]{2,1,0:T(8,128)(2,1)}, u32[]{:S(2)}) copy-start(bf16[16,16,768]{2,1,0:T(8,128)(2,1)} %copy-done.37) | copy-start | bytes 1179652
  270.5 7.2 %copy-start.84 = (bf16[256,1536]{1,0:T(8,128)(2,1)S(1)}, bf16[256,1536]{1,0:T(8,128)(2,1)}, u32[]{:S(2)}) copy-start(bf16[256,1536]{1,0:T(8,128)(2,1)} %copy-done.83) | copy-start | bytes 2359300
  277.7 5.3 %copy-start.35 = (bf16[16,16,768]{2,1,0:T(8,128)(2,1)S(1)}, bf16[16,16,768]{2,1,0:T(8,128)(2,1)}, u32[]{:S(2)}) copy-start(bf16[16,16,768]{2,1,0:T(8,128)(2,1)} %copy-done.34) | copy-start | bytes 1179652
  277.8 5.3 %copy-start.88 = (bf16[256,1536]{1,0:T(8,128)(2,1)S(1)}, bf16[256,1536]{1,0:T(8,128)(2,1)}, u32[]{:S(2)}) copy-start(bf16[256,1536]{1,0:T(8,128)(2,1)} %copy-done.87) | copy-start | bytes 2359300
  289.0 5.3 copy-start.256
  289.0 5.3 copy-start.257
  297.3 5.8 %copy-start.203 = (f32[16,8]{1,0:T(8,128)S(1)}, f32[16,8]{1,0:T(8,128)}, u32[]{:S(2)}) copy-start(f32[16,8]{1,0:T(8,128)} %get-tuple-element.45) | copy-start | bytes 1540
  297.3 6.4 %copy-start.202 = (f32[16,8]{1,0:T(8,128)S(1)}, f32[16,8]{1,0:T(8,128)}, u32[]{:S(2)}) copy-start(f32[16,8]{1,0:T(8,128)} %get-tuple-element.68) | copy-start | bytes 1540
  301.0 9.9 %slice-start = ((s8[4718592]{0:T(1024)(128)(4,1)}), s8[524288]{0:T(1024)(128)(4,1)S(1)}, s32[]{:S(2)}) async-start(s8[4718592]{0:T(1024)(128)(4,1)} %bitcast.445), calls=%async_computation.24 | async-start | bytes 1048576
  301.0 59.6 %reduce-scatter.41.cloned.1.call-start = ((), (), s32[]{:S(2)}) async-start(), calls=%async_computation.23 | async-start | bytes 589824
  304.3 6.6 %slice-start.1 = ((s8[4718592]{0:T(1024)(128)(4,1)}), s8[4194304]{0:T(1024)(128)(4,1)S(1)}, s32[]{:S(2)}) async-start(s8[4718592]{0:T(1024)(128)(4,1)} %bitcast.445), calls=%async_computation.25 | async-start | bytes 8388608
  304.3 6.6 %copy-start.69 = (bf16[16,16,768]{2,1,0:T(8,128)(2,1)S(1)}, bf16[16,16,768]{2,1,0:T(8,128)(2,1)}, u32[]{:S(2)}) copy-start(bf16[16,16,768]{2,1,0:T(8,128)(2,1)} %copy-done.68) | copy-start | bytes 1179652
  304.3 6.6 %copy-start.82 = (bf16[256,1536]{1,0:T(8,128)(2,1)S(1)}, bf16[256,1536]{1,0:T(8,128)(2,1)}, u32[]{:S(2)}) copy-start(bf16[256,1536]{1,0:T(8,128)(2,1)} %copy-done.81) | copy-start | bytes 2359300
  321.1 6.8 %copy-start.6 = (f32[6,256,256]{1,2,0:T(8,128)S(1)}, f32[6,256,256]{1,2,0:T(8,128)}, u32[]{:S(2)}) copy-start(f32[6,256,256]{1,2,0:T(8,128)} %copy-done.5) | copy-start | bytes 4718596
  333.0 5.4 %copy-start.147 = (f32[6,256]{1,0:T(8,128)S(1)}, f32[6,256]{1,0:T(8,128)}, u32[]{:S(2)}) copy-start(f32[6,256]{1,0:T(8,128)} %log_add_fusion.1) | copy-start | bytes 18436
  334.0 10.9 %copy-start.41 = (bf16[6,64,256]{2,1,0:T(8,128)(2,1)}, bf16[6,64,256]{2,1,0:T(8,128)(2,1)S(1)}, u32[]{:S(2)}) copy-start(bf16[6,64,256]{2,1,0:T(8,128)(2,1)S(1)} %get-tuple-element.182) | copy-start | bytes 589828
  350.2 39.9 %reduce-scatter.39.cloned.1.call-start = ((), (), s32[]{:S(2)}) async-start(), calls=%async_computation.22 | async-start | bytes 589824
  356.6 4.9 copy-start.10
  356.6 4.9 copy-start.27
  359.1 44.5 %reduce-scatter.37.cloned.1.call-start = ((), (), s32[]{:S(2)}) async-start(), calls=%async_computation.21 | async-start | bytes 589824
  512.1 7.1 %copy-start.248 = (pred[3,16]{1,0:T(4,128)(4,1)S(1)}, pred[3,16]{1,0:T(4,128)(4,1)}, u32[]{:S(2)}) copy-start(pred[3,16]{1,0:T(4,128)(4,1)} %and_bitcast_fusion) | copy-start | bytes 148
  513.7 6.6 %copy-start.1 = (bf16[48,8,768]{2,1,0:T(8,128)(2,1)S(1)}, bf16[48,8,768]{2,1,0:T(8,128)(2,1)}, u32[]{:S(2)}) copy-start(bf16[48,8,768]{2,1,0:T(8,128)(2,1)} %param.22) | copy-start | bytes 1769476
  (212 other events, 605.6 us)
Sparse Core Ops, SparseCore 0:
  142.5 10.9 reduce-scatter.22
  155.8 9.9 reduce-scatter.26
  168.0 10.2 reduce-scatter.18
  194.9 9.3 reduce-scatter.28
  208.8 9.4 reduce-scatter.24
  222.1 9.3 reduce-scatter.20
  248.4 9.4 reduce-scatter.32
  270.6 9.3 reduce-scatter.30
  301.1 9.4 reduce-scatter.34
  350.3 8.9 reduce-scatter.40
  361.5 8.9 reduce-scatter.38
  390.2 8.9 reduce-scatter.36

commit v2 on v0

--- a/solution.py
+++ b/solution.py
@@ -4,6 +4,8 @@
 import jax
 import jax.numpy as jnp
 from jax import lax
+from jax.experimental import pallas as pl
+from jax.experimental.pallas import tpu as pltpu
 from jax.sharding import PartitionSpec as P
 
 HEADS = 12
@@ -82,6 +84,925 @@
         * score_scale
     )
     return (grad_query_rows, grad_keys, grad_values)
+
+
+MESH = pl.DeviceIdType.MESH
+LANES = 128
+NT = (((1,), (1,)), ((), ()))
+NN = (((1,), (0,)), ((), ()))
+F32 = jnp.float32
+LOW = jnp.bfloat16
+VMEM_BYTES = 63 << 20
+
+
+def flip(place, bit):
+    return place + bit * (1 - 2 * ((place // bit) % 2))
+
+
+def bit_of(place, bit):
+    return (place // bit) % 2
+
+
+def bits_of(count):
+    return tuple(1 << i for i in range(count.bit_length() - 1))[::-1]
+
+
+def orders_of(count):
+    bits = bits_of(count)
+    return (bits, bits[:-2] + bits[-2:][::-1])
+
+
+def mm(left, right, dims=NN):
+    return lax.dot_general(left, right, dims, preferred_element_type=F32)
+
+
+class Gather:
+    def __init__(self, dp_count, place, half, order, ref, start, size, send_sem, recv_sem):
+        self.place, self.half, self.order = place, half, order
+        self.bits = bits_of(dp_count)
+        self.ref, self.cols = ref, pl.ds(start, size)
+        self.send_sem, self.recv_sem = send_sem, recv_sem
+
+    def copy(self, stage):
+        done = self.order[:stage]
+        index = tuple(
+            slice(None) if bit in done else bit_of(self.place, bit) for bit in self.bits
+        ) + (slice(None), self.cols)
+        return pltpu.make_async_remote_copy(
+            src_ref=self.ref.at[index],
+            dst_ref=self.ref.at[index],
+            send_sem=self.send_sem.at[stage],
+            recv_sem=self.recv_sem.at[stage],
+            device_id=(flip(self.place, self.order[stage]), self.half),
+            device_id_type=MESH,
+        )
+
+
+class Scatter:
+    def __init__(self, dp_count, place, half, order, ref, start, size, landing, send_sem, recv_sem):
+        self.place, self.half = place, half
+        self.order = order[::-1]
+        self.bits = bits_of(dp_count)
+        self.ref, self.cols = ref, pl.ds(start, size)
+        self.landing = landing
+        self.send_sem, self.recv_sem = send_sem, recv_sem
+
+    def view(self, stage, chosen):
+        left = [bit for bit in self.bits if bit not in self.order[:stage]]
+        own = bit_of(self.place, self.order[stage])
+        index = tuple(
+            (own if chosen == "own" else 1 - own) if bit == self.order[stage] else slice(None)
+            for bit in left
+        )
+        if stage == 0:
+            return self.ref.at[index + (slice(None), self.cols)]
+        return self.landing[stage - 1].at[index]
+
+    def copy(self, stage):
+        return pltpu.make_async_remote_copy(
+            src_ref=self.view(stage, "other"),
+            dst_ref=self.landing[stage],
+            send_sem=self.send_sem.at[stage],
+            recv_sem=self.recv_sem.at[stage],
+            device_id=(flip(self.place, self.order[stage]), self.half),
+            device_id_type=MESH,
+        )
+
+    def add(self, stage):
+        kept = self.view(stage, "own")
+        land = self.landing[stage]
+        lead = land.shape[:-2]
+        count = math.prod(lead)
+
+        def one(i, carry):
+            index, rest = [], i
+            for extent in lead[::-1]:
+                index.append(lax.rem(rest, extent))
+                rest = rest // extent
+            index = tuple(index[::-1])
+            land[index] = (kept[index].astype(F32) + land[index].astype(F32)).astype(land.dtype)
+            return carry
+
+        if count == 1:
+            one(0, 0)
+        else:
+            lax.fori_loop(0, count, one, 0)
+
+    def finish(self, stage, out_ref, out_cols):
+        kept = self.view(stage, "own")
+        out_ref[:, out_cols] = kept[...].astype(F32) + self.landing[stage][...].astype(F32)
+
+
+def layer(sizes, gather_plan, scatter_plan, *refs):
+    dp_count, micro, rows, width, heads_wide, ff = sizes
+    (
+        tokens_ref,
+        cot_ref,
+        route_ref,
+        inverse_ref,
+        lengths_ref,
+        wq_ref,
+        wk_ref,
+        wv_ref,
+        wo_ref,
+        wi_ref,
+        wu_ref,
+        small_ref,
+        bq_ref,
+        bv_ref,
+        bi_ref,
+        layer_out_ref,
+        grad_tokens_ref,
+        sum_ref,
+        vec_out_ref,
+        full,
+        grads,
+        x_send,
+        dy_send,
+        x_land,
+        dy_land,
+        out_send,
+        gx_send,
+        out_land,
+        gx_land,
+        xs,
+        hs,
+        gs,
+        gb,
+        flipped,
+        xs_flipped,
+        hs_flipped,
+        qkv,
+        dqkv,
+        attn,
+        gattn,
+        probs,
+        bias,
+        gelu_low,
+        dgelu,
+        ginner,
+        normed,
+        spread,
+        grad_keep,
+        own_part,
+        part_send,
+        part_land,
+        last_send,
+        last_land,
+        vec_buf,
+        vec_land,
+        vec,
+        vec_pair,
+        vecg_buf,
+        vecg_land,
+        vec_acc,
+        *rest,
+    ) = refs
+    stages = dp_count.bit_length() - 1
+    landings = [rest[i * stages : (i + 1) * stages] for i in range(len(scatter_plan))]
+    (
+        x_sems,
+        dy_sems,
+        out_sems,
+        gx_sems,
+        gather_sems,
+        scatter_sems,
+        vec_sems,
+        vecg_sems,
+        pair_sems,
+    ) = rest[len(scatter_plan) * stages :]
+    place, half = lax.axis_index("dp"), lax.axis_index("tensor")
+    other = 1 - half
+    bits = bits_of(dp_count)
+    orders = orders_of(dp_count)
+    bin_half = dp_count * rows
+    tall = micro * bin_half
+    blocks = micro * dp_count
+    own_width = width // dp_count
+    block_len = 2 * rows
+    pairs = heads_wide // LANES
+    key_col, value_col, out_col = heads_wide, 2 * heads_wide, 3 * heads_wide
+    inner_col, outer_col = 4 * heads_wide, 4 * heads_wide + ff
+    tile = heads_wide
+
+    def weights(start, size):
+        return full[(slice(None),) * stages + (slice(None), pl.ds(start, size))].reshape(width, size)
+
+    def pair_copy(src, dst, which):
+        return pltpu.make_async_remote_copy(
+            src_ref=src,
+            dst_ref=dst,
+            send_sem=pair_sems.at[0, which],
+            recv_sem=pair_sems.at[1, which],
+            device_id=(place, other),
+            device_id_type=MESH,
+        )
+
+    def push(send_ref, recv_ref, sems):
+        def one(step, carry):
+            peer = lax.rem(place + step, dp_count)
+            pltpu.make_async_remote_copy(
+                src_ref=send_ref.at[peer],
+                dst_ref=recv_ref.at[place],
+                send_sem=sems.at[0, step],
+                recv_sem=sems.at[1, step],
+                device_id=(peer, half),
+                device_id_type=MESH,
+            ).start()
+            return carry
+
+        lax.fori_loop(1, dp_count, one, 0)
+
+    def settle(send_ref, recv_ref, sems):
+        recv_ref[place] = send_ref[place]
+
+        def one(step, carry):
+            source = lax.rem(place + dp_count - step, dp_count)
+            pltpu.make_async_remote_copy(
+                src_ref=send_ref.at[source],
+                dst_ref=recv_ref.at[source],
+                send_sem=sems.at[0, step],
+                recv_sem=sems.at[1, step],
+                device_id=(source, half),
+                device_id_type=MESH,
+            ).wait()
+            return carry
+
+        lax.fori_loop(1, dp_count, one, 0)
+
+    def arrange(src_ref, dst_ref):
+        def one(i, carry):
+            m, peer = i // dp_count, lax.rem(i, dp_count)
+            dst_ref[peer, m] = src_ref[m * dp_count + inverse_ref[m, peer]]
+            return carry
+
+        lax.fori_loop(0, blocks, one, 0)
+
+    own = tuple(bit_of(place, bit) for bit in bits)
+    eye = (
+        lax.broadcasted_iota(jnp.int32, (own_width, own_width), 0)
+        == lax.broadcasted_iota(jnp.int32, (own_width, own_width), 1)
+    ).astype(LOW)
+    full[own + (slice(None), pl.ds(0, heads_wide))] = wq_ref[...]
+    full[own + (slice(None), pl.ds(key_col, heads_wide))] = wk_ref[...]
+    full[own + (slice(None), pl.ds(value_col, heads_wide))] = wv_ref[...]
+    full[own + (slice(None), pl.ds(out_col, heads_wide))] = mm(eye, wo_ref[...], NT).astype(LOW)
+    full[own + (slice(None), pl.ds(inner_col, ff))] = wi_ref[...]
+    full[own + (slice(None), pl.ds(outer_col, ff))] = mm(eye, wu_ref[...], NT).astype(LOW)
+
+    def spread_out(piece, total):
+        size = piece.shape[1]
+        target = lax.broadcasted_iota(jnp.int32, (size, total), 1)
+        at = lax.broadcasted_iota(jnp.int32, (size, total), 0) + place * size
+        return lax.dot_general(
+            piece,
+            (target == at).astype(F32),
+            NN,
+            precision=lax.Precision.HIGHEST,
+            preferred_element_type=F32,
+        )
+
+    vec_buf[0, 0:8, :] = spread_out(small_ref[...], width)
+    long_row = spread_out(jnp.broadcast_to(bi_ref[...].astype(F32), (8, bi_ref.shape[1])), ff)
+    vec_buf[0, 8:16, :] = jnp.zeros((8, width), F32)
+    for i in range(ff // width):
+        vec_buf[0, 8 + i : 9 + i, :] = long_row[0:1, i * width : (i + 1) * width]
+    arrange(tokens_ref, x_send)
+
+    barrier = pltpu.get_barrier_semaphore()
+
+    def hello(step, carry):
+        peer = lax.rem(place + step, dp_count)
+        pl.semaphore_signal(barrier, inc=1, device_id=(peer, half), device_id_type=MESH)
+        return carry
+
+    lax.fori_loop(1, dp_count, hello, 0)
+    pl.semaphore_signal(barrier, inc=1, device_id=(place, other), device_id_type=MESH)
+    pl.semaphore_wait(barrier, dp_count)
+
+    gathers = [
+        Gather(
+            dp_count,
+            place,
+            half,
+            orders[which],
+            full,
+            start,
+            size,
+            gather_sems.at[0, i],
+            gather_sems.at[1, i],
+        )
+        for i, (group, which, start, size) in enumerate(gather_plan)
+    ]
+
+    def advance(step):
+        for (group, _, _, _), gather in zip(gather_plan, gathers):
+            stage = step - group
+            if 0 <= stage < stages:
+                if stage > 0:
+                    gather.copy(stage - 1).wait_recv()
+                gather.copy(stage).start()
+
+    def need(wanted):
+        for (group, _, _, _), gather in zip(gather_plan, gathers):
+            if group == wanted:
+                gather.copy(stages - 1).wait_recv()
+
+    def swing(buf, land, sems, stage, last_ref):
+        copy = pltpu.make_async_remote_copy(
+            src_ref=buf.at[stage],
+            dst_ref=land.at[stage],
+            send_sem=sems.at[0, stage],
+            recv_sem=sems.at[1, stage],
+            device_id=(flip(place, bits[stage]), half),
+            device_id_type=MESH,
+        )
+
+        def fold():
+            copy.wait()
+            total = buf[stage] + land[stage]
+            if stage < stages - 1:
+                buf[stage + 1] = total
+            else:
+                last_ref[...] = total
+
+        return copy.start, fold
+
+    push(x_send, x_land, x_sems)
+    begin, fold = swing(vec_buf, vec_land, vec_sems, 0, vec)
+    begin()
+    advance(0)
+    arrange(cot_ref, dy_send)
+    for stage in range(1, stages):
+        fold()
+        begin, fold = swing(vec_buf, vec_land, vec_sems, stage, vec)
+        begin()
+        advance(stage)
+    push(dy_send, dy_land, dy_sems)
+    fold()
+
+    route = vec[6:7, :]
+    target = jnp.floor((route + 0.5) * (1.0 / blocks))
+    in_bin = route - dp_count * jnp.floor((route + 0.5) * (1.0 / dp_count))
+    placed = jnp.where(target == place.astype(F32), in_bin, 0.0)
+    placed_rows = jnp.broadcast_to(placed, (8, blocks * dp_count))
+
+    def mask_bin(m, carry):
+        shape = (2 * bin_half, blocks * dp_count)
+        row = lax.broadcasted_iota(jnp.int32, shape, 0)
+        lane = lax.broadcasted_iota(jnp.int32, shape, 1)
+        source = lax.rem(row, bin_half) // rows
+        chosen = (lane // dp_count) == source * micro + m
+        tall_place = jnp.sum(jnp.where(chosen, placed, 0.0), axis=1, keepdims=True)
+        wide_place = mm(placed_rows, chosen.astype(F32), NT)[0:1, :]
+        ends, end = [], 0
+        for i in range(lengths_ref.shape[1] - 1):
+            end = end + lengths_ref[m, i]
+            ends.append(end.astype(F32))
+
+        def sequence(at, index):
+            within = (lax.rem(index, rows) + (index // bin_half) * rows).astype(F32)
+            position = at * block_len + within
+            return sum((position >= end).astype(F32) for end in ends)
+
+        down = sequence(
+            tall_place, lax.broadcasted_iota(jnp.int32, (2 * bin_half, 1), 0)
+        )
+        across = sequence(
+            wide_place, lax.broadcasted_iota(jnp.int32, (1, 2 * bin_half), 1)
+        )
+        bias[m] = jnp.where(down == across, 0.0, -1e30)
+        return carry
+
+    lax.fori_loop(0, micro, mask_bin, 0)
+
+    settle(x_send, x_land, x_sems)
+
+    def order_rows(m, carry):
+        block = x_land[:, m].astype(F32).reshape(bin_half, width)
+        xs[half, pl.ds(pl.multiple_of(m * bin_half, bin_half), bin_half), :] = block.astype(LOW)
+        return carry
+
+    lax.fori_loop(0, micro, order_rows, 0)
+    swap_x = pair_copy(xs.at[half], xs.at[half], 0)
+    swap_x.start()
+    advance(stages)
+    swap_x.wait()
+    need(0)
+
+    def project(i, carry):
+        h = lax.rem(half + i, 2)
+        own_rows = xs[h]
+        qkv[h, :, pl.ds(0, heads_wide)] = (
+            (mm(own_rows, weights(0, heads_wide)) + bq_ref[...].astype(F32)).astype(LOW)
+            * LOW(HD ** (-0.5))
+        )
+        qkv[h, :, pl.ds(key_col, heads_wide)] = mm(own_rows, weights(key_col, heads_wide)).astype(LOW)
+        qkv[h, :, pl.ds(value_col, heads_wide)] = (
+            mm(own_rows, weights(value_col, heads_wide)) + bv_ref[...].astype(F32)
+        ).astype(LOW)
+        return carry
+
+    lax.fori_loop(0, 2, project, 0)
+    advance(stages + 1)
+
+    low_lane = lax.broadcasted_iota(jnp.int32, (2 * bin_half, LANES), 1) < HD
+    nothing = jnp.zeros((2 * bin_half, LANES), LOW)
+
+    def bin_of(ref, m, start):
+        at = pl.ds(pl.multiple_of(m * bin_half, bin_half), bin_half)
+        return jnp.concatenate([ref[0, at, pl.ds(start, LANES)], ref[1, at, pl.ds(start, LANES)]], axis=0)
+
+    def put_bin(ref, m, start, value):
+        at = pl.ds(pl.multiple_of(m * bin_half, bin_half), bin_half)
+        ref[0, at, pl.ds(start, LANES)] = value[:bin_half].astype(ref.dtype)
+        ref[1, at, pl.ds(start, LANES)] = value[bin_half:].astype(ref.dtype)
+
+    def split_heads(value):
+        return (jnp.where(low_lane, value, nothing), jnp.where(low_lane, nothing, value))
+
+    def attend(m):
+        for j in range(pairs):
+            query = bin_of(qkv, m, j * LANES)
+            key = bin_of(qkv, m, key_col + j * LANES)
+            value = bin_of(qkv, m, value_col + j * LANES)
+            total = None
+            for e, (query_e, value_e) in enumerate(zip(split_heads(query), split_heads(value))):
+                score = mm(query_e, key, NT) + bias[m]
+                power = jnp.exp(score - jnp.max(score, axis=1, keepdims=True))
+                prob = power * (1.0 / jnp.sum(power, axis=1, keepdims=True))
+                probs[m, 2 * j + e] = prob.astype(probs.dtype)
+                part = mm(prob.astype(LOW), value_e)
+                total = part if total is None else total + part
+            put_bin(attn, m, j * LANES, total)
+
+    for m in range(micro):
+        attend(m)
+        advance(stages + 2 + m)
+    for step in range(stages + 2 + micro, stages + max(g for g, _, _, _ in gather_plan)):
+        advance(step)
+
+    def two_halves(left_ref, columns, start, send_ref, which, land_ref):
+        away = mm(left_ref[other], weights(start, columns), NT)
+        send_ref[...] = away.astype(send_ref.dtype)
+        copy = pair_copy(send_ref, land_ref, which)
+        copy.start()
+        own_part[...] = mm(left_ref[half], weights(start, columns), NT)
+        return copy
+
+    need(1)
+    copy = two_halves(attn, heads_wide, out_col, part_send, 1, part_land.at[0])
+    chunk = 4 * rows
+    per_bin = bin_half // chunk
+    chunks = tall // chunk
+    ones = jnp.ones((8, tall), LOW)
+
+    def mean_of(v):
+        return jnp.sum(v, axis=1, keepdims=True) * (1.0 / width)
+
+    copy.wait()
+
+    def norm_attn(i, carry):
+        at = pl.ds(pl.multiple_of(i * chunk, chunk), chunk)
+        mid = xs[half, at, :].astype(F32) + (own_part[at, :] + part_land[0, at, :]) + vec[0:1, :]
+        centre = mid - mean_of(mid)
+        inverse_s = lax.rsqrt(mean_of(centre * centre) + EPS_NORM)
+        unit = centre * inverse_s
+        normed[at, :] = unit
+        spread[at, :] = jnp.broadcast_to(inverse_s, (chunk, LANES))
+        hs[half, at, :] = (unit * vec[1:2, :] + vec[2:3, :]).astype(LOW)
+        return carry
+
+    lax.fori_loop(0, chunks, norm_attn, 0)
+    swap_h = pair_copy(hs.at[half], hs.at[half], 2)
+    swap_h.start()
+    need(2)
+
+    def widen(h):
+        for i in range(ff // tile):
+            start = i * tile
+            row = 8 + start // width
+            inner = mm(hs[h], weights(inner_col + start, tile)) + vec[
+                row : row + 1, start % width : start % width + tile
+            ]
+            cdf = 0.5 * (1.0 + lax.erf(inner * (0.5**0.5)))
+            density = jnp.exp(-0.5 * inner * inner) * ((2.0 * math.pi) ** -0.5)
+            gelu_low[h, :, start : start + tile] = (inner * cdf).astype(LOW)
+            dgelu[h, :, start : start + tile] = (cdf + inner * density).astype(dgelu.dtype)
+
+    def widen_step(i, carry):
+        @pl.when(i == 1)
+        def _():
+            swap_h.wait()
+
+        widen(lax.rem(half + i, 2))
+        return carry
+
+    lax.fori_loop(0, 2, widen_step, 0)
+    xs_flipped[...] = xs[...].reshape(2 * tall, width).T
+    hs_flipped[...] = hs[...].reshape(2 * tall, width).T
+    for group in range(3, max(g for g, _, _, _ in gather_plan) + 1):
+        need(group)
+    copy = two_halves(gelu_low, ff, outer_col, part_send, 3, part_land.at[1])
+    settle(dy_send, dy_land, dy_sems)
+    for i in range(3):
+        vec_acc[i] = jnp.zeros((8, width), F32)
+    copy.wait()
+
+    def fold_rows(v):
+        return jnp.sum(v.reshape(chunk // 8, 8, width), axis=0)
+
+    def norm_ffn(i, carry):
+        at = pl.ds(pl.multiple_of(i * chunk, chunk), chunk)
+        m, quarter = i // per_bin, lax.rem(i, per_bin)
+        sources = pl.ds(quarter * (chunk // rows), chunk // rows)
+        hidden = normed[at, :] * vec[1:2, :] + vec[2:3, :]
+        top = hidden + (own_part[at, :] + part_land[1, at, :]) + vec[3:4, :]
+        centre = top - mean_of(top)
+        inverse_s = lax.rsqrt(mean_of(centre * centre) + EPS_NORM)
+        unit = centre * inverse_s
+        result = unit * vec[4:5, :] + vec[5:6, :]
+        out_send[sources, m] = result.reshape(chunk // rows, rows, width).astype(LOW)
+        dy = dy_land[sources, m].astype(F32).reshape(chunk, width)
+        vec_acc[0] = vec_acc[0] + fold_rows(dy * unit)
+        vec_acc[1] = vec_acc[1] + fold_rows(dy)
+        scaled = dy * vec[4:5, :]
+        grad_top = (scaled - mean_of(scaled) - unit * mean_of(scaled * unit)) * inverse_s
+        grad_keep[at, :] = grad_top
+        gs[half, at, :] = grad_top.astype(LOW)
+        return carry
+
+    lax.fori_loop(0, chunks, norm_ffn, 0)
+    swap_g = pair_copy(gs.at[half], gs.at[half], 4)
+    swap_g.start()
+    push(out_send, out_land, out_sems)
+    vecg_buf[0, 4:5, :] = jnp.sum(vec_acc[0], axis=0, keepdims=True)
+    vecg_buf[0, 5:6, :] = jnp.sum(vec_acc[1], axis=0, keepdims=True)
+    vecg_buf[0, 3:4, :] = mm(ones, gs[half])[0:1, :]
+
+    def narrow(h):
+        for i in range(ff // tile):
+            start = i * tile
+            grad = mm(gs[h], weights(outer_col + start, tile)) * dgelu[h, :, start : start + tile].astype(F32)
+            ginner[h, :, start : start + tile] = grad.astype(LOW)
+
+    def narrow_step(i, carry):
+        @pl.when(i == 1)
+        def _():
+            swap_g.wait()
+
+        narrow(lax.rem(half + i, 2))
+        return carry
+
+    lax.fori_loop(0, 2, narrow_step, 0)
+
+    scatters = [
+        Scatter(
+            dp_count,
+            place,
+            half,
+            orders[which],
+            grads,
+            start,
+            size,
+            landings[i],
+            scatter_sems.at[0, i],
+            scatter_sems.at[1, i],
+        )
+        for i, (group, which, start, size) in enumerate(scatter_plan)
+    ]
+    members = lambda wanted: [
+        (plan, scatter) for plan, scatter in zip(scatter_plan, scatters) if plan[0] == wanted
+    ]
+
+    def reduce_start(group):
+        for _, scatter in members(group):
+            scatter.copy(0).start()
+
+    def reduce_step(group, stage):
+        for _, scatter in members(group):
+            scatter.copy(stage).wait_recv()
+            if stage < stages - 1:
+                scatter.add(stage)
+                scatter.copy(stage + 1).start()
+            else:
+                scatter.finish(stage, sum_ref, scatter.cols)
+
+    def grad_columns(left_t, right_ref, start, columns, grads_start):
+        for i in range(columns // tile):
+            piece = mm(left_t, right_ref[:, :, start + i * tile : start + (i + 1) * tile].reshape(2 * tall, tile))
+            grads[(slice(None),) * (stages + 1) + (pl.ds(grads_start + i * tile, tile),)] = piece.astype(
+                LOW
+            ).reshape(bits_shape + (own_width, tile))
+
+    bits_shape = (2,) * stages
+    copy = two_halves(ginner, ff, inner_col, part_send, 5, part_land.at[2])
+    flipped[...] = gs[...].reshape(2 * tall, width).T
+    grad_columns(flipped[...], gelu_low, 0, ff, outer_col)
+    reduce_start(0)
+    for i in range(ff // width):
+        columns = slice(i * width, (i + 1) * width)
+        vecg_buf[0, 6 + i : 7 + i, :] = (mm(ones, ginner[0, :, columns]) + mm(ones, ginner[1, :, columns]))[0:1, :]
+    copy.wait()
+    for i in range(3):
+        vec_acc[i] = jnp.zeros((8, width), F32)
+
+    def norm_back(i, carry):
+        at = pl.ds(pl.multiple_of(i * chunk, chunk), chunk)
+        grad_hidden = grad_keep[at, :] + (own_part[at, :] + part_land[2, at, :])
+        unit = normed[at, :]
+        vec_acc[0] = vec_acc[0] + fold_rows(grad_hidden * unit)
+        vec_acc[1] = vec_acc[1] + fold_rows(grad_hidden)
+        scaled = grad_hidden * vec[1:2, :]
+        grad_mid = (scaled - mean_of(scaled) - unit * mean_of(scaled * unit)) * spread[at, 0:1]
+        grad_keep[at, :] = grad_mid
+        gb[half, at, :] = grad_mid.astype(LOW)
+        return carry
+
+    lax.fori_loop(0, chunks, norm_back, 0)
+    swap_b = pair_copy(gb.at[half], gb.at[half], 6)
+    swap_b.start()
+    vecg_buf[0, 1:2, :] = jnp.sum(vec_acc[0], axis=0, keepdims=True)
+    vecg_buf[0, 2:3, :] = jnp.sum(vec_acc[1], axis=0, keepdims=True)
+    vecg_buf[0, 0:1, :] = mm(ones, gb[half])[0:1, :]
+    grad_columns(hs_flipped[...], ginner, 0, ff, inner_col)
+    swap_b.wait()
+    flipped[...] = gb[...].reshape(2 * tall, width).T
+    grad_columns(flipped[...], attn, 0, heads_wide, out_col)
+    reduce_start(1)
+
+    def to_heads(h, carry):
+        gattn[h] = mm(gb[h], weights(out_col, heads_wide)).astype(LOW)
+        return carry
+
+    lax.fori_loop(0, 2, to_heads, 0)
+
+    def attend_back(m):
+        for j in range(pairs):
+            query = bin_of(qkv, m, j * LANES)
+            key = bin_of(qkv, m, key_col + j * LANES)
+            value = bin_of(qkv, m, value_col + j * LANES)
+            grad = bin_of(gattn, m, j * LANES)
+            keys, queries, upstream = split_heads(key), split_heads(query), split_heads(grad)
+            d_query = d_key = d_value = None
+            for e in range(2):
+                prob = probs[m, 2 * j + e].astype(F32)
+                d_prob = mm(upstream[e], value, NT)
+                inner = jnp.sum(prob * d_prob, axis=1, keepdims=True)
+                d_score = (prob * (d_prob - inner)).astype(LOW)
+                part_q = mm(d_score, keys[e])
+                part_k = mm(d_score.T, queries[e])
+                part_v = mm(prob.astype(LOW).T, upstream[e])
+                d_query = part_q if d_query is None else d_query + part_q
+                d_key = part_k if d_key is None else d_key + part_k
+                d_value = part_v if d_value is None else d_value + part_v
+            put_bin(dqkv, m, j * LANES, d_query * (HD ** (-0.5)))
+            put_bin(dqkv, m, key_col + j * LANES, d_key)
+            put_bin(dqkv, m, value_col + j * LANES, d_value)
+
+    attend_back(0)
+    reduce_step(0, 0)
+    for m in range(1, micro):
+        attend_back(m)
+    reduce_step(0, 1)
+
+    away = mm(dqkv[other], weights(0, 3 * heads_wide), NT)
+    last_send[...] = away.astype(LOW)
+    copy = pair_copy(last_send, last_land, 7)
+    copy.start()
+    grad_columns(xs_flipped[...], dqkv, 0, 3 * heads_wide, 0)
+    reduce_start(2)
+    own_part[...] = mm(dqkv[half], weights(0, 3 * heads_wide), NT)
+    copy.wait()
+
+    def leave(i, carry):
+        at = pl.ds(pl.multiple_of(i * chunk, chunk), chunk)
+        m, quarter = i // per_bin, lax.rem(i, per_bin)
+        sources = pl.ds(quarter * (chunk // rows), chunk // rows)
+        grad_x = grad_keep[at, :] + (own_part[at, :] + last_land[at, :].astype(F32))
+        gx_send[sources, m] = grad_x.reshape(chunk // rows, rows, width).astype(LOW)
+        return carry
+
+    lax.fori_loop(0, chunks, leave, 0)
+    push(gx_send, gx_land, gx_sems)
+    for i, start in enumerate((0, value_col)):
+        columns = slice(start, start + heads_wide)
+        vecg_buf[0, 8:9, i * heads_wide : (i + 1) * heads_wide] = (
+            mm(ones, dqkv[0, :, columns]) + mm(ones, dqkv[1, :, columns])
+        )[0:1, :]
+    vecg_buf[0, 9:16, :] = jnp.zeros((7, width), F32)
+
+    swap_v = pair_copy(vecg_buf.at[0], vec_pair, 8)
+    swap_v.start()
+    swap_v.wait()
+    vecg_buf[0, 0:6, :] = vecg_buf[0, 0:6, :] + vec_pair[0:6, :]
+    begin, fold = swing(vecg_buf, vecg_land, vecg_sems, 0, vec_out_ref)
+    begin()
+    reduce_step(1, 0)
+    reduce_step(0, 2)
+    fold()
+    begin, fold = swing(vecg_buf, vecg_land, vecg_sems, 1, vec_out_ref)
+    begin()
+    reduce_step(1, 1)
+    reduce_step(0, 3)
+    fold()
+    for stage in range(2, stages):
+        begin, fold = swing(vecg_buf, vecg_land, vecg_sems, stage, vec_out_ref)
+        begin()
+        fold()
+    reduce_step(2, 0)
+    reduce_step(1, 2)
+    reduce_step(2, 1)
+    reduce_step(1, 3)
+    settle(out_send, out_land, out_sems)
+
+    def hand_back(land_ref, result_ref):
+        def one(i, carry):
+            result_ref[i] = land_ref[route_ref[i] // blocks, i // dp_count]
+            return carry
+
+        lax.fori_loop(0, blocks, one, 0)
+
+    hand_back(out_land, layer_out_ref)
+    reduce_step(2, 2)
+    settle(gx_send, gx_land, gx_sems)
+    hand_back(gx_land, grad_tokens_ref)
+    reduce_step(2, 3)
+    for gather in gathers:
+        for stage in range(stages):
+            gather.copy(stage).wait_send()
+    for scatter in scatters:
+        for stage in range(stages):
+            scatter.copy(stage).wait_send()
+
+
+def plan_of(cuts):
+    plan = []
+    for group, (start, stop) in enumerate(cuts):
+        middle = start + (stop - start + LANES) // (2 * LANES) * LANES
+        plan.append((group, 0, start, middle - start))
+        plan.append((group, 1, middle, stop - middle))
+    return plan
+
+
+def shards_fast(
+    tokens,
+    cotangent,
+    block_route,
+    lengths,
+    w_query,
+    w_key,
+    w_value,
+    b_query,
+    b_value,
+    w_out,
+    b_out,
+    gain_attn,
+    shift_attn,
+    w_inner,
+    b_inner,
+    w_outer,
+    b_outer,
+    gain_ffn,
+    shift_ffn,
+):
+    dp_count = lax.axis_size("dp")
+    micro, rows, width = lengths.shape[0], tokens.shape[1], tokens.shape[2]
+    heads_wide, ff = w_query.shape[1], w_inner.shape[1]
+    place = lax.axis_index("dp")
+    blocks = micro * dp_count
+    own_width = width // dp_count
+    columns = 4 * heads_wide + 2 * ff
+    stages = dp_count.bit_length() - 1
+    bits = (2,) * stages
+    target = block_route.reshape(micro, dp_count) // blocks
+    inverse = jnp.argmax(
+        target[:, None, :] == jnp.arange(dp_count, dtype=jnp.int32)[None, :, None], axis=2
+    ).astype(jnp.int32)
+    nothing = jnp.zeros((1, own_width), F32)
+    small = jnp.concatenate(
+        [v.astype(F32)[None] for v in (b_out, gain_attn, shift_attn, b_outer, gain_ffn, shift_ffn, block_route)]
+        + [nothing],
+        axis=0,
+    )
+    inner_col, outer_col = 4 * heads_wide, 4 * heads_wide + ff
+    third = inner_col + ff // 2
+    gather_plan = plan_of(
+        [
+            (0, 3 * heads_wide),
+            (3 * heads_wide, third),
+            (third, outer_col),
+            (outer_col, outer_col + ff // 2),
+            (outer_col + ff // 2, columns),
+        ]
+    )
+    scatter_plan = plan_of([(outer_col, columns), (3 * heads_wide, outer_col), (0, 3 * heads_wide)])
+    bin_half = dp_count * rows
+    tall = micro * bin_half
+    vmem, smem = pl.BlockSpec(memory_space=pltpu.VMEM), pl.BlockSpec(memory_space=pltpu.SMEM)
+    dma = pltpu.SemaphoreType.DMA
+    swap_shape = (dp_count, micro, rows, width)
+    scratch = [
+        pltpu.VMEM(bits + (own_width, columns), LOW),
+        pltpu.VMEM(bits + (own_width, columns), LOW),
+    ]
+    scratch += [pltpu.VMEM(swap_shape, LOW) for _ in range(8)]
+    scratch += [pltpu.VMEM((2, tall, width), LOW) for _ in range(4)]
+    scratch += [pltpu.VMEM((width, 2 * tall), LOW) for _ in range(3)]
+    scratch += [pltpu.VMEM((2, tall, 3 * heads_wide), LOW) for _ in range(2)]
+    scratch += [pltpu.VMEM((2, tall, heads_wide), LOW) for _ in range(2)]
+    scratch += [
+        pltpu.VMEM((micro, heads_wide // HD, 2 * bin_half, 2 * bin_half), LOW),
+        pltpu.VMEM((micro, 2 * bin_half, 2 * bin_half), F32),
+    ]
+    scratch += [pltpu.VMEM((2, tall, ff), LOW) for _ in range(3)]
+    scratch += [
+        pltpu.VMEM((tall, width), F32),
+        pltpu.VMEM((tall, LANES), F32),
+        pltpu.VMEM((tall, width), F32),
+        pltpu.VMEM((tall, width), F32),
+        pltpu.VMEM((tall, width), F32),
+        pltpu.VMEM((3, tall, width), F32),
+        pltpu.VMEM((tall, width), LOW),
+        pltpu.VMEM((tall, width), LOW),
+        pltpu.VMEM((stages, 16, width), F32),
+        pltpu.VMEM((stages, 16, width), F32),
+        pltpu.VMEM((16, width), F32),
+        pltpu.VMEM((16, width), F32),
+        pltpu.VMEM((stages, 16, width), F32),
+        pltpu.VMEM((stages, 16, width), F32),
+        pltpu.VMEM((3, 8, width), F32),
+    ]
+    scratch += [
+        pltpu.VMEM((2,) * (stages - 1 - stage) + (own_width, size), LOW)
+        for _, _, _, size in scatter_plan
+        for stage in range(stages)
+    ]
+    scratch += [dma((2, dp_count)) for _ in range(4)]
+    scratch += [
+        dma((2, len(gather_plan), stages)),
+        dma((2, len(scatter_plan), stages)),
+        dma((2, stages)),
+        dma((2, stages)),
+        dma((2, 9)),
+    ]
+    sizes = (dp_count, micro, rows, width, heads_wide, ff)
+    layer_out, grad_tokens, sums, total = pl.pallas_call(
+        partial(layer, sizes, gather_plan, scatter_plan),
+        out_shape=(
+            jax.ShapeDtypeStruct(tokens.shape, tokens.dtype),
+            jax.ShapeDtypeStruct(tokens.shape, tokens.dtype),
+            jax.ShapeDtypeStruct((own_width, columns), F32),
+            jax.ShapeDtypeStruct((16, width), F32),
+        ),
+        in_specs=[vmem] * 2 + [smem] * 3 + [vmem] * 10,
+        out_specs=[vmem] * 4,
+        scratch_shapes=scratch,
+        compiler_params=pltpu.CompilerParams(
+            collective_id=0, has_side_effects=True, vmem_limit_bytes=VMEM_BYTES
+        ),
+        name="layer",
+    )(
+        tokens,
+        cotangent,
+        block_route,
+        inverse,
+        lengths,
+        w_query,
+        w_key,
+        w_value,
+        w_out,
+        w_inner,
+        w_outer,
+        small,
+        b_query,
+        b_value,
+        b_inner,
+    )
+    own_inner = b_inner.shape[1]
+    vec_own = lax.dynamic_slice_in_dim(total[:6], place * own_width, own_width, 1)
+    sum_bias_inner = lax.dynamic_slice_in_dim(
+        total[6:8].reshape(1, ff), place * own_inner, own_inner, 1
+    )
+    return (
+        layer_out,
+        grad_tokens,
+        sums[:, :heads_wide],
+        sums[:, heads_wide : 2 * heads_wide],
+        sums[:, 2 * heads_wide : 3 * heads_wide],
+        total[8:9, :heads_wide],
+        total[8:9, heads_wide:],
+        sums[:, 3 * heads_wide : 4 * heads_wide].T,
+        vec_own[0],
+        vec_own[1],
+        vec_own[2],
+        sums[:, inner_col:outer_col],
+        sum_bias_inner,
+        sums[:, outer_col:].T,
+        vec_own[3],
+        vec_own[4],
+        vec_own[5],
+    )
 
 
 def shards(
@@ -410,8 +1331,20 @@
         P("dp"),
         P("dp"),
     )
+    dp_count = mesh.shape["dp"]
+
+    def body(*args):
+        tokens, w_query, b_inner = args[0], args[4], args[14]
+        fits = (
+            dp_count & (dp_count - 1) == 0
+            and w_query.shape[0] % 16 == 0
+            and tokens.shape[1] % 8 == 0
+            and mesh.shape["tensor"] == 2
+        )
+        return (shards_fast if fits else shards)(*args)
+
     return jax.shard_map(
-        shards,
+        body,
         mesh=mesh,
         in_specs=placed,
         out_specs=(

time: 1510 us -> 242 us (0.16); the launches traced: 1490 us -> 242 us
  waiting for transfers between devices: 901 us -> 0 us
  blocking collectives: 311 us -> 0 us
  Pallas kernels: 0 us -> 224 us
  matrix products: 107 us -> 0 us
  local copies, waits for them, and re-layouts: 70.7 us -> 13 us
  other arithmetic: 54 us -> 4.25 us
  starting transfers between devices: 30.5 us -> 0 us
  between operations: 20.2 us -> 0.7 us
    reduce_scatter x15 -> x0, waiting for transfers between devices: 762 us -> none  [the longest x1 143 us: shards(): lax.psum_scatter(acc_inner, 'dp', scatter_dimension=0, tiled=True)]
    pallas_call x0 -> x1, Pallas kernels: none -> 224 us  [shards_fast(): pl.pallas_call(partial(layer, sizes, gather_plan, scatter_plan), out_shap...]
    all_gather x16 -> x0, blocking collectives: 197 us -> none  [the longest x1 45.2 us: shards(): lax.all_gather(w_query, 'dp', axis=0, tiled=True)]
    dot_general x72 -> x0, matrix products: 107 us -> none  [the longest x3 21.8 us: shards(): jnp.dot(hidden_whole, full_inner, preferred_element_type=jnp.float32)]
    unnamed x25 -> x0, waiting for transfers between devices: 104 us -> none
    unnamed x1 -> x0, blocking collectives: 72.9 us -> none
    psum x1 -> x0, blocking collectives: 41.3 us -> none  [shards(): vectors, bias_total = lax.psum((acc_vectors, bias_pair), ('dp', 'tensor'))]
    all_gather x2 -> x0, waiting for transfers between devices: 32.5 us -> none  [the longest x1 32.5 us: shards(): lax.all_gather(w_outer, 'dp', axis=1, tiled=True)]
  transfers between devices with their start and end apart: 26 -> 0, of which waited for: 13 -> 0; matrix products, arithmetic and copies ran while one was open for 9% -> 0% of each run, Pallas kernels for 0% -> 0%
where the time goes in v2:
time: 242 us
  Pallas kernels  224 us (93%)
  local copies, waits for them, and re-layouts  13 us (5%)
  other arithmetic  4.25 us (2%)
    pallas_call x1, Pallas kernels, shards_fast(): pl.pallas_call(partial(layer, sizes, gather_plan, scatter_plan), out_shap...  224 us
    unnamed x12, local copies, waits for them, and re-layouts  5.28 us

profile of v2, /device:TPU:0, one launch (start us, length us, event | category | flops | bytes accessed | tf_op | source)
XLA Modules:
  0.0 241.6 jit_solution(9781633253995072767)
XLA Ops:
  0.7 0.0 copy-start.2
  0.7 0.7 compare_and_fusion
  1.4 0.1 and.15
  1.5 0.7 bitcast_convert_fusion.4
  2.1 0.7 bitcast_convert_fusion.2
  2.8 0.7 bitcast_convert_fusion
  3.5 0.7 convert_bitcast_fusion
  4.2 0.6 concatenate.3.refs_11_
  4.8 0.1 div.14
  4.9 0.8 iota_reduce_fusion
  5.7 1.5 copy.38.refs_8_
  7.2 0.0 copy-done.2
  7.2 0.9 copy.39.refs_10_
  8.1 223.7 %layer.1 = (bf16[48,8,768]{2,1,0:T(8,128)(2,1)}, bf16[48,8,768]{2,1,0:T(8,128)(2,1)}, f32[48,4608]{1,0:T(8,128)}, f32[16,768]{1,0:T(8,128)}) custom-call(bf16[48,8,768]{2,1,0:T(8,128)(2,1)} %refs_0_.1, bf16[48,8,768]{2,1,0:T(8,128)(2,1)} %refs_1_.1, s32[48]{0:T(128)} %refs_2_.1, s32[3,16]{1,0:T(4,128)} %get-tuple-element.22.refs_3_, s32[3,3]{1,0:T(4,128)} %refs_4_.1, ...), custom_call_target="tpu_custom_call" | custom-call | tf_op jit(solution)/shard_map/layer/pallas_call | solution.py:950
  231.9 1.3 fusion
  233.2 0.7 slice_bitcast_fusion.2
  233.9 0.7 slice.54
  234.7 0.1 constant_dynamic-slice_fusion.1
  234.7 0.5 slice_bitcast_fusion.3
  235.3 0.6 constant_dynamic-slice_fusion
  235.9 1.7 slice_bitcast_fusion.1
  237.6 0.0 copy-start.1
  237.6 2.0 slice_bitcast_fusion
  239.5 0.0 copy-done.1
  239.5 0.0 copy-start
  239.5 0.8 copy.43
  240.4 0.5 copy-done
  240.8 0.8 copy.44
  (3 shorter events, 0.0 us)
Async XLA Ops:
  0.7 6.6 %copy-start.2 = (bf16[1536,48]{0,1:T(8,128)(2,1)S(1)}, bf16[1536,48]{0,1:T(8,128)(2,1)}, u32[]{:S(2)}) copy-start(bf16[1536,48]{0,1:T(8,128)(2,1)} %param.34) | copy-start | bytes 442372
  237.6 2.0 copy-start.1
  239.5 1.3 copy-start

commit v3 on v2

--- a/solution.py
+++ b/solution.py
@@ -141,7 +141,7 @@
 class Scatter:
     def __init__(self, dp_count, place, half, order, ref, start, size, landing, send_sem, recv_sem):
         self.place, self.half = place, half
-        self.order = order[::-1]
+        self.order = order
         self.bits = bits_of(dp_count)
         self.ref, self.cols = ref, pl.ds(start, size)
         self.landing = landing
@@ -188,9 +188,17 @@
         else:
             lax.fori_loop(0, count, one, 0)
 
-    def finish(self, stage, out_ref, out_cols):
+    def finish(self, stage, outs):
         kept = self.view(stage, "own")
-        out_ref[:, out_cols] = kept[...].astype(F32) + self.landing[stage][...].astype(F32)
+        sums, refs, copy_out = outs
+        sums[:, self.cols] = kept[...].astype(F32) + self.landing[stage][...].astype(F32)
+        first, begin = self.cols.start, 0
+        for ref in refs:
+            low = max(first, begin)
+            high = min(first + self.cols.size, begin + ref.shape[1])
+            if low < high:
+                copy_out(sums.at[:, pl.ds(low, high - low)], ref.at[:, pl.ds(low - begin, high - low)])
+            begin += ref.shape[1]
 
 
 def layer(sizes, gather_plan, scatter_plan, *refs):
@@ -199,7 +207,6 @@
         tokens_ref,
         cot_ref,
         route_ref,
-        inverse_ref,
         lengths_ref,
         wq_ref,
         wk_ref,
@@ -207,14 +214,28 @@
         wo_ref,
         wi_ref,
         wu_ref,
-        small_ref,
+        *small_refs,
         bq_ref,
         bv_ref,
         bi_ref,
+        layer_out_hbm,
+        grad_tokens_hbm,
+        gq_hbm,
+        gk_hbm,
+        gv_hbm,
+        go_hbm,
+        gi_hbm,
+        gu_hbm,
+    ) = refs[:28]
+    vec_out_ref = refs[28]
+    (
+        inverse_ref,
+        target_ref,
+        tokens_in,
+        cot_in,
         layer_out_ref,
         grad_tokens_ref,
-        sum_ref,
-        vec_out_ref,
+        sums,
         full,
         grads,
         x_send,
@@ -243,21 +264,22 @@
         ginner,
         normed,
         spread,
+        spread_ffn,
         grad_keep,
         own_part,
         part_send,
         part_land,
         last_send,
         last_land,
-        vec_buf,
-        vec_land,
+        piece,
+        pieces,
         vec,
         vec_pair,
         vecg_buf,
         vecg_land,
         vec_acc,
         *rest,
-    ) = refs
+    ) = refs[29:]
     stages = dp_count.bit_length() - 1
     landings = [rest[i * stages : (i + 1) * stages] for i in range(len(scatter_plan))]
     (
@@ -270,6 +292,8 @@
         vec_sems,
         vecg_sems,
         pair_sems,
+        in_sems,
+        out_copy_sems,
     ) = rest[len(scatter_plan) * stages :]
     place, half = lax.axis_index("dp"), lax.axis_index("tensor")
     other = 1 - half
@@ -298,37 +322,38 @@
             device_id_type=MESH,
         )
 
-    def push(send_ref, recv_ref, sems):
+    group = dp_count // 2
+    base, within_group = place - lax.rem(place, group), lax.rem(place, group)
+    far_base = lax.rem(base + group, dp_count)
+
+    def message(step, sign, send_ref, recv_ref, sems, near):
+        index = step if near else group + step
+        peer = (base if near else far_base) + lax.rem(within_group + group + sign * step, group)
+        return pltpu.make_async_remote_copy(
+            src_ref=send_ref.at[peer],
+            dst_ref=recv_ref.at[place if sign > 0 else peer],
+            send_sem=sems.at[0, index],
+            recv_sem=sems.at[1, index],
+            device_id=(peer, half),
+            device_id_type=MESH,
+        )
+
+    def push(send_ref, recv_ref, sems, near):
         def one(step, carry):
-            peer = lax.rem(place + step, dp_count)
-            pltpu.make_async_remote_copy(
-                src_ref=send_ref.at[peer],
-                dst_ref=recv_ref.at[place],
-                send_sem=sems.at[0, step],
-                recv_sem=sems.at[1, step],
-                device_id=(peer, half),
-                device_id_type=MESH,
-            ).start()
+            message(step, 1, send_ref, recv_ref, sems, near).start()
             return carry
 
-        lax.fori_loop(1, dp_count, one, 0)
+        lax.fori_loop(1 if near else 0, group, one, 0)
 
     def settle(send_ref, recv_ref, sems):
         recv_ref[place] = send_ref[place]
-
-        def one(step, carry):
-            source = lax.rem(place + dp_count - step, dp_count)
-            pltpu.make_async_remote_copy(
-                src_ref=send_ref.at[source],
-                dst_ref=recv_ref.at[source],
-                send_sem=sems.at[0, step],
-                recv_sem=sems.at[1, step],
-                device_id=(source, half),
-                device_id_type=MESH,
-            ).wait()
-            return carry
-
-        lax.fori_loop(1, dp_count, one, 0)
+        for near in (True, False):
+
+            def one(step, carry):
+                message(step, -1, send_ref, recv_ref, sems, near).wait()
+                return carry
+
+            lax.fori_loop(1 if near else 0, group, one, 0)
 
     def arrange(src_ref, dst_ref):
         def one(i, carry):
@@ -338,37 +363,6 @@
 
         lax.fori_loop(0, blocks, one, 0)
 
-    own = tuple(bit_of(place, bit) for bit in bits)
-    eye = (
-        lax.broadcasted_iota(jnp.int32, (own_width, own_width), 0)
-        == lax.broadcasted_iota(jnp.int32, (own_width, own_width), 1)
-    ).astype(LOW)
-    full[own + (slice(None), pl.ds(0, heads_wide))] = wq_ref[...]
-    full[own + (slice(None), pl.ds(key_col, heads_wide))] = wk_ref[...]
-    full[own + (slice(None), pl.ds(value_col, heads_wide))] = wv_ref[...]
-    full[own + (slice(None), pl.ds(out_col, heads_wide))] = mm(eye, wo_ref[...], NT).astype(LOW)
-    full[own + (slice(None), pl.ds(inner_col, ff))] = wi_ref[...]
-    full[own + (slice(None), pl.ds(outer_col, ff))] = mm(eye, wu_ref[...], NT).astype(LOW)
-
-    def spread_out(piece, total):
-        size = piece.shape[1]
-        target = lax.broadcasted_iota(jnp.int32, (size, total), 1)
-        at = lax.broadcasted_iota(jnp.int32, (size, total), 0) + place * size
-        return lax.dot_general(
-            piece,
-            (target == at).astype(F32),
-            NN,
-            precision=lax.Precision.HIGHEST,
-            preferred_element_type=F32,
-        )
-
-    vec_buf[0, 0:8, :] = spread_out(small_ref[...], width)
-    long_row = spread_out(jnp.broadcast_to(bi_ref[...].astype(F32), (8, bi_ref.shape[1])), ff)
-    vec_buf[0, 8:16, :] = jnp.zeros((8, width), F32)
-    for i in range(ff // width):
-        vec_buf[0, 8 + i : 9 + i, :] = long_row[0:1, i * width : (i + 1) * width]
-    arrange(tokens_ref, x_send)
-
     barrier = pltpu.get_barrier_semaphore()
 
     def hello(step, carry):
@@ -378,6 +372,58 @@
 
     lax.fori_loop(1, dp_count, hello, 0)
     pl.semaphore_signal(barrier, inc=1, device_id=(place, other), device_id_type=MESH)
+
+    own = tuple(bit_of(place, bit) for bit in bits)
+    fetches = [
+        pltpu.make_async_copy(src, dst, in_sems.at[i])
+        for i, (src, dst) in enumerate(
+            [
+                (ref, full.at[own + (slice(None), pl.ds(start, size))])
+                for ref, start, size in (
+                    (wq_ref, 0, heads_wide),
+                    (wk_ref, key_col, heads_wide),
+                    (wv_ref, value_col, heads_wide),
+                    (wo_ref, out_col, heads_wide),
+                    (wi_ref, inner_col, ff),
+                    (wu_ref, outer_col, ff),
+                )
+            ]
+            + [(tokens_ref, tokens_in), (cot_ref, cot_in)]
+        )
+    ]
+    for fetch in fetches:
+        fetch.start()
+    leaving = []
+
+    def copy_out(src, dst):
+        copy = pltpu.make_async_copy(src, dst, out_copy_sems.at[len(leaving)])
+        copy.start()
+        leaving.append(copy)
+
+    outs = (sums, (gq_hbm, gk_hbm, gv_hbm, go_hbm, gi_hbm, gu_hbm), copy_out)
+
+    piece[...] = jnp.zeros((16, LANES), F32)
+    for i, ref in enumerate(small_refs):
+        piece[i : i + 1, 0:own_width] = ref[...].astype(F32).reshape(1, own_width)
+    piece[8:16, 0 : bi_ref.shape[1]] = jnp.broadcast_to(bi_ref[...].astype(F32), (8, bi_ref.shape[1]))
+    route = piece[6:7, 0:own_width]
+    piece[7:8, 0:own_width] = route - dp_count * jnp.floor((route + 0.5) * (1.0 / dp_count))
+    piece[6:7, 0:own_width] = jnp.floor((route + 0.5) * (1.0 / blocks))
+    def find_target(i, carry):
+        target_ref[i] = lax.div(route_ref[i], blocks)
+        return carry
+
+
+    def invert(i, carry):
+        m, peer = lax.div(i, dp_count), lax.rem(i, dp_count)
+        slot = jnp.int32(0)
+        for k in range(dp_count):
+            slot = jnp.where(target_ref[m * dp_count + k] == peer, k, slot)
+        inverse_ref[m, peer] = slot
+        return carry
+
+    for fetch in fetches[:6]:
+        fetch.wait()
     pl.semaphore_wait(barrier, dp_count)
 
     gathers = [
@@ -385,28 +431,28 @@
             dp_count,
             place,
             half,
-            orders[which],
+            order,
             full,
             start,
             size,
             gather_sems.at[0, i],
             gather_sems.at[1, i],
         )
-        for i, (group, which, start, size) in enumerate(gather_plan)
+        for i, (group, order, start, size) in enumerate(gather_plan)
     ]
-
-    def advance(step):
-        for (group, _, _, _), gather in zip(gather_plan, gathers):
-            stage = step - group
-            if 0 <= stage < stages:
-                if stage > 0:
-                    gather.copy(stage - 1).wait_recv()
-                gather.copy(stage).start()
-
-    def need(wanted):
-        for (group, _, _, _), gather in zip(gather_plan, gathers):
-            if group == wanted:
-                gather.copy(stages - 1).wait_recv()
+    gone = {}
+
+    def advance(*groups):
+        for wanted in groups:
+            stage = gone.get(wanted, 0)
+            gone[wanted] = stage + 1
+            for (group, _, _, _), gather in zip(gather_plan, gathers):
+                if group == wanted:
+                    with jax.named_scope(f"gather_{wanted}_{stage}"):
+                        if stage > 0:
+                            gather.copy(stage - 1).wait_recv()
+                        if stage < stages:
+                            gather.copy(stage).start()
 
     def swing(buf, land, sems, stage, last_ref):
         copy = pltpu.make_async_remote_copy(
@@ -428,23 +474,68 @@
 
         return copy.start, fold
 
-    push(x_send, x_land, x_sems)
-    begin, fold = swing(vec_buf, vec_land, vec_sems, 0, vec)
-    begin()
+    def push_piece(step, carry):
+        peer = lax.rem(place + step, dp_count)
+        pltpu.make_async_remote_copy(
+            src_ref=piece,
+            dst_ref=pieces.at[place],
+            send_sem=vec_sems.at[0, step],
+            recv_sem=vec_sems.at[1, step],
+            device_id=(peer, half),
+            device_id_type=MESH,
+        ).start()
+        return carry
+
+    def wait_piece(step, carry):
+        source = lax.rem(place + dp_count - step, dp_count)
+        pltpu.make_async_remote_copy(
+            src_ref=piece,
+            dst_ref=pieces.at[source],
+            send_sem=vec_sems.at[0, step],
+            recv_sem=vec_sems.at[1, step],
+            device_id=(source, half),
+            device_id_type=MESH,
+        ).wait()
+        return carry
+
+    advance(0, 4)
+    lax.fori_loop(1, dp_count, push_piece, 0)
+    advance(1)
+    lax.fori_loop(0, blocks, find_target, 0)
+    lax.fori_loop(0, blocks, invert, 0)
+    fetches[6].wait()
+    arrange(tokens_in, x_send)
+    push(x_send, x_land, x_sems, True)
+    advance(4)
+    fetches[7].wait()
+    arrange(cot_in, dy_send)
     advance(0)
-    arrange(cot_ref, dy_send)
-    for stage in range(1, stages):
-        fold()
-        begin, fold = swing(vec_buf, vec_land, vec_sems, stage, vec)
-        begin()
-        advance(stage)
-    push(dy_send, dy_land, dy_sems)
-    fold()
-
-    route = vec[6:7, :]
-    target = jnp.floor((route + 0.5) * (1.0 / blocks))
-    in_bin = route - dp_count * jnp.floor((route + 0.5) * (1.0 / dp_count))
-    placed = jnp.where(target == place.astype(F32), in_bin, 0.0)
+    push(x_send, x_land, x_sems, False)
+    pieces[place] = piece[...]
+    lax.fori_loop(1, dp_count, wait_piece, 0)
+
+    def lay(source, total):
+        block = pieces[source]
+
+        def laid(block, size, extent):
+            target = lax.broadcasted_iota(jnp.int32, (LANES, extent), 1)
+            at = lax.broadcasted_iota(jnp.int32, (LANES, extent), 0)
+            hit = (target == at + source * size) & (at < size)
+            return mm(block.astype(LOW), hit.astype(F32).astype(LOW))
+
+        return (
+            total[0] + laid(block[0:8], own_width, width),
+            total[1] + laid(block[8:16], bi_ref.shape[1], ff),
+        )
+
+    short, long = lax.fori_loop(
+        0, dp_count, lay, (jnp.zeros((8, width), F32), jnp.zeros((8, ff), F32))
+    )
+    vec[0:8, :] = short
+    for i in range(ff // width):
+        vec[8 + i : 9 + i, :] = long[0:1, i * width : (i + 1) * width]
+
+    placed = jnp.where(vec[6:7, :] == place.astype(F32), vec[7:8, :], 0.0)
     placed_rows = jnp.broadcast_to(placed, (8, blocks * dp_count))
 
     def mask_bin(m, carry):
@@ -476,6 +567,13 @@
 
     lax.fori_loop(0, micro, mask_bin, 0)
 
+    advance(0, 1)
+    advance(2)
+    advance(0, 1)
+    advance(3)
+    advance(1)
+    advance(0)
+    advance(2)
     settle(x_send, x_land, x_sems)
 
     def order_rows(m, carry):
@@ -486,9 +584,8 @@
     lax.fori_loop(0, micro, order_rows, 0)
     swap_x = pair_copy(xs.at[half], xs.at[half], 0)
     swap_x.start()
-    advance(stages)
+    advance(3, 4)
     swap_x.wait()
-    need(0)
 
     def project(i, carry):
         h = lax.rem(half + i, 2)
@@ -504,7 +601,6 @@
         return carry
 
     lax.fori_loop(0, 2, project, 0)
-    advance(stages + 1)
 
     low_lane = lax.broadcasted_iota(jnp.int32, (2 * bin_half, LANES), 1) < HD
     nothing = jnp.zeros((2 * bin_half, LANES), LOW)
@@ -538,10 +634,13 @@
 
     for m in range(micro):
         attend(m)
-        advance(stages + 2 + m)
-    for step in range(stages + 2 + micro, stages + max(g for g, _, _, _ in gather_plan)):
-        advance(step)
-
+        if m == 0:
+            advance(2, 1)
+        if m == 1:
+            advance(3)
+        if m == 2:
+            advance(4, 2)
+            push(dy_send, dy_land, dy_sems, False)
     def two_halves(left_ref, columns, start, send_ref, which, land_ref):
         away = mm(left_ref[other], weights(start, columns), NT)
         send_ref[...] = away.astype(send_ref.dtype)
@@ -550,7 +649,7 @@
         own_part[...] = mm(left_ref[half], weights(start, columns), NT)
         return copy
 
-    need(1)
+
     copy = two_halves(attn, heads_wide, out_col, part_send, 1, part_land.at[0])
     chunk = 4 * rows
     per_bin = bin_half // chunk
@@ -576,7 +675,8 @@
     lax.fori_loop(0, chunks, norm_attn, 0)
     swap_h = pair_copy(hs.at[half], hs.at[half], 2)
     swap_h.start()
-    need(2)
+    advance(2, 3)
+    push(dy_send, dy_land, dy_sems, True)
 
     def widen(h):
         for i in range(ff // tile):
@@ -601,12 +701,8 @@
     lax.fori_loop(0, 2, widen_step, 0)
     xs_flipped[...] = xs[...].reshape(2 * tall, width).T
     hs_flipped[...] = hs[...].reshape(2 * tall, width).T
-    for group in range(3, max(g for g, _, _, _ in gather_plan) + 1):
-        need(group)
+    advance(3, 4)
     copy = two_halves(gelu_low, ff, outer_col, part_send, 3, part_land.at[1])
-    settle(dy_send, dy_land, dy_sems)
-    for i in range(3):
-        vec_acc[i] = jnp.zeros((8, width), F32)
     copy.wait()
 
     def fold_rows(v):
@@ -621,21 +717,36 @@
         centre = top - mean_of(top)
         inverse_s = lax.rsqrt(mean_of(centre * centre) + EPS_NORM)
         unit = centre * inverse_s
+        own_part[at, :] = unit
+        spread_ffn[at, :] = jnp.broadcast_to(inverse_s, (chunk, LANES))
         result = unit * vec[4:5, :] + vec[5:6, :]
         out_send[sources, m] = result.reshape(chunk // rows, rows, width).astype(LOW)
+        return carry
+
+    lax.fori_loop(0, chunks, norm_ffn, 0)
+    push(out_send, out_land, out_sems, False)
+    push(out_send, out_land, out_sems, True)
+    settle(dy_send, dy_land, dy_sems)
+    for i in range(3):
+        vec_acc[i] = jnp.zeros((8, width), F32)
+
+    def norm_ffn_back(i, carry):
+        at = pl.ds(pl.multiple_of(i * chunk, chunk), chunk)
+        m, quarter = i // per_bin, lax.rem(i, per_bin)
+        sources = pl.ds(quarter * (chunk // rows), chunk // rows)
+        unit = own_part[at, :]
         dy = dy_land[sources, m].astype(F32).reshape(chunk, width)
         vec_acc[0] = vec_acc[0] + fold_rows(dy * unit)
         vec_acc[1] = vec_acc[1] + fold_rows(dy)
         scaled = dy * vec[4:5, :]
-        grad_top = (scaled - mean_of(scaled) - unit * mean_of(scaled * unit)) * inverse_s
+        grad_top = (scaled - mean_of(scaled) - unit * mean_of(scaled * unit)) * spread_ffn[at, 0:1]
         grad_keep[at, :] = grad_top
         gs[half, at, :] = grad_top.astype(LOW)
         return carry
 
-    lax.fori_loop(0, chunks, norm_ffn, 0)
+    lax.fori_loop(0, chunks, norm_ffn_back, 0)
     swap_g = pair_copy(gs.at[half], gs.at[half], 4)
     swap_g.start()
-    push(out_send, out_land, out_sems)
     vecg_buf[0, 4:5, :] = jnp.sum(vec_acc[0], axis=0, keepdims=True)
     vecg_buf[0, 5:6, :] = jnp.sum(vec_acc[1], axis=0, keepdims=True)
     vecg_buf[0, 3:4, :] = mm(ones, gs[half])[0:1, :]
@@ -646,22 +757,15 @@
             grad = mm(gs[h], weights(outer_col + start, tile)) * dgelu[h, :, start : start + tile].astype(F32)
             ginner[h, :, start : start + tile] = grad.astype(LOW)
 
-    def narrow_step(i, carry):
-        @pl.when(i == 1)
-        def _():
-            swap_g.wait()
-
-        narrow(lax.rem(half + i, 2))
-        return carry
-
-    lax.fori_loop(0, 2, narrow_step, 0)
+    narrow(half)
+    swap_g.wait()
 
     scatters = [
         Scatter(
             dp_count,
             place,
             half,
-            orders[which],
+            order,
             grads,
             start,
             size,
@@ -669,24 +773,25 @@
             scatter_sems.at[0, i],
             scatter_sems.at[1, i],
         )
-        for i, (group, which, start, size) in enumerate(scatter_plan)
+        for i, (group, order, start, size) in enumerate(scatter_plan)
     ]
-    members = lambda wanted: [
-        (plan, scatter) for plan, scatter in zip(scatter_plan, scatters) if plan[0] == wanted
-    ]
-
-    def reduce_start(group):
-        for _, scatter in members(group):
-            scatter.copy(0).start()
-
-    def reduce_step(group, stage):
-        for _, scatter in members(group):
-            scatter.copy(stage).wait_recv()
-            if stage < stages - 1:
-                scatter.add(stage)
-                scatter.copy(stage + 1).start()
-            else:
-                scatter.finish(stage, sum_ref, scatter.cols)
+    sent = {}
+
+    def reduce(*groups):
+        for wanted in groups:
+            stage = sent.get(wanted, 0)
+            sent[wanted] = stage + 1
+            for (group, _, _, _), scatter in zip(scatter_plan, scatters):
+                if group == wanted:
+                    with jax.named_scope(f"reduce_{wanted}_{stage}"):
+                        if stage > 0:
+                            scatter.copy(stage - 1).wait_recv()
+                            if stage < stages:
+                                scatter.add(stage - 1)
+                            else:
+                                scatter.finish(stage - 1, outs)
+                        if stage < stages:
+                            scatter.copy(stage).start()
 
     def grad_columns(left_t, right_ref, start, columns, grads_start):
         for i in range(columns // tile):
@@ -696,10 +801,13 @@
             ).reshape(bits_shape + (own_width, tile))
 
     bits_shape = (2,) * stages
+    flipped[...] = gs[...].reshape(2 * tall, width).T
+    grad_columns(flipped[...], gelu_low, 0, ff // 2, outer_col)
+    reduce(0)
+    grad_columns(flipped[...], gelu_low, ff // 2, ff // 2, outer_col + ff // 2)
+    reduce(1)
+    narrow(other)
     copy = two_halves(ginner, ff, inner_col, part_send, 5, part_land.at[2])
-    flipped[...] = gs[...].reshape(2 * tall, width).T
-    grad_columns(flipped[...], gelu_low, 0, ff, outer_col)
-    reduce_start(0)
     for i in range(ff // width):
         columns = slice(i * width, (i + 1) * width)
         vecg_buf[0, 6 + i : 7 + i, :] = (mm(ones, ginner[0, :, columns]) + mm(ones, ginner[1, :, columns]))[0:1, :]
@@ -729,7 +837,7 @@
     swap_b.wait()
     flipped[...] = gb[...].reshape(2 * tall, width).T
     grad_columns(flipped[...], attn, 0, heads_wide, out_col)
-    reduce_start(1)
+    reduce(2)
 
     def to_heads(h, carry):
         gattn[h] = mm(gb[h], weights(out_col, heads_wide)).astype(LOW)
@@ -760,18 +868,17 @@
             put_bin(dqkv, m, key_col + j * LANES, d_key)
             put_bin(dqkv, m, value_col + j * LANES, d_value)
 
-    attend_back(0)
-    reduce_step(0, 0)
-    for m in range(1, micro):
+    for m in range(micro):
         attend_back(m)
-    reduce_step(0, 1)
+        if m == 1:
+            reduce(0, 1)
 
     away = mm(dqkv[other], weights(0, 3 * heads_wide), NT)
     last_send[...] = away.astype(LOW)
     copy = pair_copy(last_send, last_land, 7)
     copy.start()
     grad_columns(xs_flipped[...], dqkv, 0, 3 * heads_wide, 0)
-    reduce_start(2)
+    reduce(3)
     own_part[...] = mm(dqkv[half], weights(0, 3 * heads_wide), NT)
     copy.wait()
 
@@ -784,7 +891,9 @@
         return carry
 
     lax.fori_loop(0, chunks, leave, 0)
-    push(gx_send, gx_land, gx_sems)
+    push(gx_send, gx_land, gx_sems, False)
+    push(gx_send, gx_land, gx_sems, True)
+    reduce(0, 1)
     for i, start in enumerate((0, value_col)):
         columns = slice(start, start + heads_wide)
         vecg_buf[0, 8:9, i * heads_wide : (i + 1) * heads_wide] = (
@@ -796,38 +905,44 @@
     swap_v.start()
     swap_v.wait()
     vecg_buf[0, 0:6, :] = vecg_buf[0, 0:6, :] + vec_pair[0:6, :]
+
+    def hand_back(land_ref, result_ref, hbm_ref):
+        def one(i, carry):
+            result_ref[i] = land_ref[target_ref[i], i // dp_count]
+            return carry
+
+        lax.fori_loop(0, blocks, one, 0)
+        copy_out(result_ref, hbm_ref)
+
     begin, fold = swing(vecg_buf, vecg_land, vecg_sems, 0, vec_out_ref)
     begin()
-    reduce_step(1, 0)
-    reduce_step(0, 2)
+    reduce(2)
     fold()
     begin, fold = swing(vecg_buf, vecg_land, vecg_sems, 1, vec_out_ref)
     begin()
-    reduce_step(1, 1)
-    reduce_step(0, 3)
+    settle(out_send, out_land, out_sems)
+    hand_back(out_land, layer_out_ref, layer_out_hbm)
+    reduce(1, 0)
+    reduce(2)
     fold()
-    for stage in range(2, stages):
-        begin, fold = swing(vecg_buf, vecg_land, vecg_sems, stage, vec_out_ref)
-        begin()
-        fold()
-    reduce_step(2, 0)
-    reduce_step(1, 2)
-    reduce_step(2, 1)
-    reduce_step(1, 3)
-    settle(out_send, out_land, out_sems)
-
-    def hand_back(land_ref, result_ref):
-        def one(i, carry):
-            result_ref[i] = land_ref[route_ref[i] // blocks, i // dp_count]
-            return carry
-
-        lax.fori_loop(0, blocks, one, 0)
-
-    hand_back(out_land, layer_out_ref)
-    reduce_step(2, 2)
+    begin, fold = swing(vecg_buf, vecg_land, vecg_sems, 2, vec_out_ref)
+    begin()
+    reduce(1, 0)
+    reduce(3)
+    fold()
+    begin, fold = swing(vecg_buf, vecg_land, vecg_sems, 3, vec_out_ref)
+    begin()
+    reduce(2)
+    reduce(3)
+    reduce(2)
+    fold()
+    reduce(3)
     settle(gx_send, gx_land, gx_sems)
-    hand_back(gx_land, grad_tokens_ref)
-    reduce_step(2, 3)
+    hand_back(gx_land, grad_tokens_ref, grad_tokens_hbm)
+    reduce(3)
+    for copy in leaving:
+        copy.wait()
+    assert all(n == stages + 1 for n in (*gone.values(), *sent.values()))
     for gather in gathers:
         for stage in range(stages):
             gather.copy(stage).wait_send()
@@ -836,13 +951,75 @@
             scatter.copy(stage).wait_send()
 
 
-def plan_of(cuts):
-    plan = []
-    for group, (start, stop) in enumerate(cuts):
-        middle = start + (stop - start + LANES) // (2 * LANES) * LANES
-        plan.append((group, 0, start, middle - start))
-        plan.append((group, 1, middle, stop - middle))
-    return plan
+def finish(*refs):
+    sources, total_ref, targets = refs[:8], refs[8], refs[9:17]
+    own_ref, inner_ref, query_ref, value_ref, *held, sems = refs[17:]
+    loads = [pltpu.make_async_copy(src, hold, sems.at[0, i]) for i, (src, hold) in enumerate(zip(sources, held))]
+    stores = [pltpu.make_async_copy(hold, dst, sems.at[1, i]) for i, (hold, dst) in enumerate(zip(held, targets))]
+    for load in loads:
+        load.start()
+    for load, store in zip(loads, stores):
+        load.wait()
+        store.start()
+    place = lax.axis_index("dp")
+
+    def cut(row, size):
+        extent = row.shape[1]
+        source = lax.broadcasted_iota(jnp.int32, (extent, size), 0)
+        at = lax.broadcasted_iota(jnp.int32, (extent, size), 1) + place * size
+        return lax.dot_general(
+            row,
+            (source == at).astype(F32),
+            NN,
+            precision=lax.Precision.HIGHEST,
+            preferred_element_type=F32,
+        )
+
+    own_ref[...] = cut(total_ref[0:8, :], own_ref.shape[1])
+    width, heads_wide = total_ref.shape[1], query_ref.shape[1]
+    rows = inner_ref.shape[1] * lax.axis_size("dp") // width
+    long = jnp.concatenate([total_ref[6 + i : 7 + i, :] for i in range(rows)], axis=1)
+    inner_ref[...] = cut(jnp.broadcast_to(long, (8, long.shape[1])), inner_ref.shape[1])[0:1, :]
+    query_ref[...] = total_ref[8:9, :heads_wide]
+    value_ref[...] = total_ref[8:9, heads_wide:]
+    for store in stores:
+        store.wait()
+
+
+def plans(dp_count, heads_wide, ff):
+    bits = bits_of(dp_count)
+    far, near = bits[:-2], bits[-2:]
+    far_first = (far + near, far + near[::-1])
+    near_first = (near[::-1] + far, near + far)
+    inner_col, outer_col = 4 * heads_wide, 4 * heads_wide + ff
+
+    def plan_of(cuts):
+        plan = []
+        for group, (orders, start, stop) in enumerate(cuts):
+            middle = start + (stop - start + LANES) // (2 * LANES) * LANES
+            plan.append((group, orders[0], start, middle - start))
+            plan.append((group, orders[1], middle, stop - middle))
+        return plan
+
+    gather = plan_of(
+        [
+            (far_first, 0, 3 * heads_wide),
+            (far_first, 3 * heads_wide, inner_col + ff // 2),
+            (far_first, inner_col + ff // 2, outer_col),
+            (far_first, outer_col, outer_col + ff // 2),
+            (near_first, outer_col + ff // 2, outer_col + ff),
+        ]
+    )
+    back = lambda orders: (orders[0][::-1], orders[1][::-1])
+    scatter = plan_of(
+        [
+            (back(far_first), outer_col, outer_col + ff // 2),
+            (back(near_first), outer_col + ff // 2, outer_col + ff),
+            (back(far_first), 3 * heads_wide, outer_col),
+            (back(far_first), 0, 3 * heads_wide),
+        ]
+    )
+    return gather, scatter
 
 
 def shards_fast(
@@ -875,34 +1052,21 @@
     columns = 4 * heads_wide + 2 * ff
     stages = dp_count.bit_length() - 1
     bits = (2,) * stages
-    target = block_route.reshape(micro, dp_count) // blocks
-    inverse = jnp.argmax(
-        target[:, None, :] == jnp.arange(dp_count, dtype=jnp.int32)[None, :, None], axis=2
-    ).astype(jnp.int32)
-    nothing = jnp.zeros((1, own_width), F32)
-    small = jnp.concatenate(
-        [v.astype(F32)[None] for v in (b_out, gain_attn, shift_attn, b_outer, gain_ffn, shift_ffn, block_route)]
-        + [nothing],
-        axis=0,
-    )
     inner_col, outer_col = 4 * heads_wide, 4 * heads_wide + ff
-    third = inner_col + ff // 2
-    gather_plan = plan_of(
-        [
-            (0, 3 * heads_wide),
-            (3 * heads_wide, third),
-            (third, outer_col),
-            (outer_col, outer_col + ff // 2),
-            (outer_col + ff // 2, columns),
-        ]
-    )
-    scatter_plan = plan_of([(outer_col, columns), (3 * heads_wide, outer_col), (0, 3 * heads_wide)])
+    gather_plan, scatter_plan = plans(dp_count, heads_wide, ff)
     bin_half = dp_count * rows
     tall = micro * bin_half
     vmem, smem = pl.BlockSpec(memory_space=pltpu.VMEM), pl.BlockSpec(memory_space=pltpu.SMEM)
     dma = pltpu.SemaphoreType.DMA
     swap_shape = (dp_count, micro, rows, width)
     scratch = [
+        pltpu.SMEM((micro, dp_count), jnp.int32),
+        pltpu.SMEM((blocks,), jnp.int32),
+        pltpu.VMEM(tokens.shape, LOW),
+        pltpu.VMEM(tokens.shape, LOW),
+        pltpu.VMEM(tokens.shape, LOW),
+        pltpu.VMEM(tokens.shape, LOW),
+        pltpu.VMEM((own_width, columns), F32),
         pltpu.VMEM(bits + (own_width, columns), LOW),
         pltpu.VMEM(bits + (own_width, columns), LOW),
     ]
@@ -919,14 +1083,15 @@
     scratch += [
         pltpu.VMEM((tall, width), F32),
         pltpu.VMEM((tall, LANES), F32),
+        pltpu.VMEM((tall, LANES), F32),
         pltpu.VMEM((tall, width), F32),
         pltpu.VMEM((tall, width), F32),
         pltpu.VMEM((tall, width), F32),
         pltpu.VMEM((3, tall, width), F32),
         pltpu.VMEM((tall, width), LOW),
         pltpu.VMEM((tall, width), LOW),
-        pltpu.VMEM((stages, 16, width), F32),
-        pltpu.VMEM((stages, 16, width), F32),
+        pltpu.VMEM((16, LANES), F32),
+        pltpu.VMEM((dp_count, 16, LANES), F32),
         pltpu.VMEM((16, width), F32),
         pltpu.VMEM((16, width), F32),
         pltpu.VMEM((stages, 16, width), F32),
@@ -942,21 +1107,25 @@
     scratch += [
         dma((2, len(gather_plan), stages)),
         dma((2, len(scatter_plan), stages)),
-        dma((2, stages)),
+        dma((2, dp_count)),
         dma((2, stages)),
         dma((2, 9)),
+        dma((8,)),
+        dma((32,)),
     ]
     sizes = (dp_count, micro, rows, width, heads_wide, ff)
-    layer_out, grad_tokens, sums, total = pl.pallas_call(
+    hbm = pl.BlockSpec(memory_space=pl.ANY)
+    grad_shapes = [jax.ShapeDtypeStruct((own_width, size), F32) for size in (heads_wide,) * 4 + (ff,) * 2]
+    made = (
+        jax.ShapeDtypeStruct(tokens.shape, tokens.dtype),
+        jax.ShapeDtypeStruct(tokens.shape, tokens.dtype),
+        *grad_shapes,
+    )
+    *big, total = pl.pallas_call(
         partial(layer, sizes, gather_plan, scatter_plan),
-        out_shape=(
-            jax.ShapeDtypeStruct(tokens.shape, tokens.dtype),
-            jax.ShapeDtypeStruct(tokens.shape, tokens.dtype),
-            jax.ShapeDtypeStruct((own_width, columns), F32),
-            jax.ShapeDtypeStruct((16, width), F32),
-        ),
-        in_specs=[vmem] * 2 + [smem] * 3 + [vmem] * 10,
-        out_specs=[vmem] * 4,
+        out_shape=(*made, jax.ShapeDtypeStruct((16, width), F32)),
+        in_specs=[hbm] * 2 + [smem] * 2 + [hbm] * 6 + [vmem] * 10,
+        out_specs=[hbm] * 8 + [vmem],
         scratch_shapes=scratch,
         compiler_params=pltpu.CompilerParams(
             collective_id=0, has_side_effects=True, vmem_limit_bytes=VMEM_BYTES
@@ -966,42 +1135,58 @@
         tokens,
         cotangent,
         block_route,
-        inverse,
         lengths,
         w_query,
         w_key,
         w_value,
-        w_out,
+        w_out.T,
         w_inner,
-        w_outer,
-        small,
+        w_outer.T,
+        b_out,
+        gain_attn,
+        shift_attn,
+        b_outer,
+        gain_ffn,
+        shift_ffn,
+        block_route,
         b_query,
         b_value,
         b_inner,
     )
     own_inner = b_inner.shape[1]
-    vec_own = lax.dynamic_slice_in_dim(total[:6], place * own_width, own_width, 1)
-    sum_bias_inner = lax.dynamic_slice_in_dim(
-        total[6:8].reshape(1, ff), place * own_inner, own_inner, 1
-    )
+    *big, own, bias_inner, bias_query, bias_value = pl.pallas_call(
+        finish,
+        out_shape=(
+            *made,
+            jax.ShapeDtypeStruct((8, own_width), F32),
+            jax.ShapeDtypeStruct((1, own_inner), F32),
+            jax.ShapeDtypeStruct((1, heads_wide), F32),
+            jax.ShapeDtypeStruct((1, heads_wide), F32),
+        ),
+        in_specs=[hbm] * 8 + [vmem],
+        out_specs=[hbm] * 8 + [vmem] * 4,
+        scratch_shapes=[pltpu.VMEM(result.shape, result.dtype) for result in made] + [dma((2, 8))],
+        name="finish",
+    )(*big, total)
+    layer_out, grad_tokens, gq, gk, gv, go, gi, gu = big
     return (
         layer_out,
         grad_tokens,
-        sums[:, :heads_wide],
-        sums[:, heads_wide : 2 * heads_wide],
-        sums[:, 2 * heads_wide : 3 * heads_wide],
-        total[8:9, :heads_wide],
-        total[8:9, heads_wide:],
-        sums[:, 3 * heads_wide : 4 * heads_wide].T,
-        vec_own[0],
-        vec_own[1],
-        vec_own[2],
-        sums[:, inner_col:outer_col],
-        sum_bias_inner,
-        sums[:, outer_col:].T,
-        vec_own[3],
-        vec_own[4],
-        vec_own[5],
+        gq,
+        gk,
+        gv,
+        bias_query,
+        bias_value,
+        go.T,
+        own[0],
+        own[1],
+        own[2],
+        gi,
+        bias_inner,
+        gu.T,
+        own[3],
+        own[4],
+        own[5],
     )
 
 

time: 242 us -> 189 us (0.78)
  Pallas kernels: 224 us -> 186 us
  local copies, waits for them, and re-layouts: 13 us -> 1.2 us
  other arithmetic: 4.25 us -> 0 us
    pallas_call x1, Pallas kernels: 224 us -> 183 us  [shards_fast(): pl.pallas_call(partial(layer, sizes, gather_plan, scatter_plan), out_shap...]
    unnamed x12 -> x2, local copies, waits for them, and re-layouts: 5.28 us -> 0.66 us
    pallas_call x0 -> x1, Pallas kernels: none -> 3.89 us  [shards_fast(): pl.pallas_call(finish, out_shape=(*made, jax.ShapeDtypeStruct((8, own_wid...]
    transpose x2 -> x0, local copies, waits for them, and re-layouts: 3.67 us -> none  [the longest x1 1.96 us: shards_fast(): sums[:, outer_col:]]
    broadcast_in_dim x4 -> x0, other arithmetic: 2.76 us -> none  [shards_fast(): v.astype(F32)[None]]
where the time goes in v3:
time: 189 us; the launch traced here: 188 us
  Pallas kernels  186 us (98%)
    pallas_call x1, Pallas kernels, shards_fast(): pl.pallas_call(partial(layer, sizes, gather_plan, scatter_plan), out_shap...  183 us
    pallas_call x1, Pallas kernels, shards_fast(): pl.pallas_call(finish, out_shape=(*made, jax.ShapeDtypeStruct((8, own_wid...  3.89 us

profile of v3, /device:TPU:0, one launch (start us, length us, event | category | flops | bytes accessed | tf_op | source)
XLA Modules:
  0.0 188.3 jit_solution(1066257295153787435)
XLA Ops:
  0.7 182.5 %layer.1 = (bf16[48,8,768]{2,1,0:T(8,128)(2,1)}, bf16[48,8,768]{2,1,0:T(8,128)(2,1)}, f32[48,384]{1,0:T(8,128)}, f32[48,384]{1,0:T(8,128)}, f32[48,384]{1,0:T(8,...) custom-call(bf16[48,8,768]{2,1,0:T(8,128)(2,1)} %refs_0_.1, ...), custom_call_target="tpu_custom_call" | custom-call | tf_op jit(solution)/shard_map/layer/pallas_call | solution.py:1124
  183.2 3.9 %finish.1 = (bf16[48,8,768]{2,1,0:T(8,128)(2,1)}, bf16[48,8,768]{2,1,0:T(8,128)(2,1)}, f32[48,384]{1,0:T(8,128)}, f32[48,384]{1,0:T(8,128)}, f32[48,384]{1,0:T(8...) custom-call(bf16[48,8,768]{2,1,0:T(8,128)(2,1)} %get-tuple-element.3, ...), custom_call_target="tpu_custom_call" | custom-call | tf_op jit(solution)/shard_map/finish/pallas_call | solution.py:1157
  187.1 0.0 copy-start
  187.1 0.7 copy-done
  187.8 0.5 slice_bitcast_fusion
Async XLA Ops:
  187.1 0.7 copy-start

commit v4 on v3

--- a/solution.py
+++ b/solution.py
@@ -92,6 +92,173 @@
 NN = (((1,), (0,)), ((), ()))
 F32 = jnp.float32
 LOW = jnp.bfloat16
+FAR_FIRST, NEAR_FIRST = range(2)
+X, DY, OUT, GX = range(4)
+(
+    GATHER,
+    REDUCE,
+    NEAR,
+    FAR,
+    VECTORS,
+    FIND_SLOTS,
+    SEND_PIECES,
+    ARRANGE_TOKENS,
+    ARRANGE_COTANGENT,
+    WHOLE_VECTORS,
+    MASK_BINS,
+    TAKE_TOKENS,
+    PROJECT_HEADS,
+    ATTEND_THIRD,
+    ATTEND_BACK_THIRD,
+    PROJECT_OUT,
+    NORM_AFTER_ATTENTION,
+    WIDEN_TOKENS,
+    NARROW_TOKENS,
+    NORM_AFTER_FFN,
+    NORM_FFN_BACKWARD,
+    GRAD_OUTER,
+    FFN_BACKWARD,
+    GRAD_INNER,
+    GRAD_OUT,
+    HEADS_BACKWARD,
+    INPUT_AWAY,
+    GRAD_HEADS,
+    INPUT_BACKWARD,
+    PAIR_VECTORS,
+    TAKE_OUTPUT,
+    TAKE_INPUT_GRAD,
+) = range(32)
+
+GATHERS = (
+    (FAR_FIRST, 0, 3),
+    (FAR_FIRST, 3, 6),
+    (FAR_FIRST, 9, 7),
+    (FAR_FIRST, 16, 8),
+    (FAR_FIRST, 24, 4),
+    (NEAR_FIRST, 28, 4),
+    (NEAR_FIRST, 32, 4),
+)
+SCATTERS = (
+    (FAR_FIRST, 24, 4),
+    (NEAR_FIRST, 28, 8),
+    (FAR_FIRST, 12, 12),
+    (FAR_FIRST, 9, 3),
+    (FAR_FIRST, 0, 5),
+    (FAR_FIRST, 5, 4),
+)
+SCHEDULE = (
+    (GATHER, 1),
+    (GATHER, 5),
+    (GATHER, 2),
+    (SEND_PIECES,),
+    (GATHER, 6),
+    (GATHER, 0),
+    (FIND_SLOTS,),
+    (ARRANGE_TOKENS,),
+    (GATHER, 5),
+    (NEAR, X),
+    (ARRANGE_COTANGENT,),
+    (GATHER, 1),
+    (GATHER, 0),
+    (GATHER, 6),
+    (GATHER, 2),
+    (FAR, X),
+    (GATHER, 3),
+    (GATHER, 4),
+    (GATHER, 1),
+    (GATHER, 0),
+    (WHOLE_VECTORS,),
+    (GATHER, 0),
+    (GATHER, 2),
+    (GATHER, 3),
+    (GATHER, 4),
+    (GATHER, 5),
+    (GATHER, 1),
+    (MASK_BINS,),
+    (GATHER, 6),
+    (GATHER, 2),
+    (TAKE_TOKENS,),
+    (GATHER, 0),
+    (GATHER, 5),
+    (GATHER, 3),
+    (GATHER, 1),
+    (PROJECT_HEADS,),
+    (NEAR, DY),
+    (ATTEND_THIRD, 0),
+    (GATHER, 2),
+    (GATHER, 6),
+    (ATTEND_THIRD, 1),
+    (GATHER, 4),
+    (ATTEND_THIRD, 2),
+    (PROJECT_OUT,),
+    (GATHER, 3),
+    (GATHER, 4),
+    (GATHER, 6),
+    (FAR, DY),
+    (NORM_AFTER_ATTENTION,),
+    (GATHER, 3),
+    (GATHER, 5),
+    (WIDEN_TOKENS,),
+    (GATHER, 4),
+    (NARROW_TOKENS,),
+    (NORM_AFTER_FFN,),
+    (NEAR, OUT),
+    (FAR, OUT),
+    (NORM_FFN_BACKWARD,),
+    (GRAD_OUTER, 0),
+    (GRAD_OUTER, 1),
+    (REDUCE, 0),
+    (REDUCE, 1),
+    (FFN_BACKWARD,),
+    (GRAD_INNER,),
+    (REDUCE, 2),
+    (TAKE_OUTPUT,),
+    (GRAD_OUT,),
+    (HEADS_BACKWARD,),
+    (ATTEND_BACK_THIRD, 0),
+    (ATTEND_BACK_THIRD, 1),
+    (ATTEND_BACK_THIRD, 2),
+    (REDUCE, 0),
+    (REDUCE, 1),
+    (INPUT_AWAY,),
+    (REDUCE, 2),
+    (REDUCE, 3),
+    (GRAD_HEADS,),
+    (REDUCE, 5),
+    (REDUCE, 4),
+    (REDUCE, 0),
+    (REDUCE, 2),
+    (REDUCE, 0),
+    (REDUCE, 5),
+    (INPUT_BACKWARD,),
+    (REDUCE, 2),
+    (REDUCE, 1),
+    (PAIR_VECTORS,),
+    (NEAR, GX),
+    (REDUCE, 5),
+    (REDUCE, 3),
+    (REDUCE, 4),
+    (VECTORS,),
+    (FAR, GX),
+    (VECTORS,),
+    (REDUCE, 4),
+    (VECTORS,),
+    (REDUCE, 2),
+    (REDUCE, 3),
+    (REDUCE, 5),
+    (REDUCE, 1),
+    (VECTORS,),
+    (REDUCE, 0),
+    (REDUCE, 4),
+    (REDUCE, 3),
+    (TAKE_INPUT_GRAD,),
+    (REDUCE, 1),
+    (REDUCE, 5),
+    (VECTORS,),
+    (REDUCE, 4),
+    (REDUCE, 3),
+)
+
 VMEM_BYTES = 63 << 20
 
 
@@ -281,20 +448,23 @@
         *rest,
     ) = refs[29:]
     stages = dp_count.bit_length() - 1
-    landings = [rest[i * stages : (i + 1) * stages] for i in range(len(scatter_plan))]
+    groups = max(group for group, _, _, _ in scatter_plan) + 1
+    landings = [rest[i * stages : (i + 1) * stages] for i in range(groups)]
     (
         x_sems,
         dy_sems,
         out_sems,
         gx_sems,
-        gather_sems,
-        scatter_sems,
+        gather_sends,
+        gather_recvs,
+        scatter_sends,
+        scatter_recvs,
         vec_sems,
         vecg_sems,
         pair_sems,
         in_sems,
         out_copy_sems,
-    ) = rest[len(scatter_plan) * stages :]
+    ) = rest[groups * stages :]
     place, half = lax.axis_index("dp"), lax.axis_index("tensor")
     other = 1 - half
     bits = bits_of(dp_count)
@@ -326,34 +496,37 @@
     base, within_group = place - lax.rem(place, group), lax.rem(place, group)
     far_base = lax.rem(base + group, dp_count)
 
-    def message(step, sign, send_ref, recv_ref, sems, near):
-        index = step if near else group + step
-        peer = (base if near else far_base) + lax.rem(within_group + group + sign * step, group)
+    def message(step, send_ref, recv_ref, sems, near):
+        peer = (base if near else far_base) + lax.rem(within_group + step, group)
         return pltpu.make_async_remote_copy(
             src_ref=send_ref.at[peer],
-            dst_ref=recv_ref.at[place if sign > 0 else peer],
-            send_sem=sems.at[0, index],
-            recv_sem=sems.at[1, index],
+            dst_ref=recv_ref.at[place],
+            send_sem=sems.at[0],
+            recv_sem=sems.at[1],
             device_id=(peer, half),
             device_id_type=MESH,
         )
 
     def push(send_ref, recv_ref, sems, near):
         def one(step, carry):
-            message(step, 1, send_ref, recv_ref, sems, near).start()
+            message(step, send_ref, recv_ref, sems, near).start()
             return carry
 
         lax.fori_loop(1 if near else 0, group, one, 0)
 
     def settle(send_ref, recv_ref, sems):
         recv_ref[place] = send_ref[place]
-        for near in (True, False):
-
-            def one(step, carry):
-                message(step, -1, send_ref, recv_ref, sems, near).wait()
-                return carry
-
-            lax.fori_loop(1 if near else 0, group, one, 0)
+        whole = pl.ds(0, dp_count - 1)
+        every = pltpu.make_async_remote_copy(
+            src_ref=send_ref.at[whole],
+            dst_ref=recv_ref.at[whole],
+            send_sem=sems.at[0],
+            recv_sem=sems.at[1],
+            device_id=(place, other),
+            device_id_type=MESH,
+        )
+        every.wait_recv()
+        every.wait_send()
 
     def arrange(src_ref, dst_ref):
         def one(i, carry):
@@ -435,24 +608,40 @@
             full,
             start,
             size,
-            gather_sems.at[0, i],
-            gather_sems.at[1, i],
-        )
-        for i, (group, order, start, size) in enumerate(gather_plan)
+            gather_sends,
+            gather_recvs.at[i],
+        )
+        for i, (_, order, start, size) in enumerate(gather_plan)
     ]
     gone = {}
+
+    def extent(plan, wanted):
+        own_plan = [(start, start + size) for group, _, start, size in plan if group == wanted]
+        start, stop = min(own_plan)[0], max(own_plan)[1]
+        return pl.ds(start, stop - start)
+
+    def shards_copy(ref, dropped, cols, send_sem, recv_sem):
+        view = ref.at[(0,) * dropped + (slice(None),) * (stages - dropped + 1) + (cols,)]
+        return pltpu.make_async_remote_copy(
+            src_ref=view,
+            dst_ref=view,
+            send_sem=send_sem,
+            recv_sem=recv_sem,
+            device_id=(place, other),
+            device_id_type=MESH,
+        )
 
     def advance(*groups):
         for wanted in groups:
             stage = gone.get(wanted, 0)
+            if stage > stages:
+                continue
             gone[wanted] = stage + 1
-            for (group, _, _, _), gather in zip(gather_plan, gathers):
-                if group == wanted:
-                    with jax.named_scope(f"gather_{wanted}_{stage}"):
-                        if stage > 0:
-                            gather.copy(stage - 1).wait_recv()
-                        if stage < stages:
-                            gather.copy(stage).start()
+            for (member, _, _, _), gather in zip(gather_plan, gathers):
+                if member == wanted and stage > 0:
+                    gather.copy(stage - 1).wait_recv()
+                if member == wanted and stage < stages:
+                    gather.copy(stage).start()
 
     def swing(buf, land, sems, stage, last_ref):
         copy = pltpu.make_async_remote_copy(
@@ -479,128 +668,60 @@
         pltpu.make_async_remote_copy(
             src_ref=piece,
             dst_ref=pieces.at[place],
-            send_sem=vec_sems.at[0, step],
-            recv_sem=vec_sems.at[1, step],
+            send_sem=vec_sems.at[0],
+            recv_sem=vec_sems.at[1],
             device_id=(peer, half),
             device_id_type=MESH,
         ).start()
         return carry
 
-    def wait_piece(step, carry):
-        source = lax.rem(place + dp_count - step, dp_count)
-        pltpu.make_async_remote_copy(
-            src_ref=piece,
-            dst_ref=pieces.at[source],
-            send_sem=vec_sems.at[0, step],
-            recv_sem=vec_sems.at[1, step],
-            device_id=(source, half),
-            device_id_type=MESH,
-        ).wait()
-        return carry
-
-    advance(0, 4)
-    lax.fori_loop(1, dp_count, push_piece, 0)
-    advance(1)
-    lax.fori_loop(0, blocks, find_target, 0)
-    lax.fori_loop(0, blocks, invert, 0)
-    fetches[6].wait()
-    arrange(tokens_in, x_send)
-    push(x_send, x_land, x_sems, True)
-    advance(4)
-    fetches[7].wait()
-    arrange(cot_in, dy_send)
-    advance(0)
-    push(x_send, x_land, x_sems, False)
-    pieces[place] = piece[...]
-    lax.fori_loop(1, dp_count, wait_piece, 0)
-
-    def lay(source, total):
-        block = pieces[source]
-
-        def laid(block, size, extent):
-            target = lax.broadcasted_iota(jnp.int32, (LANES, extent), 1)
-            at = lax.broadcasted_iota(jnp.int32, (LANES, extent), 0)
-            hit = (target == at + source * size) & (at < size)
-            return mm(block.astype(LOW), hit.astype(F32).astype(LOW))
-
-        return (
-            total[0] + laid(block[0:8], own_width, width),
-            total[1] + laid(block[8:16], bi_ref.shape[1], ff),
-        )
-
-    short, long = lax.fori_loop(
-        0, dp_count, lay, (jnp.zeros((8, width), F32), jnp.zeros((8, ff), F32))
-    )
-    vec[0:8, :] = short
-    for i in range(ff // width):
-        vec[8 + i : 9 + i, :] = long[0:1, i * width : (i + 1) * width]
-
-    placed = jnp.where(vec[6:7, :] == place.astype(F32), vec[7:8, :], 0.0)
-    placed_rows = jnp.broadcast_to(placed, (8, blocks * dp_count))
-
-    def mask_bin(m, carry):
-        shape = (2 * bin_half, blocks * dp_count)
-        row = lax.broadcasted_iota(jnp.int32, shape, 0)
-        lane = lax.broadcasted_iota(jnp.int32, shape, 1)
-        source = lax.rem(row, bin_half) // rows
-        chosen = (lane // dp_count) == source * micro + m
-        tall_place = jnp.sum(jnp.where(chosen, placed, 0.0), axis=1, keepdims=True)
-        wide_place = mm(placed_rows, chosen.astype(F32), NT)[0:1, :]
-        ends, end = [], 0
-        for i in range(lengths_ref.shape[1] - 1):
-            end = end + lengths_ref[m, i]
-            ends.append(end.astype(F32))
-
-        def sequence(at, index):
-            within = (lax.rem(index, rows) + (index // bin_half) * rows).astype(F32)
-            position = at * block_len + within
-            return sum((position >= end).astype(F32) for end in ends)
-
-        down = sequence(
-            tall_place, lax.broadcasted_iota(jnp.int32, (2 * bin_half, 1), 0)
-        )
-        across = sequence(
-            wide_place, lax.broadcasted_iota(jnp.int32, (1, 2 * bin_half), 1)
-        )
-        bias[m] = jnp.where(down == across, 0.0, -1e30)
-        return carry
-
-    lax.fori_loop(0, micro, mask_bin, 0)
-
-    advance(0, 1)
-    advance(2)
-    advance(0, 1)
-    advance(3)
-    advance(1)
-    advance(0)
-    advance(2)
-    settle(x_send, x_land, x_sems)
-
-    def order_rows(m, carry):
-        block = x_land[:, m].astype(F32).reshape(bin_half, width)
-        xs[half, pl.ds(pl.multiple_of(m * bin_half, bin_half), bin_half), :] = block.astype(LOW)
-        return carry
-
-    lax.fori_loop(0, micro, order_rows, 0)
-    swap_x = pair_copy(xs.at[half], xs.at[half], 0)
-    swap_x.start()
-    advance(3, 4)
-    swap_x.wait()
-
-    def project(i, carry):
-        h = lax.rem(half + i, 2)
-        own_rows = xs[h]
-        qkv[h, :, pl.ds(0, heads_wide)] = (
-            (mm(own_rows, weights(0, heads_wide)) + bq_ref[...].astype(F32)).astype(LOW)
-            * LOW(HD ** (-0.5))
-        )
-        qkv[h, :, pl.ds(key_col, heads_wide)] = mm(own_rows, weights(key_col, heads_wide)).astype(LOW)
-        qkv[h, :, pl.ds(value_col, heads_wide)] = (
-            mm(own_rows, weights(value_col, heads_wide)) + bv_ref[...].astype(F32)
-        ).astype(LOW)
-        return carry
-
-    lax.fori_loop(0, 2, project, 0)
+    bits_shape = (2,) * stages
+    scatters = [
+        Scatter(
+            dp_count,
+            place,
+            half,
+            order,
+            grads,
+            start,
+            size,
+            [
+                land.at[
+                    (slice(None),) * (stages - stage)
+                    + (pl.ds(start - extent(scatter_plan, group).start, size),)
+                ]
+                for stage, land in enumerate(landings[group])
+            ],
+            scatter_sends,
+            scatter_recvs.at[i],
+        )
+        for i, (group, order, start, size) in enumerate(scatter_plan)
+    ]
+    sent = {}
+
+    def reduce(*wanted_groups):
+        for wanted in wanted_groups:
+            stage = sent.get(wanted, 0)
+            if stage > stages:
+                continue
+            sent[wanted] = stage + 1
+            for (group, _, _, _), scatter in zip(scatter_plan, scatters):
+                if group == wanted:
+                    if stage > 0:
+                        scatter.copy(stage - 1).wait_recv()
+                    if 0 < stage < stages:
+                        scatter.add(stage - 1)
+                    elif stage == stages:
+                        scatter.finish(stage - 1, outs)
+                    if stage < stages:
+                        scatter.copy(stage).start()
+
+    def grad_columns(left_t, right_ref, start, columns, grads_start, tile=tile):
+        for i in range(columns // tile):
+            piece = mm(left_t, right_ref[:, :, start + i * tile : start + (i + 1) * tile].reshape(2 * tall, tile))
+            grads[(slice(None),) * (stages + 1) + (pl.ds(grads_start + i * tile, tile),)] = piece.astype(
+                LOW
+            ).reshape(bits_shape + (own_width, tile))
 
     low_lane = lax.broadcasted_iota(jnp.int32, (2 * bin_half, LANES), 1) < HD
     nothing = jnp.zeros((2 * bin_half, LANES), LOW)
@@ -632,15 +753,6 @@
                 total = part if total is None else total + part
             put_bin(attn, m, j * LANES, total)
 
-    for m in range(micro):
-        attend(m)
-        if m == 0:
-            advance(2, 1)
-        if m == 1:
-            advance(3)
-        if m == 2:
-            advance(4, 2)
-            push(dy_send, dy_land, dy_sems, False)
     def two_halves(left_ref, columns, start, send_ref, which, land_ref):
         away = mm(left_ref[other], weights(start, columns), NT)
         send_ref[...] = away.astype(send_ref.dtype)
@@ -649,8 +761,6 @@
         own_part[...] = mm(left_ref[half], weights(start, columns), NT)
         return copy
 
-
-    copy = two_halves(attn, heads_wide, out_col, part_send, 1, part_land.at[0])
     chunk = 4 * rows
     per_bin = bin_half // chunk
     chunks = tall // chunk
@@ -659,191 +769,127 @@
     def mean_of(v):
         return jnp.sum(v, axis=1, keepdims=True) * (1.0 / width)
 
-    copy.wait()
-
-    def norm_attn(i, carry):
-        at = pl.ds(pl.multiple_of(i * chunk, chunk), chunk)
-        mid = xs[half, at, :].astype(F32) + (own_part[at, :] + part_land[0, at, :]) + vec[0:1, :]
-        centre = mid - mean_of(mid)
-        inverse_s = lax.rsqrt(mean_of(centre * centre) + EPS_NORM)
-        unit = centre * inverse_s
-        normed[at, :] = unit
-        spread[at, :] = jnp.broadcast_to(inverse_s, (chunk, LANES))
-        hs[half, at, :] = (unit * vec[1:2, :] + vec[2:3, :]).astype(LOW)
-        return carry
-
-    lax.fori_loop(0, chunks, norm_attn, 0)
-    swap_h = pair_copy(hs.at[half], hs.at[half], 2)
-    swap_h.start()
-    advance(2, 3)
-    push(dy_send, dy_land, dy_sems, True)
-
-    def widen(h):
-        for i in range(ff // tile):
-            start = i * tile
-            row = 8 + start // width
-            inner = mm(hs[h], weights(inner_col + start, tile)) + vec[
-                row : row + 1, start % width : start % width + tile
-            ]
-            cdf = 0.5 * (1.0 + lax.erf(inner * (0.5**0.5)))
-            density = jnp.exp(-0.5 * inner * inner) * ((2.0 * math.pi) ** -0.5)
-            gelu_low[h, :, start : start + tile] = (inner * cdf).astype(LOW)
-            dgelu[h, :, start : start + tile] = (cdf + inner * density).astype(dgelu.dtype)
-
-    def widen_step(i, carry):
-        @pl.when(i == 1)
-        def _():
-            swap_h.wait()
-
-        widen(lax.rem(half + i, 2))
-        return carry
-
-    lax.fori_loop(0, 2, widen_step, 0)
-    xs_flipped[...] = xs[...].reshape(2 * tall, width).T
-    hs_flipped[...] = hs[...].reshape(2 * tall, width).T
-    advance(3, 4)
-    copy = two_halves(gelu_low, ff, outer_col, part_send, 3, part_land.at[1])
-    copy.wait()
-
     def fold_rows(v):
         return jnp.sum(v.reshape(chunk // 8, 8, width), axis=0)
 
-    def norm_ffn(i, carry):
-        at = pl.ds(pl.multiple_of(i * chunk, chunk), chunk)
-        m, quarter = i // per_bin, lax.rem(i, per_bin)
-        sources = pl.ds(quarter * (chunk // rows), chunk // rows)
-        hidden = normed[at, :] * vec[1:2, :] + vec[2:3, :]
-        top = hidden + (own_part[at, :] + part_land[1, at, :]) + vec[3:4, :]
-        centre = top - mean_of(top)
-        inverse_s = lax.rsqrt(mean_of(centre * centre) + EPS_NORM)
-        unit = centre * inverse_s
-        own_part[at, :] = unit
-        spread_ffn[at, :] = jnp.broadcast_to(inverse_s, (chunk, LANES))
-        result = unit * vec[4:5, :] + vec[5:6, :]
-        out_send[sources, m] = result.reshape(chunk // rows, rows, width).astype(LOW)
-        return carry
-
-    lax.fori_loop(0, chunks, norm_ffn, 0)
-    push(out_send, out_land, out_sems, False)
-    push(out_send, out_land, out_sems, True)
-    settle(dy_send, dy_land, dy_sems)
-    for i in range(3):
-        vec_acc[i] = jnp.zeros((8, width), F32)
-
-    def norm_ffn_back(i, carry):
-        at = pl.ds(pl.multiple_of(i * chunk, chunk), chunk)
-        m, quarter = i // per_bin, lax.rem(i, per_bin)
-        sources = pl.ds(quarter * (chunk // rows), chunk // rows)
-        unit = own_part[at, :]
-        dy = dy_land[sources, m].astype(F32).reshape(chunk, width)
-        vec_acc[0] = vec_acc[0] + fold_rows(dy * unit)
-        vec_acc[1] = vec_acc[1] + fold_rows(dy)
-        scaled = dy * vec[4:5, :]
-        grad_top = (scaled - mean_of(scaled) - unit * mean_of(scaled * unit)) * spread_ffn[at, 0:1]
-        grad_keep[at, :] = grad_top
-        gs[half, at, :] = grad_top.astype(LOW)
-        return carry
-
-    lax.fori_loop(0, chunks, norm_ffn_back, 0)
-    swap_g = pair_copy(gs.at[half], gs.at[half], 4)
-    swap_g.start()
-    vecg_buf[0, 4:5, :] = jnp.sum(vec_acc[0], axis=0, keepdims=True)
-    vecg_buf[0, 5:6, :] = jnp.sum(vec_acc[1], axis=0, keepdims=True)
-    vecg_buf[0, 3:4, :] = mm(ones, gs[half])[0:1, :]
-
-    def narrow(h):
-        for i in range(ff // tile):
-            start = i * tile
-            grad = mm(gs[h], weights(outer_col + start, tile)) * dgelu[h, :, start : start + tile].astype(F32)
-            ginner[h, :, start : start + tile] = grad.astype(LOW)
-
-    narrow(half)
-    swap_g.wait()
-
-    scatters = [
-        Scatter(
-            dp_count,
-            place,
-            half,
-            order,
-            grads,
-            start,
-            size,
-            landings[i],
-            scatter_sems.at[0, i],
-            scatter_sems.at[1, i],
-        )
-        for i, (group, order, start, size) in enumerate(scatter_plan)
-    ]
-    sent = {}
-
-    def reduce(*groups):
-        for wanted in groups:
-            stage = sent.get(wanted, 0)
-            sent[wanted] = stage + 1
-            for (group, _, _, _), scatter in zip(scatter_plan, scatters):
-                if group == wanted:
-                    with jax.named_scope(f"reduce_{wanted}_{stage}"):
-                        if stage > 0:
-                            scatter.copy(stage - 1).wait_recv()
-                            if stage < stages:
-                                scatter.add(stage - 1)
-                            else:
-                                scatter.finish(stage - 1, outs)
-                        if stage < stages:
-                            scatter.copy(stage).start()
-
-    def grad_columns(left_t, right_ref, start, columns, grads_start):
-        for i in range(columns // tile):
-            piece = mm(left_t, right_ref[:, :, start + i * tile : start + (i + 1) * tile].reshape(2 * tall, tile))
-            grads[(slice(None),) * (stages + 1) + (pl.ds(grads_start + i * tile, tile),)] = piece.astype(
-                LOW
-            ).reshape(bits_shape + (own_width, tile))
-
-    bits_shape = (2,) * stages
-    flipped[...] = gs[...].reshape(2 * tall, width).T
-    grad_columns(flipped[...], gelu_low, 0, ff // 2, outer_col)
-    reduce(0)
-    grad_columns(flipped[...], gelu_low, ff // 2, ff // 2, outer_col + ff // 2)
-    reduce(1)
-    narrow(other)
-    copy = two_halves(ginner, ff, inner_col, part_send, 5, part_land.at[2])
-    for i in range(ff // width):
-        columns = slice(i * width, (i + 1) * width)
-        vecg_buf[0, 6 + i : 7 + i, :] = (mm(ones, ginner[0, :, columns]) + mm(ones, ginner[1, :, columns]))[0:1, :]
-    copy.wait()
-    for i in range(3):
-        vec_acc[i] = jnp.zeros((8, width), F32)
-
-    def norm_back(i, carry):
-        at = pl.ds(pl.multiple_of(i * chunk, chunk), chunk)
-        grad_hidden = grad_keep[at, :] + (own_part[at, :] + part_land[2, at, :])
-        unit = normed[at, :]
-        vec_acc[0] = vec_acc[0] + fold_rows(grad_hidden * unit)
-        vec_acc[1] = vec_acc[1] + fold_rows(grad_hidden)
-        scaled = grad_hidden * vec[1:2, :]
-        grad_mid = (scaled - mean_of(scaled) - unit * mean_of(scaled * unit)) * spread[at, 0:1]
-        grad_keep[at, :] = grad_mid
-        gb[half, at, :] = grad_mid.astype(LOW)
-        return carry
-
-    lax.fori_loop(0, chunks, norm_back, 0)
-    swap_b = pair_copy(gb.at[half], gb.at[half], 6)
-    swap_b.start()
-    vecg_buf[0, 1:2, :] = jnp.sum(vec_acc[0], axis=0, keepdims=True)
-    vecg_buf[0, 2:3, :] = jnp.sum(vec_acc[1], axis=0, keepdims=True)
-    vecg_buf[0, 0:1, :] = mm(ones, gb[half])[0:1, :]
-    grad_columns(hs_flipped[...], ginner, 0, ff, inner_col)
-    swap_b.wait()
-    flipped[...] = gb[...].reshape(2 * tall, width).T
-    grad_columns(flipped[...], attn, 0, heads_wide, out_col)
-    reduce(2)
-
-    def to_heads(h, carry):
-        gattn[h] = mm(gb[h], weights(out_col, heads_wide)).astype(LOW)
-        return carry
-
-    lax.fori_loop(0, 2, to_heads, 0)
+    def hand_back(land_ref, result_ref, hbm_ref):
+        def one(i, carry):
+            result_ref[i] = land_ref[target_ref[i], i // dp_count]
+            return carry
+
+        lax.fori_loop(0, blocks, one, 0)
+        copy_out(result_ref, hbm_ref)
+
+    def find_slots():
+        lax.fori_loop(0, blocks, find_target, 0)
+        lax.fori_loop(0, blocks, invert, 0)
+
+    def send_pieces():
+        lax.fori_loop(1, dp_count, push_piece, 0)
+
+    def arrange_tokens():
+        fetches[6].wait()
+        arrange(tokens_in, x_send)
+
+    def arrange_cotangent():
+        fetches[7].wait()
+        arrange(cot_in, dy_send)
+
+    def whole_vectors():
+        pieces[place] = piece[...]
+        every_piece = pltpu.make_async_remote_copy(
+            src_ref=pieces.at[pl.ds(0, dp_count - 1)],
+            dst_ref=pieces.at[pl.ds(0, dp_count - 1)],
+            send_sem=vec_sems.at[0],
+            recv_sem=vec_sems.at[1],
+            device_id=(place, other),
+            device_id_type=MESH,
+        )
+        every_piece.wait_recv()
+        every_piece.wait_send()
+
+        def lay(source, total):
+            block = pieces[source]
+
+            def laid(block, size, extent):
+                target = lax.broadcasted_iota(jnp.int32, (LANES, extent), 1)
+                at = lax.broadcasted_iota(jnp.int32, (LANES, extent), 0)
+                hit = (target == at + source * size) & (at < size)
+                return mm(block.astype(LOW), hit.astype(F32).astype(LOW))
+
+            return (
+                total[0] + laid(block[0:8], own_width, width),
+                total[1] + laid(block[8:16], bi_ref.shape[1], ff),
+            )
+
+        short, long = lax.fori_loop(
+            0, dp_count, lay, (jnp.zeros((8, width), F32), jnp.zeros((8, ff), F32))
+        )
+        vec[0:8, :] = short
+        for i in range(ff // width):
+            vec[8 + i : 9 + i, :] = long[0:1, i * width : (i + 1) * width]
+
+    def mask_bins():
+        placed = jnp.where(vec[6:7, :] == place.astype(F32), vec[7:8, :], 0.0)
+        placed_rows = jnp.broadcast_to(placed, (8, blocks * dp_count))
+
+        def mask_bin(m, carry):
+            shape = (2 * bin_half, blocks * dp_count)
+            row = lax.broadcasted_iota(jnp.int32, shape, 0)
+            lane = lax.broadcasted_iota(jnp.int32, shape, 1)
+            source = lax.rem(row, bin_half) // rows
+            chosen = (lane // dp_count) == source * micro + m
+            tall_place = jnp.sum(jnp.where(chosen, placed, 0.0), axis=1, keepdims=True)
+            wide_place = mm(placed_rows, chosen.astype(F32), NT)[0:1, :]
+            ends, end = [], 0
+            for i in range(lengths_ref.shape[1] - 1):
+                end = end + lengths_ref[m, i]
+                ends.append(end.astype(F32))
+
+            def sequence(at, index):
+                within = (lax.rem(index, rows) + (index // bin_half) * rows).astype(F32)
+                position = at * block_len + within
+                return sum((position >= end).astype(F32) for end in ends)
+
+            down = sequence(
+                tall_place, lax.broadcasted_iota(jnp.int32, (2 * bin_half, 1), 0)
+            )
+            across = sequence(
+                wide_place, lax.broadcasted_iota(jnp.int32, (1, 2 * bin_half), 1)
+            )
+            bias[m] = jnp.where(down == across, 0.0, -1e30)
+            return carry
+
+        lax.fori_loop(0, micro, mask_bin, 0)
+
+    def take_tokens():
+        settle(x_send, x_land, x_sems)
+
+        def order_rows(m, carry):
+            block = x_land[:, m].astype(F32).reshape(bin_half, width)
+            xs[half, pl.ds(pl.multiple_of(m * bin_half, bin_half), bin_half), :] = block.astype(LOW)
+            return carry
+
+        lax.fori_loop(0, micro, order_rows, 0)
+        swap_x = pair_copy(xs.at[half], xs.at[half], 0)
+        swap_x.start()
+        swap_x.wait()
+
+    def project_heads():
+        def project(i, carry):
+            h = lax.rem(half + i, 2)
+            own_rows = xs[h]
+            qkv[h, :, pl.ds(0, heads_wide)] = (
+                (mm(own_rows, weights(0, heads_wide)) + bq_ref[...].astype(F32)).astype(LOW)
+                * LOW(HD ** (-0.5))
+            )
+            qkv[h, :, pl.ds(key_col, heads_wide)] = mm(own_rows, weights(key_col, heads_wide)).astype(LOW)
+            qkv[h, :, pl.ds(value_col, heads_wide)] = (
+                mm(own_rows, weights(value_col, heads_wide)) + bv_ref[...].astype(F32)
+            ).astype(LOW)
+            return carry
+
+        lax.fori_loop(0, 2, project, 0)
 
     def attend_back(m):
         for j in range(pairs):
@@ -868,92 +914,301 @@
             put_bin(dqkv, m, key_col + j * LANES, d_key)
             put_bin(dqkv, m, value_col + j * LANES, d_value)
 
-    for m in range(micro):
-        attend_back(m)
-        if m == 1:
-            reduce(0, 1)
-
-    away = mm(dqkv[other], weights(0, 3 * heads_wide), NT)
-    last_send[...] = away.astype(LOW)
-    copy = pair_copy(last_send, last_land, 7)
-    copy.start()
-    grad_columns(xs_flipped[...], dqkv, 0, 3 * heads_wide, 0)
-    reduce(3)
-    own_part[...] = mm(dqkv[half], weights(0, 3 * heads_wide), NT)
-    copy.wait()
-
-    def leave(i, carry):
-        at = pl.ds(pl.multiple_of(i * chunk, chunk), chunk)
-        m, quarter = i // per_bin, lax.rem(i, per_bin)
-        sources = pl.ds(quarter * (chunk // rows), chunk // rows)
-        grad_x = grad_keep[at, :] + (own_part[at, :] + last_land[at, :].astype(F32))
-        gx_send[sources, m] = grad_x.reshape(chunk // rows, rows, width).astype(LOW)
-        return carry
-
-    lax.fori_loop(0, chunks, leave, 0)
-    push(gx_send, gx_land, gx_sems, False)
-    push(gx_send, gx_land, gx_sems, True)
-    reduce(0, 1)
-    for i, start in enumerate((0, value_col)):
-        columns = slice(start, start + heads_wide)
-        vecg_buf[0, 8:9, i * heads_wide : (i + 1) * heads_wide] = (
-            mm(ones, dqkv[0, :, columns]) + mm(ones, dqkv[1, :, columns])
-        )[0:1, :]
-    vecg_buf[0, 9:16, :] = jnp.zeros((7, width), F32)
-
-    swap_v = pair_copy(vecg_buf.at[0], vec_pair, 8)
-    swap_v.start()
-    swap_v.wait()
-    vecg_buf[0, 0:6, :] = vecg_buf[0, 0:6, :] + vec_pair[0:6, :]
-
-    def hand_back(land_ref, result_ref, hbm_ref):
-        def one(i, carry):
-            result_ref[i] = land_ref[target_ref[i], i // dp_count]
+    def attend_third(third):
+        for m in range(third * micro // 3, (third + 1) * micro // 3):
+            attend(m)
+
+    def attend_back_third(third):
+        for m in range(third * micro // 3, (third + 1) * micro // 3):
+            attend_back(m)
+
+    def project_out():
+        two_halves(attn, heads_wide, out_col, part_send, 1, part_land.at[0]).wait()
+
+    pending = {}
+
+    def norm_after_attention():
+        def norm_attn(i, carry):
+            at = pl.ds(pl.multiple_of(i * chunk, chunk), chunk)
+            mid = xs[half, at, :].astype(F32) + (own_part[at, :] + part_land[0, at, :].astype(F32)) + vec[0:1, :]
+            centre = mid - mean_of(mid)
+            inverse_s = lax.rsqrt(mean_of(centre * centre) + EPS_NORM)
+            unit = centre * inverse_s
+            normed[at, :] = unit
+            spread[at, :] = jnp.broadcast_to(inverse_s, (chunk, LANES))
+            hs[half, at, :] = (unit * vec[1:2, :] + vec[2:3, :]).astype(LOW)
             return carry
 
-        lax.fori_loop(0, blocks, one, 0)
-        copy_out(result_ref, hbm_ref)
-
-    begin, fold = swing(vecg_buf, vecg_land, vecg_sems, 0, vec_out_ref)
-    begin()
-    reduce(2)
-    fold()
-    begin, fold = swing(vecg_buf, vecg_land, vecg_sems, 1, vec_out_ref)
-    begin()
-    settle(out_send, out_land, out_sems)
-    hand_back(out_land, layer_out_ref, layer_out_hbm)
-    reduce(1, 0)
-    reduce(2)
-    fold()
-    begin, fold = swing(vecg_buf, vecg_land, vecg_sems, 2, vec_out_ref)
-    begin()
-    reduce(1, 0)
-    reduce(3)
-    fold()
-    begin, fold = swing(vecg_buf, vecg_land, vecg_sems, 3, vec_out_ref)
-    begin()
-    reduce(2)
-    reduce(3)
-    reduce(2)
-    fold()
-    reduce(3)
-    settle(gx_send, gx_land, gx_sems)
-    hand_back(gx_land, grad_tokens_ref, grad_tokens_hbm)
-    reduce(3)
+        lax.fori_loop(0, chunks, norm_attn, 0)
+        pending[2] = pair_copy(hs.at[half], hs.at[half], 2)
+        pending[2].start()
+
+    def widen_tokens():
+        def widen(h):
+            for i in range(ff // tile):
+                start = i * tile
+                row = 8 + start // width
+                inner = mm(hs[h], weights(inner_col + start, tile)) + vec[
+                    row : row + 1, start % width : start % width + tile
+                ]
+                cdf = 0.5 * (1.0 + lax.erf(inner * (0.5**0.5)))
+                density = jnp.exp(-0.5 * inner * inner) * ((2.0 * math.pi) ** -0.5)
+                gelu_low[h, :, start : start + tile] = (inner * cdf).astype(LOW)
+                dgelu[h, :, start : start + tile] = (cdf + inner * density).astype(dgelu.dtype)
+
+        def widen_step(i, carry):
+            @pl.when(i == 1)
+            def _():
+                pending[2].wait()
+
+            widen(lax.rem(half + i, 2))
+            return carry
+
+        lax.fori_loop(0, 2, widen_step, 0)
+        xs_flipped[...] = xs[...].reshape(2 * tall, width).T
+        hs_flipped[...] = hs[...].reshape(2 * tall, width).T
+
+    def narrow_tokens():
+        two_halves(gelu_low, ff, outer_col, part_send, 3, part_land.at[1]).wait()
+
+    def norm_after_ffn():
+        def norm_ffn(i, carry):
+            at = pl.ds(pl.multiple_of(i * chunk, chunk), chunk)
+            m, quarter = i // per_bin, lax.rem(i, per_bin)
+            sources = pl.ds(quarter * (chunk // rows), chunk // rows)
+            hidden = normed[at, :] * vec[1:2, :] + vec[2:3, :]
+            top = hidden + (own_part[at, :] + part_land[1, at, :].astype(F32)) + vec[3:4, :]
+            centre = top - mean_of(top)
+            inverse_s = lax.rsqrt(mean_of(centre * centre) + EPS_NORM)
+            unit = centre * inverse_s
+            own_part[at, :] = unit
+            spread_ffn[at, :] = jnp.broadcast_to(inverse_s, (chunk, LANES))
+            result = unit * vec[4:5, :] + vec[5:6, :]
+            out_send[sources, m] = result.reshape(chunk // rows, rows, width).astype(LOW)
+            return carry
+
+        lax.fori_loop(0, chunks, norm_ffn, 0)
+
+    def norm_ffn_backward():
+        settle(dy_send, dy_land, dy_sems)
+        for i in range(3):
+            vec_acc[i] = jnp.zeros((8, width), F32)
+
+        def norm_ffn_back(i, carry):
+            at = pl.ds(pl.multiple_of(i * chunk, chunk), chunk)
+            m, quarter = i // per_bin, lax.rem(i, per_bin)
+            sources = pl.ds(quarter * (chunk // rows), chunk // rows)
+            unit = own_part[at, :]
+            dy = dy_land[sources, m].astype(F32).reshape(chunk, width)
+            vec_acc[0] = vec_acc[0] + fold_rows(dy * unit)
+            vec_acc[1] = vec_acc[1] + fold_rows(dy)
+            scaled = dy * vec[4:5, :]
+            grad_top = (scaled - mean_of(scaled) - unit * mean_of(scaled * unit)) * spread_ffn[at, 0:1]
+            grad_keep[at, :] = grad_top
+            gs[half, at, :] = grad_top.astype(LOW)
+            return carry
+
+        swaps = []
+        for i, which in enumerate((4, 9)):
+            lax.fori_loop(i * (chunks // 2), (i + 1) * (chunks // 2), norm_ffn_back, 0)
+            piece_of = gs.at[half, pl.ds(i * (tall // 2), tall // 2)]
+            swap_g = pair_copy(piece_of, piece_of, which)
+            swap_g.start()
+            swaps.append(swap_g)
+        for swap_g in swaps:
+            swap_g.wait()
+        flipped[...] = gs[...].reshape(2 * tall, width).T
+
+    middle = scatter_plan[1][2] + scatter_plan[1][3] - outer_col
+
+    def grad_outer(part):
+        start, stop = ((0, middle), (middle, ff))[part]
+        grad_columns(flipped[...], gelu_low, start, stop - start, outer_col + start, stop - start)
+
+    def ffn_backward():
+        def narrow(h):
+            for i in range(ff // tile):
+                start = i * tile
+                grad = mm(gs[h], weights(outer_col + start, tile)) * dgelu[h, :, start : start + tile].astype(F32)
+                ginner[h, :, start : start + tile] = grad.astype(LOW)
+
+        vecg_buf[0, 4:5, :] = jnp.sum(vec_acc[0], axis=0, keepdims=True)
+        vecg_buf[0, 5:6, :] = jnp.sum(vec_acc[1], axis=0, keepdims=True)
+        vecg_buf[0, 3:4, :] = mm(ones, gs[half])[0:1, :]
+
+        narrow(half)
+        narrow(other)
+        copy = two_halves(ginner, ff, inner_col, part_send, 5, part_land.at[2])
+        for i in range(ff // width):
+            columns = slice(i * width, (i + 1) * width)
+            vecg_buf[0, 6 + i : 7 + i, :] = (mm(ones, ginner[0, :, columns]) + mm(ones, ginner[1, :, columns]))[0:1, :]
+        copy.wait()
+        for i in range(3):
+            vec_acc[i] = jnp.zeros((8, width), F32)
+
+        def norm_back(i, carry):
+            at = pl.ds(pl.multiple_of(i * chunk, chunk), chunk)
+            grad_hidden = grad_keep[at, :] + (own_part[at, :] + part_land[2, at, :].astype(F32))
+            unit = normed[at, :]
+            vec_acc[0] = vec_acc[0] + fold_rows(grad_hidden * unit)
+            vec_acc[1] = vec_acc[1] + fold_rows(grad_hidden)
+            scaled = grad_hidden * vec[1:2, :]
+            grad_mid = (scaled - mean_of(scaled) - unit * mean_of(scaled * unit)) * spread[at, 0:1]
+            grad_keep[at, :] = grad_mid
+            gb[half, at, :] = grad_mid.astype(LOW)
+            return carry
+
+        lax.fori_loop(0, chunks, norm_back, 0)
+        pending[6] = pair_copy(gb.at[half], gb.at[half], 6)
+        pending[6].start()
+        vecg_buf[0, 1:2, :] = jnp.sum(vec_acc[0], axis=0, keepdims=True)
+        vecg_buf[0, 2:3, :] = jnp.sum(vec_acc[1], axis=0, keepdims=True)
+        vecg_buf[0, 0:1, :] = mm(ones, gb[half])[0:1, :]
+
+    def grad_inner():
+        grad_columns(hs_flipped[...], ginner, 0, ff, inner_col)
+
+    def grad_out():
+        pending[6].wait()
+        flipped[...] = gb[...].reshape(2 * tall, width).T
+        grad_columns(flipped[...], attn, 0, heads_wide, out_col)
+
+    def heads_backward():
+        def to_heads(h, carry):
+            gattn[h] = mm(gb[h], weights(out_col, heads_wide)).astype(LOW)
+            return carry
+
+        lax.fori_loop(0, 2, to_heads, 0)
+
+    def input_away():
+        last_send[...] = mm(dqkv[other], weights(0, 3 * heads_wide), NT).astype(LOW)
+        pending[7] = pair_copy(last_send, last_land, 7)
+        pending[7].start()
+
+    def grad_heads():
+        grad_columns(xs_flipped[...], dqkv, 0, 3 * heads_wide, 0)
+
+    def input_backward():
+        own_part[...] = mm(dqkv[half], weights(0, 3 * heads_wide), NT)
+        pending[7].wait()
+
+        def leave(i, carry):
+            at = pl.ds(pl.multiple_of(i * chunk, chunk), chunk)
+            m, quarter = i // per_bin, lax.rem(i, per_bin)
+            sources = pl.ds(quarter * (chunk // rows), chunk // rows)
+            grad_x = grad_keep[at, :] + (own_part[at, :] + last_land[at, :].astype(F32))
+            gx_send[sources, m] = grad_x.reshape(chunk // rows, rows, width).astype(LOW)
+            return carry
+
+        lax.fori_loop(0, chunks, leave, 0)
+
+    def pair_vectors():
+        for i, start in enumerate((0, value_col)):
+            columns = slice(start, start + heads_wide)
+            vecg_buf[0, 8:9, i * heads_wide : (i + 1) * heads_wide] = (
+                mm(ones, dqkv[0, :, columns]) + mm(ones, dqkv[1, :, columns])
+            )[0:1, :]
+        vecg_buf[0, 9:16, :] = jnp.zeros((7, width), F32)
+
+        swap_v = pair_copy(vecg_buf.at[0], vec_pair, 8)
+        swap_v.start()
+        swap_v.wait()
+        vecg_buf[0, 0:6, :] = vecg_buf[0, 0:6, :] + vec_pair[0:6, :]
+
+    def take_output():
+        settle(out_send, out_land, out_sems)
+        hand_back(out_land, layer_out_ref, layer_out_hbm)
+
+    def take_input_grad():
+        settle(gx_send, gx_land, gx_sems)
+        hand_back(gx_land, grad_tokens_ref, grad_tokens_hbm)
+
+    folds = []
+
+    def sum_vectors(turn=None):
+        if folds:
+            folds[-1]()
+        if len(folds) < stages:
+            begin, fold = swing(vecg_buf, vecg_land, vecg_sems, len(folds), vec_out_ref)
+            begin()
+            folds.append(fold)
+        else:
+            folds.append(lambda: None)
+
+    exchanges = {
+        X: (x_send, x_land, x_sems),
+        DY: (dy_send, dy_land, dy_sems),
+        OUT: (out_send, out_land, out_sems),
+        GX: (gx_send, gx_land, gx_sems),
+    }
+    steps = {
+        GATHER: advance,
+        REDUCE: reduce,
+        NEAR: lambda name: push(*exchanges[name], True),
+        FAR: lambda name: push(*exchanges[name], False),
+        VECTORS: sum_vectors,
+        FIND_SLOTS: find_slots,
+        SEND_PIECES: send_pieces,
+        ARRANGE_TOKENS: arrange_tokens,
+        ARRANGE_COTANGENT: arrange_cotangent,
+        WHOLE_VECTORS: whole_vectors,
+        MASK_BINS: mask_bins,
+        TAKE_TOKENS: take_tokens,
+        PROJECT_HEADS: project_heads,
+        ATTEND_THIRD: attend_third,
+        ATTEND_BACK_THIRD: attend_back_third,
+        PROJECT_OUT: project_out,
+        NORM_AFTER_ATTENTION: norm_after_attention,
+        WIDEN_TOKENS: widen_tokens,
+        NARROW_TOKENS: narrow_tokens,
+        NORM_AFTER_FFN: norm_after_ffn,
+        NORM_FFN_BACKWARD: norm_ffn_backward,
+        GRAD_OUTER: grad_outer,
+        FFN_BACKWARD: ffn_backward,
+        GRAD_INNER: grad_inner,
+        GRAD_OUT: grad_out,
+        HEADS_BACKWARD: heads_backward,
+        INPUT_AWAY: input_away,
+        GRAD_HEADS: grad_heads,
+        INPUT_BACKWARD: input_backward,
+        PAIR_VECTORS: pair_vectors,
+        TAKE_OUTPUT: take_output,
+        TAKE_INPUT_GRAD: take_input_grad,
+    }
+    covered = {
+        PROJECT_HEADS: (0, 3 * heads_wide),
+        PROJECT_OUT: (out_col, inner_col),
+        WIDEN_TOKENS: (inner_col, outer_col),
+        NARROW_TOKENS: (outer_col, outer_col + ff),
+    }
+    for name, *which in SCHEDULE:
+        low, high = covered.get(name, (0, 0))
+        for number in sorted({plan[0] for plan in gather_plan}):
+            cols = extent(gather_plan, number)
+            while cols.start < high and cols.start + cols.size > low and gone.get(number, 0) <= stages:
+                advance(number)
+        steps[name](*which)
+    for number in sorted({plan[0] for plan in scatter_plan}):
+        while sent[number] <= stages:
+            reduce(number)
+    while len(folds) <= stages:
+        sum_vectors()
+    every_column = pl.ds(0, full.shape[-1])
+    for stage in range(stages):
+        shards_copy(
+            full, stages - stage, every_column, gather_sends.at[stage], gather_recvs.at[0, stage]
+        ).wait_send()
+        shards_copy(
+            grads, stage + 1, every_column, scatter_sends.at[stage], scatter_recvs.at[0, stage]
+        ).wait_send()
     for copy in leaving:
         copy.wait()
-    assert all(n == stages + 1 for n in (*gone.values(), *sent.values()))
-    for gather in gathers:
-        for stage in range(stages):
-            gather.copy(stage).wait_send()
-    for scatter in scatters:
-        for stage in range(stages):
-            scatter.copy(stage).wait_send()
 
 
 def finish(*refs):
     sources, total_ref, targets = refs[:8], refs[8], refs[9:17]
-    own_ref, inner_ref, query_ref, value_ref, *held, sems = refs[17:]
+    *own_refs, inner_ref, query_ref, value_ref = refs[17:26]
+    *held, sems = refs[26:]
     loads = [pltpu.make_async_copy(src, hold, sems.at[0, i]) for i, (src, hold) in enumerate(zip(sources, held))]
     stores = [pltpu.make_async_copy(hold, dst, sems.at[1, i]) for i, (hold, dst) in enumerate(zip(held, targets))]
     for load in loads:
@@ -975,7 +1230,9 @@
             preferred_element_type=F32,
         )
 
-    own_ref[...] = cut(total_ref[0:8, :], own_ref.shape[1])
+    own = cut(total_ref[0:8, :], own_refs[0].shape[0])
+    for i, ref in enumerate(own_refs):
+        ref[...] = own[i : i + 1, :].reshape(ref.shape)
     width, heads_wide = total_ref.shape[1], query_ref.shape[1]
     rows = inner_ref.shape[1] * lax.axis_size("dp") // width
     long = jnp.concatenate([total_ref[6 + i : 7 + i, :] for i in range(rows)], axis=1)
@@ -989,37 +1246,21 @@
 def plans(dp_count, heads_wide, ff):
     bits = bits_of(dp_count)
     far, near = bits[:-2], bits[-2:]
-    far_first = (far + near, far + near[::-1])
-    near_first = (near[::-1] + far, near + far)
-    inner_col, outer_col = 4 * heads_wide, 4 * heads_wide + ff
-
-    def plan_of(cuts):
+    orders = {
+        FAR_FIRST: (far + near, far + near[::-1]),
+        NEAR_FIRST: (near[::-1] + far, near + far),
+    }
+
+    def plan_of(groups, turned):
         plan = []
-        for group, (orders, start, stop) in enumerate(cuts):
-            middle = start + (stop - start + LANES) // (2 * LANES) * LANES
-            plan.append((group, orders[0], start, middle - start))
-            plan.append((group, orders[1], middle, stop - middle))
+        for group, (kind, first, tiles) in enumerate(groups):
+            start, size = first * LANES, (tiles + 1) // 2 * LANES
+            one, two = (order[::-1] if turned else order for order in orders[kind])
+            plan.append((group, one, start, size))
+            plan.append((group, two, start + size, tiles * LANES - size))
         return plan
 
-    gather = plan_of(
-        [
-            (far_first, 0, 3 * heads_wide),
-            (far_first, 3 * heads_wide, inner_col + ff // 2),
-            (far_first, inner_col + ff // 2, outer_col),
-            (far_first, outer_col, outer_col + ff // 2),
-            (near_first, outer_col + ff // 2, outer_col + ff),
-        ]
-    )
-    back = lambda orders: (orders[0][::-1], orders[1][::-1])
-    scatter = plan_of(
-        [
-            (back(far_first), outer_col, outer_col + ff // 2),
-            (back(near_first), outer_col + ff // 2, outer_col + ff),
-            (back(far_first), 3 * heads_wide, outer_col),
-            (back(far_first), 0, 3 * heads_wide),
-        ]
-    )
-    return gather, scatter
+    return plan_of(GATHERS, False), plan_of(SCATTERS, True)
 
 
 def shards_fast(
@@ -1086,8 +1327,8 @@
         pltpu.VMEM((tall, LANES), F32),
         pltpu.VMEM((tall, width), F32),
         pltpu.VMEM((tall, width), F32),
-        pltpu.VMEM((tall, width), F32),
-        pltpu.VMEM((3, tall, width), F32),
+        pltpu.VMEM((tall, width), LOW),
+        pltpu.VMEM((3, tall, width), LOW),
         pltpu.VMEM((tall, width), LOW),
         pltpu.VMEM((tall, width), LOW),
         pltpu.VMEM((16, LANES), F32),
@@ -1099,19 +1340,25 @@
         pltpu.VMEM((3, 8, width), F32),
     ]
     scratch += [
-        pltpu.VMEM((2,) * (stages - 1 - stage) + (own_width, size), LOW)
-        for _, _, _, size in scatter_plan
+        pltpu.VMEM(
+            (2,) * (stages - 1 - stage)
+            + (own_width, sum(size for group, _, _, size in scatter_plan if group == wanted)),
+            LOW,
+        )
+        for wanted in range(max(group for group, _, _, _ in scatter_plan) + 1)
         for stage in range(stages)
     ]
-    scratch += [dma((2, dp_count)) for _ in range(4)]
+    scratch += [dma((2,)) for _ in range(4)]
     scratch += [
-        dma((2, len(gather_plan), stages)),
-        dma((2, len(scatter_plan), stages)),
-        dma((2, dp_count)),
+        dma((stages,)),
+        dma((len(gather_plan), stages)),
+        dma((stages,)),
+        dma((len(scatter_plan), stages)),
+        dma((2,)),
         dma((2, stages)),
-        dma((2, 9)),
+        dma((2, 10)),
         dma((8,)),
-        dma((32,)),
+        dma((24,)),
     ]
     sizes = (dp_count, micro, rows, width, heads_wide, ff)
     hbm = pl.BlockSpec(memory_space=pl.ANY)
@@ -1154,21 +1401,22 @@
         b_inner,
     )
     own_inner = b_inner.shape[1]
-    *big, own, bias_inner, bias_query, bias_value = pl.pallas_call(
+    results = pl.pallas_call(
         finish,
         out_shape=(
             *made,
-            jax.ShapeDtypeStruct((8, own_width), F32),
+            *[jax.ShapeDtypeStruct((own_width,), F32) for _ in range(6)],
             jax.ShapeDtypeStruct((1, own_inner), F32),
             jax.ShapeDtypeStruct((1, heads_wide), F32),
             jax.ShapeDtypeStruct((1, heads_wide), F32),
         ),
         in_specs=[hbm] * 8 + [vmem],
-        out_specs=[hbm] * 8 + [vmem] * 4,
+        out_specs=[hbm] * 8 + [vmem] * 9,
         scratch_shapes=[pltpu.VMEM(result.shape, result.dtype) for result in made] + [dma((2, 8))],
         name="finish",
     )(*big, total)
-    layer_out, grad_tokens, gq, gk, gv, go, gi, gu = big
+    layer_out, grad_tokens, gq, gk, gv, go, gi, gu = results[:8]
+    own, (bias_inner, bias_query, bias_value) = results[8:14], results[14:]
     return (
         layer_out,
         grad_tokens,

time: 189 us -> 175 us (0.926)
  Pallas kernels: 186 us -> 173 us
    pallas_call x1, Pallas kernels: 183 us -> 170 us  [shards_fast(): pl.pallas_call(partial(layer, sizes, gather_plan, scatter_plan), out_shap...]
where the time goes in v4:
time: 175 us; the launch traced here: 174 us
  Pallas kernels  173 us (99%)
    pallas_call x1, Pallas kernels, shards_fast(): pl.pallas_call(partial(layer, sizes, gather_plan, scatter_plan), out_shap...  170 us
    pallas_call x1, Pallas kernels, shards_fast(): pl.pallas_call(finish, out_shape=(*made, *[jax.ShapeDtypeStruct((own_widt...  3.91 us

profile of v4, /device:TPU:0, one launch (start us, length us, event | category | flops | bytes accessed | tf_op | source)
XLA Modules:
  0.0 174.3 jit_solution(15632602490695870511)
XLA Ops:
  0.7 169.6 %layer.1 = (bf16[48,8,768]{2,1,0:T(8,128)(2,1)}, bf16[48,8,768]{2,1,0:T(8,128)(2,1)}, f32[48,384]{1,0:T(8,128)}, f32[48,384]{1,0:T(8,128)}, f32[48,384]{1,0:T(8,...) custom-call(bf16[48,8,768]{2,1,0:T(8,128)(2,1)} %refs_0_.1, ...), custom_call_target="tpu_custom_call" | custom-call | tf_op jit(solution)/shard_map/layer/pallas_call | solution.py:1371
  170.3 3.9 %finish.1 = (bf16[48,8,768]{2,1,0:T(8,128)(2,1)}, bf16[48,8,768]{2,1,0:T(8,128)(2,1)}, f32[48,384]{1,0:T(8,128)}, f32[48,384]{1,0:T(8,128)}, f32[48,384]{1,0:T(8...) custom-call(bf16[48,8,768]{2,1,0:T(8,128)(2,1)} %get-tuple-element.4, ...), custom_call_target="tpu_custom_call" | custom-call | tf_op jit(solution)/shard_map/finish/pallas_call | solution.py:1404

commit v5 on v4

--- a/solution.py
+++ b/solution.py
@@ -148,58 +148,58 @@
 )
 SCHEDULE = (
     (GATHER, 1),
-    (GATHER, 5),
+    (GATHER, 6),
     (GATHER, 2),
     (SEND_PIECES,),
+    (FIND_SLOTS,),
+    (GATHER, 5),
+    (GATHER, 0),
+    (ARRANGE_TOKENS,),
+    (NEAR, X),
+    (GATHER, 1),
+    (GATHER, 5),
+    (GATHER, 0),
+    (GATHER, 2),
     (GATHER, 6),
+    (FAR, X),
+    (GATHER, 3),
     (GATHER, 0),
-    (FIND_SLOTS,),
-    (ARRANGE_TOKENS,),
-    (GATHER, 5),
-    (NEAR, X),
-    (ARRANGE_COTANGENT,),
     (GATHER, 1),
     (GATHER, 0),
+    (GATHER, 4),
+    (GATHER, 2),
+    (GATHER, 1),
+    (GATHER, 5),
+    (WHOLE_VECTORS,),
+    (GATHER, 3),
+    (TAKE_TOKENS,),
     (GATHER, 6),
     (GATHER, 2),
-    (FAR, X),
-    (GATHER, 3),
+    (ARRANGE_COTANGENT,),
     (GATHER, 4),
     (GATHER, 1),
     (GATHER, 0),
-    (WHOLE_VECTORS,),
-    (GATHER, 0),
+    (PROJECT_HEADS,),
+    (GATHER, 3),
+    (GATHER, 5),
+    (MASK_BINS,),
+    (ATTEND_THIRD, 0),
+    (NEAR, DY),
+    (GATHER, 4),
     (GATHER, 2),
+    (ATTEND_THIRD, 1),
+    (GATHER, 6),
+    (ATTEND_THIRD, 2),
     (GATHER, 3),
     (GATHER, 4),
+    (PROJECT_OUT,),
     (GATHER, 5),
-    (GATHER, 1),
-    (MASK_BINS,),
-    (GATHER, 6),
-    (GATHER, 2),
-    (TAKE_TOKENS,),
-    (GATHER, 0),
-    (GATHER, 5),
-    (GATHER, 3),
-    (GATHER, 1),
-    (PROJECT_HEADS,),
-    (NEAR, DY),
-    (ATTEND_THIRD, 0),
-    (GATHER, 2),
-    (GATHER, 6),
-    (ATTEND_THIRD, 1),
-    (GATHER, 4),
-    (ATTEND_THIRD, 2),
-    (PROJECT_OUT,),
-    (GATHER, 3),
-    (GATHER, 4),
-    (GATHER, 6),
     (FAR, DY),
     (NORM_AFTER_ATTENTION,),
     (GATHER, 3),
-    (GATHER, 5),
     (WIDEN_TOKENS,),
     (GATHER, 4),
+    (GATHER, 6),
     (NARROW_TOKENS,),
     (NORM_AFTER_FFN,),
     (NEAR, OUT),
@@ -207,54 +207,54 @@
     (NORM_FFN_BACKWARD,),
     (GRAD_OUTER, 0),
     (GRAD_OUTER, 1),
+    (REDUCE, 1),
     (REDUCE, 0),
-    (REDUCE, 1),
     (FFN_BACKWARD,),
     (GRAD_INNER,),
     (REDUCE, 2),
-    (TAKE_OUTPUT,),
     (GRAD_OUT,),
+    (REDUCE, 0),
     (HEADS_BACKWARD,),
     (ATTEND_BACK_THIRD, 0),
     (ATTEND_BACK_THIRD, 1),
     (ATTEND_BACK_THIRD, 2),
-    (REDUCE, 0),
     (REDUCE, 1),
+    (REDUCE, 3),
+    (TAKE_OUTPUT,),
     (INPUT_AWAY,),
+    (GRAD_HEADS,),
     (REDUCE, 2),
-    (REDUCE, 3),
-    (GRAD_HEADS,),
     (REDUCE, 5),
-    (REDUCE, 4),
     (REDUCE, 0),
     (REDUCE, 2),
+    (REDUCE, 4),
     (REDUCE, 0),
     (REDUCE, 5),
     (INPUT_BACKWARD,),
     (REDUCE, 2),
+    (NEAR, GX),
     (REDUCE, 1),
+    (REDUCE, 0),
+    (REDUCE, 3),
     (PAIR_VECTORS,),
-    (NEAR, GX),
+    (VECTORS,),
+    (REDUCE, 4),
+    (FAR, GX),
+    (REDUCE, 5),
+    (VECTORS,),
+    (REDUCE, 4),
     (REDUCE, 5),
     (REDUCE, 3),
-    (REDUCE, 4),
-    (VECTORS,),
-    (FAR, GX),
+    (REDUCE, 1),
     (VECTORS,),
     (REDUCE, 4),
-    (VECTORS,),
+    (REDUCE, 1),
+    (TAKE_INPUT_GRAD,),
     (REDUCE, 2),
     (REDUCE, 3),
+    (VECTORS,),
+    (VECTORS,),
     (REDUCE, 5),
-    (REDUCE, 1),
-    (VECTORS,),
-    (REDUCE, 0),
-    (REDUCE, 4),
-    (REDUCE, 3),
-    (TAKE_INPUT_GRAD,),
-    (REDUCE, 1),
-    (REDUCE, 5),
-    (VECTORS,),
     (REDUCE, 4),
     (REDUCE, 3),
 )
@@ -394,7 +394,7 @@
         gi_hbm,
         gu_hbm,
     ) = refs[:28]
-    vec_out_ref = refs[28]
+    vec_out_hbm = refs[28]
     (
         inverse_ref,
         target_ref,
@@ -445,6 +445,7 @@
         vecg_buf,
         vecg_land,
         vec_acc,
+        vec_total,
         *rest,
     ) = refs[29:]
     stages = dp_count.bit_length() - 1
@@ -812,10 +813,10 @@
             block = pieces[source]
 
             def laid(block, size, extent):
-                target = lax.broadcasted_iota(jnp.int32, (LANES, extent), 1)
-                at = lax.broadcasted_iota(jnp.int32, (LANES, extent), 0)
-                hit = (target == at + source * size) & (at < size)
-                return mm(block.astype(LOW), hit.astype(F32).astype(LOW))
+                target = lax.broadcasted_iota(jnp.int32, (size, extent), 1)
+                at = lax.broadcasted_iota(jnp.int32, (size, extent), 0)
+                hit = target == at + source * size
+                return mm(block[:, :size].astype(LOW), hit.astype(F32).astype(LOW))
 
             return (
                 total[0] + laid(block[0:8], own_width, width),
@@ -927,6 +928,10 @@
 
     pending = {}
 
+    def turn(ref, h):
+        columns = pl.ds(pl.multiple_of(h * tall, LANES), tall)
+        flipped[:, columns] = ref[h].T
+
     def norm_after_attention():
         def norm_attn(i, carry):
             at = pl.ds(pl.multiple_of(i * chunk, chunk), chunk)
@@ -1015,9 +1020,10 @@
             swap_g = pair_copy(piece_of, piece_of, which)
             swap_g.start()
             swaps.append(swap_g)
+        turn(gs, half)
         for swap_g in swaps:
             swap_g.wait()
-        flipped[...] = gs[...].reshape(2 * tall, width).T
+        turn(gs, other)
 
     middle = scatter_plan[1][2] + scatter_plan[1][3] - outer_col
 
@@ -1069,8 +1075,9 @@
         grad_columns(hs_flipped[...], ginner, 0, ff, inner_col)
 
     def grad_out():
+        turn(gb, half)
         pending[6].wait()
-        flipped[...] = gb[...].reshape(2 * tall, width).T
+        turn(gb, other)
         grad_columns(flipped[...], attn, 0, heads_wide, out_col)
 
     def heads_backward():
@@ -1129,10 +1136,11 @@
         if folds:
             folds[-1]()
         if len(folds) < stages:
-            begin, fold = swing(vecg_buf, vecg_land, vecg_sems, len(folds), vec_out_ref)
+            begin, fold = swing(vecg_buf, vecg_land, vecg_sems, len(folds), vec_total)
             begin()
             folds.append(fold)
         else:
+            copy_out(vec_total, vec_out_hbm)
             folds.append(lambda: None)
 
     exchanges = {
@@ -1338,6 +1346,7 @@
         pltpu.VMEM((stages, 16, width), F32),
         pltpu.VMEM((stages, 16, width), F32),
         pltpu.VMEM((3, 8, width), F32),
+        pltpu.VMEM((16, width), F32),
     ]
     scratch += [
         pltpu.VMEM(
@@ -1372,7 +1381,7 @@
         partial(layer, sizes, gather_plan, scatter_plan),
         out_shape=(*made, jax.ShapeDtypeStruct((16, width), F32)),
         in_specs=[hbm] * 2 + [smem] * 2 + [hbm] * 6 + [vmem] * 10,
-        out_specs=[hbm] * 8 + [vmem],
+        out_specs=[hbm] * 9,
         scratch_shapes=scratch,
         compiler_params=pltpu.CompilerParams(
             collective_id=0, has_side_effects=True, vmem_limit_bytes=VMEM_BYTES

time: 175 us -> 172 us (0.983)
  Pallas kernels: 173 us -> 171 us
    pallas_call x1, Pallas kernels: 170 us -> 167 us  [shards_fast(): pl.pallas_call(partial(layer, sizes, gather_plan, scatter_plan), out_shap...]
where the time goes in v5:
time: 172 us
  Pallas kernels  171 us (99%)
    pallas_call x1, Pallas kernels, shards_fast(): pl.pallas_call(partial(layer, sizes, gather_plan, scatter_plan), out_shap...  167 us
    pallas_call x1, Pallas kernels, shards_fast(): pl.pallas_call(finish, out_shape=(*made, *[jax.ShapeDtypeStruct((own_widt...  3.91 us

profile of v5, /device:TPU:0, one launch (start us, length us, event | category | flops | bytes accessed | tf_op | source)
XLA Modules:
  0.0 171.9 jit_solution(12526674593268356942)
XLA Ops:
  0.7 167.2 %layer.1 = (bf16[48,8,768]{2,1,0:T(8,128)(2,1)}, bf16[48,8,768]{2,1,0:T(8,128)(2,1)}, f32[48,384]{1,0:T(8,128)}, f32[48,384]{1,0:T(8,128)}, f32[48,384]{1,0:T(8,...) custom-call(bf16[48,8,768]{2,1,0:T(8,128)(2,1)} %refs_0_.1, ...), custom_call_target="tpu_custom_call" | custom-call | tf_op jit(solution)/shard_map/layer/pallas_call | solution.py:1380
  167.8 3.9 %finish.1 = (bf16[48,8,768]{2,1,0:T(8,128)(2,1)}, bf16[48,8,768]{2,1,0:T(8,128)(2,1)}, f32[48,384]{1,0:T(8,128)}, f32[48,384]{1,0:T(8,128)}, f32[48,384]{1,0:T(8...) custom-call(bf16[48,8,768]{2,1,0:T(8,128)(2,1)} %get-tuple-element.4, ...), custom_call_target="tpu_custom_call" | custom-call | tf_op jit(solution)/shard_map/finish/pallas_call | solution.py:1413
